TPU v7x, 32 devices: a whole 2x2x4 slice. The times are simulated.
32 devices in a mesh: gx: 16 (over z, y, x), gy: 2 (over core).
Axes of the slice: x: 2, y: 2, z: 4, core: 2. Of those that a mesh axis runs over, the one named last changes fastest.
Arguments:
- forcing: float32 [128, 64, 256], P('gx', 'gy'), may hold values from -20 to 20
- reaction: float32 [128, 64, 256], P('gx', 'gy'), may hold values from 0.1 to 1.9
- velocity: float32 [3, 128, 64, 256], P(None, 'gx', 'gy'), may hold values from -0.08 to 0.08
Outputs:
- basis_q: float32 [9, 128, 64, 256], P(None, 'gx', 'gy')
- factor_r: float32 [9, 9], replicated
All inputs are finite; a program needn't handle non-finite values.
Results may differ from a plain program's by a relative error of at most 0.0018.
Values sent between devices are 32-bit elements; how exact they have to be, the bound alone decides.
No kernel may reach another device: no remote copies, remote signals or barrier semaphores. Data moves between devices by JAX's collectives and lax.ppermute only.
A program may use at most 128 MiB of HBM per device.

v0:
```python
import math

import jax
import jax.numpy as jnp
from jax import lax
from jax.sharding import PartitionSpec as P

STEPS = 8


DIFFUSION = 0.03
CENTRE_SHIFT = 1.18
HALF_WIDTH = 0.95
EPSILON = 1e-06


def with_halo(cells, sides, width):
    for axis, dim in sides:
        count = lax.axis_size(axis)
        head = lax.slice_in_dim(cells, 0, width, axis=dim)
        tail = lax.slice_in_dim(cells, cells.shape[dim] - width, cells.shape[dim], axis=dim)
        cells = jnp.concatenate(
            [
                lax.ppermute(tail, axis, [(i, (i + 1) % count) for i in range(count)]),
                cells,
                lax.ppermute(head, axis, [((i + 1) % count, i) for i in range(count)]),
            ],
            axis=dim,
        )
    return cells


def from_partner(block, axis, distance):
    count = lax.axis_size(axis)
    route = []
    for low in range(count):
        high = low | 1 << distance
        if high != low and high < count:
            route += [(low, high), (high, low)]
    return lax.ppermute(block, axis, route)


def apply_scaled(padded, reaction, velocity):
    centre = padded[1:-1, 1:-1]
    east_cell = padded[2:, 1:-1]
    west_cell = padded[:-2, 1:-1]
    north_cell = padded[1:-1, 2:]
    south_cell = padded[1:-1, :-2]
    upper_cell = jnp.roll(centre, -1, axis=2)
    lower_cell = jnp.roll(centre, 1, axis=2)
    neighbours = east_cell + west_cell + north_cell + south_cell + upper_cell + lower_cell
    advection = (
        velocity[0] * (east_cell - west_cell)
        + velocity[1] * (north_cell - south_cell)
        + velocity[2] * (upper_cell - lower_cell)
    )
    operated = reaction * centre + DIFFUSION * (6.0 * centre - neighbours) + 0.5 * advection
    return (operated - CENTRE_SHIFT * centre) / HALF_WIDTH


def shallow_apply(field, reaction, velocity):
    padded = with_halo(field, (("gx", 0), ("gy", 1)), 1)
    return apply_scaled(padded, reaction, velocity)


def shallow_basis(start, reaction, velocity):
    previous = start
    current = shallow_apply(start, reaction, velocity)
    vectors = [previous, current]
    for step_index in range(STEPS - 1):
        following = 2.0 * shallow_apply(current, reaction, velocity) - previous
        previous, current = (current, following)
        vectors.append(current)
    return vectors


def orth_upper(stacked):
    count = stacked.shape[1]
    upper_rows = jnp.zeros((count, count), jnp.float32)
    columns = []
    for column_index in range(count):
        vector = stacked[:, column_index]
        for row_index in range(column_index):
            projection = jnp.sum(columns[row_index] * vector)
            vector = vector - projection * columns[row_index]
            upper_rows = upper_rows.at[row_index, column_index].set(projection)
        length = jnp.sqrt(jnp.sum(vector * vector))
        upper_rows = upper_rows.at[column_index, column_index].set(length)
        columns.append(vector / length)
    return upper_rows


def order_pair(mine, partner, is_lower):
    return jnp.where(
        is_lower, jnp.concatenate([mine, partner], axis=0), jnp.concatenate([partner, mine], axis=0)
    )


def tree_factor(local_gram):
    factor = jnp.linalg.cholesky(local_gram).T
    for bit_index in range(lax.axis_size("gx").bit_length() - 1):
        partner = from_partner(factor, "gx", bit_index)
        is_lower = lax.axis_index("gx") // 2**bit_index % 2 == 0
        factor = orth_upper(order_pair(factor, partner, is_lower))
    for bit_index in range(lax.axis_size("gy").bit_length() - 1):
        partner = from_partner(factor, "gy", bit_index)
        is_lower = lax.axis_index("gy") // 2**bit_index % 2 == 0
        factor = orth_upper(order_pair(factor, partner, is_lower))
    return factor


def upper_inverse(factor):
    count = factor.shape[0]
    identity = jnp.eye(count, dtype=jnp.float32)
    inverse_rows = [None] * count
    for row_index in reversed(range(count)):
        accumulated = identity[row_index]
        for later_index in range(row_index + 1, count):
            accumulated = accumulated - factor[row_index, later_index] * inverse_rows[later_index]
        inverse_rows[row_index] = accumulated / factor[row_index, row_index]
    return jnp.stack(inverse_rows)


def per_device(forcing, reaction, velocity):
    cell_count = float(
        forcing.shape[0]
        * forcing.shape[1]
        * forcing.shape[2]
        * lax.axis_size("gx")
        * lax.axis_size("gy")
    )
    mean_square = lax.psum(jnp.sum(forcing * forcing), ("gx", "gy")) / cell_count
    divisor = jnp.sqrt(mean_square + EPSILON)
    start = forcing / divisor
    vectors = shallow_basis(start, reaction, velocity)
    basis = jnp.stack(vectors)
    flattened = basis.reshape(basis.shape[0], -1)
    local_gram = jnp.dot(
        flattened, flattened.T, precision=lax.Precision.HIGHEST, preferred_element_type=jnp.float32
    )
    factor = tree_factor(local_gram) / math.sqrt(cell_count)
    inverse = upper_inverse(factor)
    orthonormal = jnp.tensordot(inverse, basis, axes=((0,), (0,)), precision=lax.Precision.HIGHEST)
    return (orthonormal, factor)


def solution(mesh):
    in_specs = (P("gx", "gy", None), P("gx", "gy", None), P(None, "gx", "gy", None))
    out_specs = (P(None, "gx", "gy", None), P())
    return jax.shard_map(
        per_device, mesh=mesh, in_specs=in_specs, out_specs=out_specs, check_vma=False
    )
```

profile of v0, /device:TPU:0, one launch (start us, length us, event | category | flops | bytes accessed | tf_op | source)
XLA Modules:
  0.0 786.8 jit_solution(12336831169029621820)
XLA Ops:
  2.4 42.2 %psum.7 = f32[]{:T(128)} all-reduce(f32[]{:T(128)} %multiply_reduce_fusion), channel_id=1, replica_groups=mesh['gx'=16,'gy'=2] {'gx','gy'}, use_global_device_ids=true, to_apply=%region_1.0 | all-reduce | flops 1 | bytes 8 | tf_op jit(solution)/shard_map/psum | solution.py:132
  48.6 3.3 collective-permute-start
  63.7 5.6 collective-permute-start.4
  73.1 5.7 collective-permute-start.8
  82.5 5.7 collective-permute-start.12
  91.9 5.7 collective-permute-start.16
  101.3 5.7 collective-permute-start.20
  110.8 5.7 collective-permute-start.24
  120.1 5.9 collective-permute-start.28
  129.7 8.0 %stack.51 = f32[9,8,32,256]{3,0,2,1:T(8,128)} concatenate(f32[1,8,32,256]{3,0,2,1:T(1,128)S(1)} %copy.16, f32[1,8,32,256]{3,0,2,1:T(1,128)S(1)} %copy.17, f32[1,8,32,256]{3,0,2,1:T(1,128)S(1)} %copy.18, f32[1,8,32,256]{3,0,2,1:T(1,128)S(1)} %copy.19, f32[1,8,32,256]{3,0,2,1:T(1,128)S(1)} %copy.20, f32[1,8,32,256]{3,0,2,1:T(1,128)S(1)} %copy.21, f32[1,8,32,256]{3,0,2,1:T(1,128)S(1)} %copy.22, ...), dimensions={0} | concatenate | bytes 4718592 | tf_op jit(solution)/shard_map/stack | solution.py:136
  137.7 8.7 %convolution_bitcast_fusion = f32[9,9]{1,0:T(8,128)S(1)} fusion(f32[9,8,32,256]{3,0,2,1:T(8,128)} %stack.51), kind=kOutput, calls=%fused_computation | convolution fusion | flops 63700992 | bytes 2359620 | tf_op jit(solution)/shard_map/dot_general | solution.py:138
  150.0 2.4 collective-permute-done.32
  158.2 5.2 multiply_reduce_fusion.188
  164.1 5.1 multiply_reduce_fusion.187
  173.6 6.3 multiply_reduce_fusion.186
  180.6 3.9 multiply_reduce_fusion.185
  188.9 3.9 multiply_reduce_fusion.184
  193.4 2.6 multiply_reduce_fusion.183
  267.2 3.6 collective-permute-done.33
  275.1 5.7 multiply_reduce_fusion.144
  285.3 7.5 multiply_reduce_fusion.143
  293.4 4.4 multiply_reduce_fusion.142
  302.4 5.1 multiply_reduce_fusion.141
  308.2 3.2 multiply_reduce_fusion.140
  315.7 2.7 multiply_reduce_fusion.139
  387.8 3.6 collective-permute-done.34
  395.7 5.7 multiply_reduce_fusion.100
  405.9 7.5 multiply_reduce_fusion.99
  414.0 4.4 multiply_reduce_fusion.98
  423.0 5.1 multiply_reduce_fusion.97
  428.8 3.2 multiply_reduce_fusion.96
  436.3 2.7 multiply_reduce_fusion.95
  509.8 2.9 collective-permute-done.35
  517.1 5.7 multiply_reduce_fusion.56
  527.2 7.5 multiply_reduce_fusion.55
  535.3 4.4 multiply_reduce_fusion.54
  544.3 5.1 multiply_reduce_fusion.53
  550.1 3.2 multiply_reduce_fusion.52
  557.7 2.7 multiply_reduce_fusion.51
  635.0 5.6 multiply_reduce_fusion.12
  645.0 7.7 multiply_reduce_fusion.11
  653.3 4.5 multiply_reduce_fusion.10
  662.4 4.9 multiply_reduce_fusion.9
  668.0 3.1 multiply_reduce_fusion.8
  675.6 2.5 multiply_reduce_fusion.7
  749.8 28.2 %subtract_divide_fusion = (f32[1,9]{1,0:T(1,128)S(1)}, f32[1,9]{1,0:T(1,128)S(1)}, f32[1,9]{1,0:T(1,128)S(1)}, f32[1,9]{1,0:T(1,128)S(1)}, f32[1,9]{1,0:T(1,128)...) fusion(f32[9,9]{1,0:T(8,128)S(1)} %fusion.57, f32[]{:T(128)} %bitcast.318, ...), kind=kLoop, calls=%fused_computation.315 | loop fusion | flops 729 | bytes 828 | tf_op jit(solution)/shard_map/div | solution.py:120
  778.1 5.5 fusion.54
  783.6 2.8 copy.26
  (488 shorter events, 383.6 us)
Async XLA Ops:
  0.6 62.5 %copy-start = (f32[3,8,32,256]{3,2,1,0:T(8,128)S(1)}, f32[3,8,32,256]{3,2,1,0:T(8,128)}, u32[]{:S(2)}) copy-start(f32[3,8,32,256]{3,2,1,0:T(8,128)} %param.455) | copy-start | bytes 2359300
  0.6 62.5 %copy-start.1 = (f32[8,32,256]{2,1,0:T(8,128)S(1)}, f32[8,32,256]{2,1,0:T(8,128)}, u32[]{:S(2)}) copy-start(f32[8,32,256]{2,1,0:T(8,128)} %param.454) | copy-start | bytes 786436
  46.2 11.4 %collective-permute-start.1 = (f32[1,32,256]{2,1,0:T(8,128)S(1)}, f32[1,32,256]{2,1,0:T(8,128)S(1)}, u32[]{:S(2)}, u32[]{:S(2)}) collective-permute-start(f32[1,32,256]{2,1,0:T(8,128)S(1)} %get-tuple-element.3137), channel_id=1, source_target_pairs={{0,2},{2,4},{4,6},{6,8},{8,10},{10,12},{12,14},{14,16},{16,18},{18... | collective-permute-start | bytes 98312 | tf_op jit(solution)/shard_map/ppermute | solution.py:24
  48.6 9.1 %collective-permute-start = (f32[1,32,256]{2,1,0:T(8,128)S(1)}, f32[1,32,256]{2,1,0:T(8,128)S(1)}, u32[]{:S(2)}, u32[]{:S(2)}) collective-permute-start(f32[1,32,256]{2,1,0:T(8,128)S(1)} %get-tuple-element.3138), channel_id=1, source_target_pairs={{2,0},{4,2},{6,4},{8,6},{10,8},{12,10},{14,12},{16,14},{18,16},{20... | collective-permute-start | bytes 98312 | tf_op jit(solution)/shard_map/ppermute | solution.py:26
  52.9 19.7 %copy-start.2 = (f32[8,32,256]{2,1,0:T(8,128)S(1)}, f32[8,32,256]{2,1,0:T(8,128)}, u32[]{:S(2)}) copy-start(f32[8,32,256]{2,1,0:T(8,128)} %param.453) | copy-start | bytes 786436
  57.6 5.5 collective-permute-start.2
  57.7 5.4 collective-permute-start.3
  63.6 7.6 collective-permute-start.5
  63.7 7.5 collective-permute-start.4
  71.2 1.2 collective-permute-start.6
  71.3 1.3 collective-permute-start.7
  73.0 7.6 collective-permute-start.9
  73.1 7.5 collective-permute-start.8
  80.6 1.2 collective-permute-start.10
  80.7 1.3 collective-permute-start.11
  82.4 7.6 collective-permute-start.13
  82.5 7.6 collective-permute-start.12
  90.0 1.2 collective-permute-start.14
  90.1 1.3 collective-permute-start.15
  91.8 7.6 collective-permute-start.17
  91.9 7.6 collective-permute-start.16
  99.5 1.2 collective-permute-start.18
  99.6 1.3 collective-permute-start.19
  101.2 7.7 collective-permute-start.21
  101.3 7.6 collective-permute-start.20
  108.9 1.2 collective-permute-start.22
  109.0 1.3 collective-permute-start.23
  110.7 7.6 collective-permute-start.25
  110.8 7.5 collective-permute-start.24
  118.3 1.2 collective-permute-start.26
  118.4 1.3 collective-permute-start.27
  120.1 7.6 collective-permute-start.29
  120.1 7.6 collective-permute-start.28
  127.7 1.2 collective-permute-start.30
  127.8 1.3 collective-permute-start.31
  148.7 3.7 collective-permute-start.32
  267.1 3.7 collective-permute-start.33
  387.7 3.7 collective-permute-start.34
  508.1 4.6 collective-permute-start.35
  629.6 1.2 collective-permute-start.36
  747.7 35.9 %copy-start.3 = (f32[9,9]{1,0:T(8,128)}, f32[9,9]{1,0:T(8,128)S(1)}, u32[]{:S(2)}) copy-start(f32[9,9]{1,0:T(8,128)S(1)} %broadcast_multiply_fusion.1) | copy-start | bytes 976
where the time goes:
time: 801 us; the launch traced here: 787 us
  other arithmetic  273 us (34%)
  local copies, waits for them, and re-layouts  265 us (33%)
  between operations  111 us (14%)
  starting transfers between devices  52.7 us (7%)
  blocking collectives  42.2 us (5%)
  waiting for transfers between devices  28.7 us (4%)
  matrix products  14.2 us (2%)
    reduce_sum x60, other arithmetic, orth_upper(): projection = jnp.sum(columns[row_index] * vector)  188 us
    scatter x180, local copies, waits for them, and re-layouts, orth_upper(): upper_rows = upper_rows.at[row_index, column_index].set(projection)  163 us
    another operation x49, local copies, waits for them, and re-layouts  78.4 us
    ppermute x16, starting transfers between devices, with_halo(): lax.ppermute(head, axis, [((i + 1) % count, i) for i in range(count)])  44 us
    psum x1, blocking collectives, per_device(): lax.psum(jnp.sum(forcing * forcing), ('gx', 'gy')) / cell_count  42.2 us
    reduce_sum x25, other arithmetic, orth_upper(): length = jnp.sqrt(jnp.sum(vector * vector))  40.6 us
    div x1, other arithmetic, upper_inverse(): inverse_rows[row_index] = accumulated / factor[row_index, row_index]  28.2 us
  transfers between devices with their start and end apart: 37, of which 26 were waited for; matrix products, arithmetic and copies ran while one was open for 2% of the time, Pallas kernels for 0%

commit v1 on v0

v1 whole, which is shorter than its diff:
```python
import jax
import jax.numpy as jnp
from jax import lax
from jax.experimental import pallas as pl
from jax.experimental.pallas import tpu as pltpu
from jax.sharding import PartitionSpec as P

BASIS = 9
HALO = 4

DIFFUSION = 0.03
CENTRE_SHIFT = 1.18
HALF_WIDTH = 0.95
EPSILON = 1e-06
LIFT = 1024.0
AXES = ("gx", "gy")
PAIRS = [(i, j) for i in range(BASIS) for j in range(i, BASIS)]
VMEM = pl.BlockSpec(memory_space=pltpu.VMEM)


def ring(axis, step):
    count = lax.axis_size(axis)
    return [(i, (i + step) % count) for i in range(count)]


def swap_x(to_low, to_high):
    return lax.ppermute(to_high, "gx", ring("gx", 1)), lax.ppermute(to_low, "gx", ring("gx", -1))


def swap_y(tile):
    if lax.axis_size("gy") == 2:
        return lax.ppermute(tile, "gy", ring("gy", 1))
    above = lax.ppermute(tile[:, :HALO], "gy", ring("gy", -1))
    below = lax.ppermute(tile[:, HALO:], "gy", ring("gy", 1))
    return jnp.concatenate([above, below], axis=1)


def edge_rows(block):
    rows = block.shape[-2]
    low, high = block[..., : 2 * HALO, :], block[..., rows - 2 * HALO :, :]
    lane = lax.broadcasted_iota(jnp.int32, low.shape, low.ndim - 2)
    return jnp.where(lane < HALO, low, high)


def doubled(centre, east, west, coef):
    rows, lanes = centre.shape
    north = pltpu.roll(centre, rows - 1, 0)
    south = pltpu.roll(centre, 1, 0)
    upper = pltpu.roll(centre, lanes - 1, 1)
    lower = pltpu.roll(centre, 1, 1)
    around = (east + west) + (north + south) + (upper + lower)
    slopes = coef[1] * (east - west) + coef[2] * (north - south) + coef[3] * (upper - lower)
    return coef[0] * centre + slopes - (2.0 * DIFFUSION / HALF_WIDTH) * around


def first_kernel(f, r, vel, low, high, own_rows, corner_rows, vectors, to_low, to_high, rows_out, coef, grid):
    bx, by, _ = f.shape
    h = HALO
    ext = bx + 2 * h
    grid[0, 0:h, 0:by] = low[0:h] * LIFT
    grid[0, h : h + bx, 0:by] = f[...] * LIFT
    grid[0, h + bx : ext, 0:by] = high[0:h] * LIFT
    grid[0, 0:h, by:] = corner_rows[0:h] * LIFT
    grid[0, h : h + bx, by:] = own_rows[0:bx] * LIFT
    half = low.shape[0]
    grid[0, h + bx : ext, by:] = corner_rows[half : half + h] * LIFT
    c = h - 1
    for k in range(4):
        scale = 2.0 / HALF_WIDTH if k == 0 else 1.0 / HALF_WIDTH
        shift = (6.0 * DIFFUSION - CENTRE_SHIFT) * scale if k == 0 else 0.0
        at = h + c * k
        coef[k, 0:c, 0:by] = low[at : at + c] * scale + shift
        coef[k, c : c + bx, 0:by] = (r[...] if k == 0 else vel[k - 1]) * scale + shift
        coef[k, c + bx :, 0:by] = high[at : at + c] * scale + shift
        coef[k, 0:c, by:] = corner_rows[at : at + c] * scale + shift
        coef[k, c : c + bx, by:] = own_rows[bx * (k + 1) : bx * (k + 2)] * scale + shift
        coef[k, c + bx :, by:] = corner_rows[half + at : half + at + c] * scale + shift
    for step in range(1, h + 1):

        def layer(x, carry, step=step):
            new = doubled(
                grid[step - 1, x], grid[step - 1, x + 1], grid[step - 1, x - 1], [coef[k, x - 1] for k in range(4)]
            )
            new = new * 0.5 if step == 1 else new - grid[step - 2, x]
            grid[step, x] = new
            return carry

        lax.fori_loop(step, ext - step, layer, 0)
    for step in range(h + 1):
        vectors[step] = grid[step, h : h + bx, 0:by]
    to_low[0:h] = grid[h, h : 2 * h, 0:by]
    to_low[h:] = grid[h - 1, h : 2 * h - 1, 0:by]
    to_high[0:h] = grid[h, bx : bx + h, 0:by]
    to_high[h:] = grid[h - 1, bx + 1 : bx + h, 0:by]
    rows_out[0:bx] = edge_rows(grid[h, h : h + bx, 0:by])
    rows_out[bx:] = edge_rows(grid[h - 1, h : h + bx, 0:by])


def second_kernel(vectors, coef, low, high, own_rows, corner_rows, later, gram, grid, sums):
    _, bx, by, nz = vectors.shape
    h = HALO
    ext = bx + 2 * h
    half = low.shape[0]
    last = h
    grid[1, 0:h, 0:by] = low[0:h]
    grid[1, h : h + bx, 0:by] = vectors[last]
    grid[1, h + bx : ext, 0:by] = high[0:h]
    grid[1, 0:h, by:] = corner_rows[0:h]
    grid[1, h : h + bx, by:] = own_rows[0:bx]
    grid[1, h + bx : ext, by:] = corner_rows[half : half + h]
    grid[0, 1:h, 0:by] = low[h:]
    grid[0, h : h + bx, 0:by] = vectors[last - 1]
    grid[0, h + bx : ext - 1, 0:by] = high[h:]
    grid[0, 1:h, by:] = corner_rows[h:half]
    grid[0, h : h + bx, by:] = own_rows[bx:]
    grid[0, h + bx : ext - 1, by:] = corner_rows[half + h :]
    for step in range(1, h + 1):

        def layer(x, carry, step=step):
            new = doubled(grid[step, x], grid[step, x + 1], grid[step, x - 1], [coef[k, x - 1] for k in range(4)])
            grid[step + 1, x] = new - grid[step - 1, x]
            return carry

        lax.fori_loop(step, ext - step, layer, 0)
    for step in range(h):
        later[step] = grid[step + 2, h : h + bx, 0:by]

    tiles = by // 8

    def products(at, totals):
        x, y = at // tiles, pl.multiple_of(at % tiles * 8, 8)
        for z in range(0, nz, 128):
            window = (pl.ds(y, 8), pl.ds(z, 128))
            cells = [vectors[(k, x) + window] for k in range(h + 1)]
            cells += [later[(k, x) + window] for k in range(h)]
            totals = tuple(t + cells[i] * cells[j] for t, (i, j) in zip(totals, PAIRS))
        return totals

    totals = lax.fori_loop(0, bx * tiles, products, tuple(jnp.zeros((8, 128), jnp.float32) for _ in PAIRS))
    sublane = lax.broadcasted_iota(jnp.int32, (8, 128), 0)
    sums[...] = jnp.zeros_like(sums)
    for base in range(0, len(PAIRS), 8):
        packed = jnp.zeros((8, 128), jnp.float32)
        for k, total in enumerate(totals[base : base + 8]):
            for distance in (4, 2, 1):
                total = total + pltpu.roll(total, distance, 0)
            packed = jnp.where(sublane == k, total, packed)
        sums[base : base + 8] = packed
    ones = jnp.ones(gram.shape, jnp.float32)
    gram[...] = lax.dot_general(
        ones, sums[...], (((1,), (1,)), ((), ())), precision=lax.Precision.HIGHEST, preferred_element_type=jnp.float32
    )


def last_kernel(cell_count, gram, vectors, later, out, factor, coef, result, sem):
    _, bx, by, nz = vectors.shape
    total = gram[0:8]
    for row in range(8, gram.shape[0], 8):
        total = total + gram[row : row + 8]
    for distance in (4, 2, 1):
        total = total + pltpu.roll(total, distance, 0)
    total = total * (1.0 / cell_count)
    entry = {}
    for k, (i, j) in enumerate(PAIRS):
        entry[i, j] = jnp.broadcast_to(total[:, k : k + 1], (8, 128))
    divisor = jnp.sqrt(entry[0, 0] * (1.0 / (LIFT * LIFT)) + EPSILON)
    scale = 1.0 / (divisor * LIFT)
    place = {pair: k for k, pair in enumerate(PAIRS)}
    for j in range(BASIS):
        length = jnp.sqrt(entry[j, j])
        inverse = 1.0 / length
        row = {k: entry[j, k] * inverse for k in range(j + 1, BASIS)}
        for i in range(j + 1, BASIS):
            for k in range(i, BASIS):
                entry[i, k] = entry[i, k] - row[i] * row[k]
        entry[j, j] = length
        coef[place[j, j]] = inverse
        for k in range(j + 1, BASIS):
            entry[j, k] = row[k]
            coef[place[j, k]] = row[k]
    sublane = lax.broadcasted_iota(jnp.int32, (8, 128), 0)
    lane = lax.broadcasted_iota(jnp.int32, (8, 128), 1)
    tops = []
    for base in range(0, BASIS, 8):
        packed = jnp.zeros((8, 128), jnp.float32)
        for (i, j), value in entry.items():
            if base <= i < base + 8:
                packed = jnp.where((sublane == i - base) & (lane == j), value, packed)
        tops.append(packed * scale)
    factor[...] = jnp.concatenate(tops, axis=0)[:BASIS, :BASIS]

    tiles = by // 8

    def solve(x, carry):
        for y in range(tiles):
            for z in range(0, nz, 128):
                window = (x, slice(8 * y, 8 * y + 8), slice(z, z + 128))
                columns = []
                for j in range(BASIS):
                    value = vectors[(j,) + window] if j <= HALO else later[(j - HALO - 1,) + window]
                    for i in range(j):
                        value = value - coef[place[i, j]] * columns[i]
                    value = value * coef[place[j, j]]
                    result[(j,) + window] = value
                    columns.append(value)
        pltpu.make_async_copy(result.at[:, x], out.at[:, x], sem.at[x]).start()
        return carry

    lax.fori_loop(0, bx, solve, 0)
    for x in range(bx):
        pltpu.make_async_copy(result.at[:, x], out.at[:, x], sem.at[x]).wait()


def shape(*dims):
    return jax.ShapeDtypeStruct(dims, jnp.float32)


def per_device(forcing, reaction, velocity):
    bx, by, nz = forcing.shape
    devices = lax.axis_size("gx") * lax.axis_size("gy")
    cell_count = float(bx * by * nz * devices)
    h, c, ext = HALO, HALO - 1, bx + 2 * HALO
    fields = [reaction, velocity[0], velocity[1], velocity[2]]
    params = pltpu.CompilerParams(vmem_limit_bytes=24 << 20)

    to_low = jnp.concatenate([forcing[:h]] + [v[:c] for v in fields])
    to_high = jnp.concatenate([forcing[bx - h :]] + [v[bx - c :] for v in fields])
    low, high = swap_x(to_low, to_high)
    own_rows = swap_y(edge_rows(jnp.concatenate([forcing] + fields)))
    corner_rows = swap_y(edge_rows(jnp.concatenate([low, high])))
    vectors, to_low, to_high, rows, coef = pl.pallas_call(
        first_kernel,
        out_shape=[
            shape(h + 1, bx, by, nz),
            shape(h + c, by, nz),
            shape(h + c, by, nz),
            shape(2 * bx, 2 * h, nz),
            shape(4, bx + 2 * c, by + 2 * h, nz),
        ],
        in_specs=[VMEM] * 7,
        out_specs=[VMEM] * 5,
        scratch_shapes=[pltpu.VMEM((h + 1, ext, by + 2 * h, nz), jnp.float32)],
        compiler_params=params,
        name="first",
    )(forcing, reaction, velocity, low, high, own_rows, corner_rows)

    low, high = swap_x(to_low, to_high)
    own_rows = swap_y(rows)
    corner_rows = swap_y(edge_rows(jnp.concatenate([low, high])))
    later, gram = pl.pallas_call(
        second_kernel,
        out_shape=[shape(h, bx, by, nz), shape(devices, 128)],
        in_specs=[VMEM] * 6,
        out_specs=[VMEM] * 2,
        scratch_shapes=[
            pltpu.VMEM((h + 2, ext, by + 2 * h, nz), jnp.float32),
            pltpu.VMEM((128, 128), jnp.float32),
        ],
        compiler_params=params,
        name="second",
    )(vectors, coef, low, high, own_rows, corner_rows)
    gram = lax.all_to_all(gram, AXES, 0, 0, tiled=True)

    def last(*refs):
        last_kernel(cell_count, *refs)

    return pl.pallas_call(
        last,
        out_shape=[shape(BASIS, bx, by, nz), shape(BASIS, BASIS)],
        in_specs=[VMEM] * 3,
        out_specs=[pl.BlockSpec(memory_space=pl.ANY), VMEM],
        scratch_shapes=[
            pltpu.VMEM((len(PAIRS), 8, 128), jnp.float32),
            pltpu.VMEM((BASIS, bx, by, nz), jnp.float32),
            pltpu.SemaphoreType.DMA((bx,)),
        ],
        compiler_params=params,
        name="last",
    )(gram, vectors, later)


def solution(mesh):
    in_specs = (P("gx", "gy", None), P("gx", "gy", None), P(None, "gx", "gy", None))
    out_specs = (P(None, "gx", "gy", None), P())
    return jax.shard_map(per_device, mesh=mesh, in_specs=in_specs, out_specs=out_specs, check_vma=False)
```

time: 801 us -> 72.6 us (0.09); the launches traced: 787 us -> 72.3 us
  other arithmetic: 273 us -> 0.28 us
  local copies, waits for them, and re-layouts: 265 us -> 3.26 us
  between operations: 111 us -> 0.82 us
  starting transfers between devices: 52.7 us -> 12.9 us
  blocking collectives: 42.2 us -> 11.2 us
  matrix products: 14.2 us -> 0 us
  Pallas kernels: 0 us -> 13.6 us
    reduce_sum x86 -> x0, other arithmetic: 231 us -> none  [the longest x60 188 us: orth_upper(): projection = jnp.sum(columns[row_index] * vector)]
    scatter x225 -> x0, local copies, waits for them, and re-layouts: 170 us -> none  [the longest x180 163 us: orth_upper(): upper_rows = upper_rows.at[row_index, column_index].set(projection)]
    another operation x60 -> x0, local copies, waits for them, and re-layouts: 88.8 us -> none
    psum x1 -> x0, blocking collectives: 42.2 us -> none  [per_device(): lax.psum(jnp.sum(forcing * forcing), ('gx', 'gy')) / cell_count]
    ppermute x37 -> x8, starting transfers between devices: 52.7 us -> 12.9 us  [the longest x2 10.1 us: swap_x(): lax.ppermute(to_low, 'gx', ring('gx', -1))]
    div x5 -> x0, other arithmetic: 29.5 us -> none  [the longest x1 28.2 us: upper_inverse(): inverse_rows[row_index] = accumulated / factor[row_index, row_index]]
    dot_general x2 -> x0, matrix products: 14.2 us -> none  [the longest x1 8.7 us: per_device(): jnp.dot(flattened, flattened.T, precision=lax.Precision.HIGHEST, preferre...]
    pallas_call x0 -> x3, Pallas kernels: none -> 13.6 us  [the longest x1 6.19 us: per_device(): pl.pallas_call(second_kernel, out_shape=[shape(h, bx, by, nz), shape(devi...]
  transfers between devices with their start and end apart: 37 -> 8, of which waited for: 26 -> 5; matrix products, arithmetic and copies ran while one was open for 2% -> 1% of each run, Pallas kernels for 0% -> 0%
where the time goes in v1:
time: 72.6 us; the launch traced here: 72.3 us
  waiting for transfers between devices  30.4 us (42%)
  Pallas kernels  13.6 us (19%)
  starting transfers between devices  12.9 us (18%)
  blocking collectives  11.2 us (15%)
  local copies, waits for them, and re-layouts  3.26 us (4%)
  between operations  0.82 us (1%)
    ppermute x2, waiting for transfers between devices, swap_x(): lax.ppermute(to_high, 'gx', ring('gx', 1))  26.9 us
    all_to_all x1, blocking collectives, per_device(): gram = lax.all_to_all(gram, AXES, 0, 0, tiled=True)  11.2 us
    ppermute x2, starting transfers between devices, swap_x(): lax.ppermute(to_low, 'gx', ring('gx', -1))  10.1 us
    pallas_call x1, Pallas kernels, per_device(): pl.pallas_call(second_kernel, out_shape=[shape(h, bx, by, nz), shape(devi...  6.19 us
    pallas_call x1, Pallas kernels, per_device(): pl.pallas_call(first_kernel, out_shape=[shape(h + 1, bx, by, nz), shape(h...  4.94 us
    unnamed x16, local copies, waits for them, and re-layouts  3.16 us
    ppermute x4, waiting for transfers between devices, swap_y(): return lax.ppermute(tile, 'gy', ring('gy', 1))  2.82 us
    ppermute x2, starting transfers between devices, swap_x(): lax.ppermute(to_high, 'gx', ring('gx', 1))  2.54 us
  transfers between devices with their start and end apart: 8, of which 5 were waited for; matrix products, arithmetic and copies ran while one was open for 1% of the time, Pallas kernels for 0%

profile of v1, /device:TPU:0, one launch (start us, length us, event | category | flops | bytes accessed | tf_op | source)
XLA Modules:
  0.0 72.3 jit_solution(7285880406783142874)
XLA Ops:
  0.6 0.0 copy-start.1
  0.6 0.0 copy-start.2
  0.7 0.0 copy-start
  0.7 1.1 %slice_dynamic-update-slice_fusion = (f32[16,32,256]{2,1,0:T(8,128)S(1)}, f32[16,32,256]{2,1,0:T(8,128)S(1)}) fusion(f32[8,32,256]{2,1,0:T(8,128)} %f.1), kind=kLoop, calls=%fused_computation.5 | loop fusion | bytes 524288
  1.8 1.0 %slice_dynamic-update-slice_fusion.2 = (f32[16,32,256]{2,1,0:T(8,128)S(1)}, f32[16,32,256]{2,1,0:T(8,128)S(1)}) fusion(f32[16,32,256]{2,1,0:T(8,128)S(1)} %get-tuple-element.24, f32[8,32,256]{2,1,0:T(8,128)} %r.1, f32[16,32,256]{2,1,0:T(8,128)S(1)} %get-tuple-element.25), kind=kLoop, calls=%fused_computation.14 | loop fusion | bytes 393216
  2.7 1.0 %bitcast_dynamic-update-slice_fusion.5 = (f32[16,32,256]{2,1,0:T(8,128)S(1)}, f32[16,32,256]{2,1,0:T(8,128)S(1)}) fusion(f32[16,32,256]{2,1,0:T(8,128)S(1)} %get-tuple-element.22, f32[3,8,32,256]{3,2,1,0:T(8,128)} %vel.1, f32[16,32,256]{2,1,0:T(8,128)S(1)} %get-tuple-element.23), kind=kLoop, calls=%fused_computation.10 | loop fusion | bytes 393216
  3.7 0.0 copy-done
  3.7 7.0 %collective-permute-start.1 = (f32[16,32,256]{2,1,0:T(8,128)S(1)}, f32[16,32,256]{2,1,0:T(8,128)S(1)}, u32[]{:S(2)}, u32[]{:S(2)}) collective-permute-start(f32[16,32,256]{2,1,0:T(8,128)S(1)} %get-tuple-element.16), channel_id=1, source_target_pairs={{0,30},{2,0},{4,2},{6,4},{8,6},{10,8},{12,10},{14,12},{16,14},{18,... | collective-permute-start | bytes 1572872 | tf_op jit(solution)/shard_map/ppermute | solution.py:27
  10.7 0.0 collective-permute-start
  10.7 0.0 copy-done.1
  10.7 0.0 copy-done.2
  10.9 0.1 slice_select_fusion
  11.0 0.1 collective-permute-start.2
  11.1 19.9 %collective-permute-done.low = f32[16,32,256]{2,1,0:T(8,128)S(1)} collective-permute-done((f32[16,32,256]{2,1,0:T(8,128)S(1)}, f32[16,32,256]{2,1,0:T(8,128)S(1)}, u32[]{:S(2)}, u32[]{:S(2)}) %collective-permute-start) | collective-permute-done | bytes 524320 | tf_op jit(solution)/shard_map/ppermute | solution.py:27
  31.0 0.0 collective-permute-done.1.high
  31.1 0.1 slice_select_fusion.1
  31.2 0.1 collective-permute-start.3
  31.3 0.0 collective-permute-done.2.own_rows
  31.3 1.5 %collective-permute-done.3.corner_rows = f32[32,8,256]{2,1,0:T(8,128)S(1)} collective-permute-done((f32[32,8,256]{2,1,0:T(8,128)S(1)}, f32[32,8,256]{2,1,0:T(8,128)S(1)}, u32[]{:S(2)}, u32[]{:S(2)}) %collective-permute-start.3) | collective-permute-done | bytes 262176 | tf_op jit(solution)/shard_map/ppermute | solution.py:32
  32.8 4.9 %first.1 = (f32[5,8,32,256]{3,2,1,0:T(8,128)S(1)}, f32[7,32,256]{2,1,0:T(8,128)S(1)}, f32[7,32,256]{2,1,0:T(8,128)S(1)}, f32[16,8,256]{2,1,0:T(8,128)S(1)}, f32[4,14,40,256]{3,2,1,0:T(8,128)S(1)}) custom-call(f32[8,32,256]{2,1,0:T(8,128)S(1)} %copy-done.1, f32[8,32,256]{2,1,0:T(8,128)S(1)} %copy-done.2, f32[3,8,32,256]{3,2,1,0:T(8,128)S(1)} %copy-done, ...), custom_call_target="tpu_custom_call" | custom-call | tf_op jit(solution)/shard_map/first/pallas_call | solution.py:231
  37.7 2.5 %collective-permute-start.4 = (f32[7,32,256]{2,1,0:T(8,128)S(1)}, f32[7,32,256]{2,1,0:T(8,128)S(1)}, u32[]{:S(2)}, u32[]{:S(2)}) collective-permute-start(f32[7,32,256]{2,1,0:T(8,128)S(1)} %get-tuple-element.11), channel_id=1, source_target_pairs={{0,2},{2,4},{4,6},{6,8},{8,10},{10,12},{12,14},{14,16},{16,18},{18... | collective-permute-start | bytes 688136 | tf_op jit(solution)/shard_map/ppermute | solution.py:27
  40.3 3.1 %collective-permute-start.5 = (f32[7,32,256]{2,1,0:T(8,128)S(1)}, f32[7,32,256]{2,1,0:T(8,128)S(1)}, u32[]{:S(2)}, u32[]{:S(2)}) collective-permute-start(f32[7,32,256]{2,1,0:T(8,128)S(1)} %get-tuple-element.12), channel_id=1, source_target_pairs={{0,30},{2,0},{4,2},{6,4},{8,6},{10,8},{12,10},{14,12},{16,14},{18,... | collective-permute-start | bytes 688136 | tf_op jit(solution)/shard_map/ppermute | solution.py:27
  43.4 0.0 collective-permute-start.6
  43.4 6.9 %collective-permute-done.4.low = f32[7,32,256]{2,1,0:T(8,128)S(1)} collective-permute-done((f32[7,32,256]{2,1,0:T(8,128)S(1)}, f32[7,32,256]{2,1,0:T(8,128)S(1)}, u32[]{:S(2)}, u32[]{:S(2)}) %collective-permute-start.4) | collective-permute-done | bytes 229408 | tf_op jit(solution)/shard_map/ppermute | solution.py:27
  50.4 0.7 collective-permute-done.5.high
  51.1 0.1 slice_select_fusion.2
  51.2 0.1 collective-permute-start.7
  51.3 0.0 collective-permute-done.6.own_rows
  51.3 1.3 %collective-permute-done.7.corner_rows = f32[14,8,256]{2,1,0:T(8,128)S(1)} collective-permute-done((f32[14,8,256]{2,1,0:T(8,128)S(1)}, f32[14,8,256]{2,1,0:T(8,128)S(1)}, u32[]{:S(2)}, u32[]{:S(2)}) %collective-permute-start.7) | collective-permute-done | bytes 114720 | tf_op jit(solution)/shard_map/ppermute | solution.py:32
  52.6 6.2 %second.1 = (f32[4,8,32,256]{3,2,1,0:T(8,128)S(1)}, f32[32,128]{1,0:T(8,128)S(1)}) custom-call(f32[5,8,32,256]{3,2,1,0:T(8,128)S(1)} %get-tuple-element.9.vectors.refs_1_, f32[4,14,40,256]{3,2,1,0:T(8,128)S(1)} %get-tuple-element.10.coef, f32[7,32,256]{2,1,0:T(8,128)S(1)} %collective-permute-done.4.low, f32[7,32,256]{2,1,0:T(8,128)S(1)} %collective-permute-done.5.high, ...), custom_call_target="tpu_custom_call" | custom-call | tf_op jit(solution)/shard_map/second/pallas_call | solution.py:250
  58.8 11.2 %all_to_all.11 = f32[32,1,128]{2,1,0:T(1,128)S(1)} all-to-all(f32[32,1,128]{2,1,0:T(1,128)S(1)} %bitcast.23), channel_id=1, replica_groups=mesh['gx'=16,'gy'=2] {'gx','gy'}, dimensions={0} | all-to-all | bytes 32768 | tf_op jit(solution)/shard_map/all_to_all | solution.py:262
  69.9 2.4 %last.1 = (f32[9,8,32,256]{3,2,1,0:T(8,128)}, f32[9,9]{1,0:T(8,128)}) custom-call(f32[32,128]{1,0:T(8,128)S(1)} %bitcast.22, f32[5,8,32,256]{3,2,1,0:T(8,128)S(1)} %get-tuple-element.9.vectors.refs_1_, f32[4,8,32,256]{3,2,1,0:T(8,128)S(1)} %get-tuple-element.15.refs_2_), custom_call_target="tpu_custom_call" | custom-call | tf_op jit(solution)/shard_map/last/pallas_call | solution.py:267
  (12 shorter events, 0.2 us)
Async XLA Ops:
  0.6 10.1 %copy-start.1 = (f32[8,32,256]{2,1,0:T(8,128)S(1)}, f32[8,32,256]{2,1,0:T(8,128)}, u32[]{:S(2)}) copy-start(f32[8,32,256]{2,1,0:T(8,128)} %f.1) | copy-start | bytes 786436
  0.6 10.1 %copy-start.2 = (f32[8,32,256]{2,1,0:T(8,128)S(1)}, f32[8,32,256]{2,1,0:T(8,128)}, u32[]{:S(2)}) copy-start(f32[8,32,256]{2,1,0:T(8,128)} %r.1) | copy-start | bytes 786436
  0.7 3.0 %copy-start = (f32[3,8,32,256]{3,2,1,0:T(8,128)S(1)}, f32[3,8,32,256]{3,2,1,0:T(8,128)}, u32[]{:S(2)}) copy-start(f32[3,8,32,256]{3,2,1,0:T(8,128)} %vel.1) | copy-start | bytes 2359300
  3.7 27.3 %collective-permute-start.1 = (f32[16,32,256]{2,1,0:T(8,128)S(1)}, f32[16,32,256]{2,1,0:T(8,128)S(1)}, u32[]{:S(2)}, u32[]{:S(2)}) collective-permute-start(f32[16,32,256]{2,1,0:T(8,128)S(1)} %get-tuple-element.16), channel_id=1, source_target_pairs={{0,30},{2,0},{4,2},{6,4},{8,6},{10,8},{12,10},{14,12},{16,14},{18,... | collective-permute-start | bytes 1572872 | tf_op jit(solution)/shard_map/ppermute | solution.py:27
  10.7 20.3 %collective-permute-start = (f32[16,32,256]{2,1,0:T(8,128)S(1)}, f32[16,32,256]{2,1,0:T(8,128)S(1)}, u32[]{:S(2)}, u32[]{:S(2)}) collective-permute-start(f32[16,32,256]{2,1,0:T(8,128)S(1)} %get-tuple-element.17), channel_id=1, source_target_pairs={{0,2},{2,4},{4,6},{6,8},{8,10},{10,12},{12,14},{14,16},{16,18},{18... | collective-permute-start | bytes 1572872 | tf_op jit(solution)/shard_map/ppermute | solution.py:27
  11.0 20.3 %collective-permute-start.2 = (f32[40,8,256]{2,1,0:T(8,128)S(1)}, f32[40,8,256]{2,1,0:T(8,128)S(1)}, u32[]{:S(2)}, u32[]{:S(2)}) collective-permute-start(f32[40,8,256]{2,1,0:T(8,128)S(1)} %slice_select_fusion), channel_id=1, source_target_pairs={{0,1},{1,0},{2,3},{3,2},{4,5},{5,4},{6,7},{7,6},{8,9},{9,8},{10,11... | collective-permute-start | bytes 983048 | tf_op jit(solution)/shard_map/ppermute | solution.py:32
  31.2 1.6 %collective-permute-start.3 = (f32[32,8,256]{2,1,0:T(8,128)S(1)}, f32[32,8,256]{2,1,0:T(8,128)S(1)}, u32[]{:S(2)}, u32[]{:S(2)}) collective-permute-start(f32[32,8,256]{2,1,0:T(8,128)S(1)} %slice_select_fusion.1), channel_id=1, source_target_pairs={{0,1},{1,0},{2,3},{3,2},{4,5},{5,4},{6,7},{7,6},{8,9},{9,8},{10,11... | collective-permute-start | bytes 786440 | tf_op jit(solution)/shard_map/ppermute | solution.py:32
  37.7 12.6 %collective-permute-start.4 = (f32[7,32,256]{2,1,0:T(8,128)S(1)}, f32[7,32,256]{2,1,0:T(8,128)S(1)}, u32[]{:S(2)}, u32[]{:S(2)}) collective-permute-start(f32[7,32,256]{2,1,0:T(8,128)S(1)} %get-tuple-element.11), channel_id=1, source_target_pairs={{0,2},{2,4},{4,6},{6,8},{8,10},{10,12},{12,14},{14,16},{16,18},{18... | collective-permute-start | bytes 688136 | tf_op jit(solution)/shard_map/ppermute | solution.py:27
  40.3 10.8 %collective-permute-start.5 = (f32[7,32,256]{2,1,0:T(8,128)S(1)}, f32[7,32,256]{2,1,0:T(8,128)S(1)}, u32[]{:S(2)}, u32[]{:S(2)}) collective-permute-start(f32[7,32,256]{2,1,0:T(8,128)S(1)} %get-tuple-element.12), channel_id=1, source_target_pairs={{0,30},{2,0},{4,2},{6,4},{8,6},{10,8},{12,10},{14,12},{16,14},{18,... | collective-permute-start | bytes 688136 | tf_op jit(solution)/shard_map/ppermute | solution.py:27
  43.4 7.8 %collective-permute-start.6 = (f32[16,8,256]{2,1,0:T(8,128)S(1)}, f32[16,8,256]{2,1,0:T(8,128)S(1)}, u32[]{:S(2)}, u32[]{:S(2)}) collective-permute-start(f32[16,8,256]{2,1,0:T(8,128)S(1)} %get-tuple-element.13), channel_id=1, source_target_pairs={{0,1},{1,0},{2,3},{3,2},{4,5},{5,4},{6,7},{7,6},{8,9},{9,8},{10,11... | collective-permute-start | bytes 393224 | tf_op jit(solution)/shard_map/ppermute | solution.py:32
  51.2 1.4 %collective-permute-start.7 = (f32[14,8,256]{2,1,0:T(8,128)S(1)}, f32[14,8,256]{2,1,0:T(8,128)S(1)}, u32[]{:S(2)}, u32[]{:S(2)}) collective-permute-start(f32[14,8,256]{2,1,0:T(8,128)S(1)} %slice_select_fusion.2), channel_id=1, source_target_pairs={{0,1},{1,0},{2,3},{3,2},{4,5},{5,4},{6,7},{7,6},{8,9},{9,8},{10,11... | collective-permute-start | bytes 344072 | tf_op jit(solution)/shard_map/ppermute | solution.py:32

commit v2 on v1

--- a/solution.py
+++ b/solution.py
@@ -85,7 +85,7 @@
             grid[step, x] = new
             return carry
 
-        lax.fori_loop(step, ext - step, layer, 0)
+        lax.fori_loop(step, ext - step, layer, 0, unroll=True)
     for step in range(h + 1):
         vectors[step] = grid[step, h : h + bx, 0:by]
     to_low[0:h] = grid[h, h : 2 * h, 0:by]
@@ -121,7 +121,7 @@
             grid[step + 1, x] = new - grid[step - 1, x]
             return carry
 
-        lax.fori_loop(step, ext - step, layer, 0)
+        lax.fori_loop(step, ext - step, layer, 0, unroll=True)
     for step in range(h):
         later[step] = grid[step + 2, h : h + bx, 0:by]
 

time: 72.6 us -> 66 us (0.909)
  Pallas kernels: 13.6 us -> 7.03 us
    pallas_call x1, Pallas kernels: 6.19 us -> 2.91 us  [per_device(): pl.pallas_call(second_kernel, out_shape=[shape(h, bx, by, nz), shape(devi...]
    pallas_call x1, Pallas kernels: 4.94 us -> 1.69 us  [per_device(): pl.pallas_call(first_kernel, out_shape=[shape(h + 1, bx, by, nz), shape(h...]
where the time goes in v2:
time: 66 us; the launch traced here: 65.8 us
  waiting for transfers between devices  30.4 us (46%)
  starting transfers between devices  12.9 us (20%)
  blocking collectives  11.2 us (17%)
  Pallas kernels  7.03 us (11%)
  local copies, waits for them, and re-layouts  3.26 us (5%)
  between operations  0.81 us (1%)
    ppermute x2, waiting for transfers between devices, swap_x(): lax.ppermute(to_high, 'gx', ring('gx', 1))  26.9 us
    all_to_all x1, blocking collectives, per_device(): gram = lax.all_to_all(gram, AXES, 0, 0, tiled=True)  11.2 us
    ppermute x2, starting transfers between devices, swap_x(): lax.ppermute(to_low, 'gx', ring('gx', -1))  10.1 us
    unnamed x16, local copies, waits for them, and re-layouts  3.16 us
    pallas_call x1, Pallas kernels, per_device(): pl.pallas_call(second_kernel, out_shape=[shape(h, bx, by, nz), shape(devi...  2.91 us
    ppermute x4, waiting for transfers between devices, swap_y(): return lax.ppermute(tile, 'gy', ring('gy', 1))  2.82 us
    ppermute x2, starting transfers between devices, swap_x(): lax.ppermute(to_high, 'gx', ring('gx', 1))  2.54 us
    pallas_call x1, Pallas kernels, per_device(): pl.pallas_call(last, out_shape=[shape(BASIS, bx, by, nz), shape(BASIS, BA...  2.42 us
  transfers between devices with their start and end apart: 8, of which 5 were waited for; matrix products, arithmetic and copies ran while one was open for 1% of the time, Pallas kernels for 0%

profile of v2, /device:TPU:0, one launch (start us, length us, event | category | flops | bytes accessed | tf_op | source)
XLA Modules:
  0.0 65.8 jit_solution(2049963171714903146)
XLA Ops:
  0.6 0.0 copy-start.1
  0.6 0.0 copy-start.2
  0.7 0.0 copy-start
  0.7 1.1 %slice_dynamic-update-slice_fusion = (f32[16,32,256]{2,1,0:T(8,128)S(1)}, f32[16,32,256]{2,1,0:T(8,128)S(1)}) fusion(f32[8,32,256]{2,1,0:T(8,128)} %f.1), kind=kLoop, calls=%fused_computation.5 | loop fusion | bytes 524288
  1.8 1.0 %slice_dynamic-update-slice_fusion.2 = (f32[16,32,256]{2,1,0:T(8,128)S(1)}, f32[16,32,256]{2,1,0:T(8,128)S(1)}) fusion(f32[16,32,256]{2,1,0:T(8,128)S(1)} %get-tuple-element.24, f32[8,32,256]{2,1,0:T(8,128)} %r.1, f32[16,32,256]{2,1,0:T(8,128)S(1)} %get-tuple-element.25), kind=kLoop, calls=%fused_computation.14 | loop fusion | bytes 393216
  2.7 1.0 %bitcast_dynamic-update-slice_fusion.5 = (f32[16,32,256]{2,1,0:T(8,128)S(1)}, f32[16,32,256]{2,1,0:T(8,128)S(1)}) fusion(f32[16,32,256]{2,1,0:T(8,128)S(1)} %get-tuple-element.22, f32[3,8,32,256]{3,2,1,0:T(8,128)} %vel.1, f32[16,32,256]{2,1,0:T(8,128)S(1)} %get-tuple-element.23), kind=kLoop, calls=%fused_computation.10 | loop fusion | bytes 393216
  3.7 0.0 copy-done
  3.7 7.0 %collective-permute-start.1 = (f32[16,32,256]{2,1,0:T(8,128)S(1)}, f32[16,32,256]{2,1,0:T(8,128)S(1)}, u32[]{:S(2)}, u32[]{:S(2)}) collective-permute-start(f32[16,32,256]{2,1,0:T(8,128)S(1)} %get-tuple-element.16), channel_id=1, source_target_pairs={{0,30},{2,0},{4,2},{6,4},{8,6},{10,8},{12,10},{14,12},{16,14},{18,... | collective-permute-start | bytes 1572872 | tf_op jit(solution)/shard_map/ppermute | solution.py:27
  10.7 0.0 collective-permute-start
  10.7 0.0 copy-done.1
  10.7 0.0 copy-done.2
  10.9 0.1 slice_select_fusion
  11.0 0.1 collective-permute-start.2
  11.1 19.9 %collective-permute-done.low = f32[16,32,256]{2,1,0:T(8,128)S(1)} collective-permute-done((f32[16,32,256]{2,1,0:T(8,128)S(1)}, f32[16,32,256]{2,1,0:T(8,128)S(1)}, u32[]{:S(2)}, u32[]{:S(2)}) %collective-permute-start) | collective-permute-done | bytes 524320 | tf_op jit(solution)/shard_map/ppermute | solution.py:27
  31.0 0.0 collective-permute-done.1.high
  31.1 0.1 slice_select_fusion.1
  31.2 0.1 collective-permute-start.3
  31.3 0.0 collective-permute-done.2.own_rows
  31.3 1.5 %collective-permute-done.3.corner_rows = f32[32,8,256]{2,1,0:T(8,128)S(1)} collective-permute-done((f32[32,8,256]{2,1,0:T(8,128)S(1)}, f32[32,8,256]{2,1,0:T(8,128)S(1)}, u32[]{:S(2)}, u32[]{:S(2)}) %collective-permute-start.3) | collective-permute-done | bytes 262176 | tf_op jit(solution)/shard_map/ppermute | solution.py:32
  32.8 1.7 %first.1 = (f32[5,8,32,256]{3,2,1,0:T(8,128)S(1)}, f32[7,32,256]{2,1,0:T(8,128)S(1)}, f32[7,32,256]{2,1,0:T(8,128)S(1)}, f32[16,8,256]{2,1,0:T(8,128)S(1)}, f32[4,14,40,256]{3,2,1,0:T(8,128)S(1)}) custom-call(f32[8,32,256]{2,1,0:T(8,128)S(1)} %copy-done.1, f32[8,32,256]{2,1,0:T(8,128)S(1)} %copy-done.2, f32[3,8,32,256]{3,2,1,0:T(8,128)S(1)} %copy-done, ...), custom_call_target="tpu_custom_call" | custom-call | tf_op jit(solution)/shard_map/first/pallas_call | solution.py:231
  34.5 2.5 %collective-permute-start.4 = (f32[7,32,256]{2,1,0:T(8,128)S(1)}, f32[7,32,256]{2,1,0:T(8,128)S(1)}, u32[]{:S(2)}, u32[]{:S(2)}) collective-permute-start(f32[7,32,256]{2,1,0:T(8,128)S(1)} %get-tuple-element.11), channel_id=1, source_target_pairs={{0,2},{2,4},{4,6},{6,8},{8,10},{10,12},{12,14},{14,16},{16,18},{18... | collective-permute-start | bytes 688136 | tf_op jit(solution)/shard_map/ppermute | solution.py:27
  37.0 3.1 %collective-permute-start.5 = (f32[7,32,256]{2,1,0:T(8,128)S(1)}, f32[7,32,256]{2,1,0:T(8,128)S(1)}, u32[]{:S(2)}, u32[]{:S(2)}) collective-permute-start(f32[7,32,256]{2,1,0:T(8,128)S(1)} %get-tuple-element.12), channel_id=1, source_target_pairs={{0,30},{2,0},{4,2},{6,4},{8,6},{10,8},{12,10},{14,12},{16,14},{18,... | collective-permute-start | bytes 688136 | tf_op jit(solution)/shard_map/ppermute | solution.py:27
  40.2 0.0 collective-permute-start.6
  40.2 6.9 %collective-permute-done.4.low = f32[7,32,256]{2,1,0:T(8,128)S(1)} collective-permute-done((f32[7,32,256]{2,1,0:T(8,128)S(1)}, f32[7,32,256]{2,1,0:T(8,128)S(1)}, u32[]{:S(2)}, u32[]{:S(2)}) %collective-permute-start.4) | collective-permute-done | bytes 229408 | tf_op jit(solution)/shard_map/ppermute | solution.py:27
  47.1 0.7 %collective-permute-done.5.high = f32[7,32,256]{2,1,0:T(8,128)S(1)} collective-permute-done((f32[7,32,256]{2,1,0:T(8,128)S(1)}, f32[7,32,256]{2,1,0:T(8,128)S(1)}, u32[]{:S(2)}, u32[]{:S(2)}) %collective-permute-start.5) | collective-permute-done | bytes 229408 | tf_op jit(solution)/shard_map/ppermute | solution.py:27
  47.9 0.1 slice_select_fusion.2
  48.0 0.1 collective-permute-start.7
  48.0 0.0 collective-permute-done.6.own_rows
  48.0 1.3 %collective-permute-done.7.corner_rows = f32[14,8,256]{2,1,0:T(8,128)S(1)} collective-permute-done((f32[14,8,256]{2,1,0:T(8,128)S(1)}, f32[14,8,256]{2,1,0:T(8,128)S(1)}, u32[]{:S(2)}, u32[]{:S(2)}) %collective-permute-start.7) | collective-permute-done | bytes 114720 | tf_op jit(solution)/shard_map/ppermute | solution.py:32
  49.3 2.9 %second.1 = (f32[4,8,32,256]{3,2,1,0:T(8,128)S(1)}, f32[32,128]{1,0:T(8,128)S(1)}) custom-call(f32[5,8,32,256]{3,2,1,0:T(8,128)S(1)} %get-tuple-element.9.vectors.refs_1_, f32[4,14,40,256]{3,2,1,0:T(8,128)S(1)} %get-tuple-element.10.coef, f32[7,32,256]{2,1,0:T(8,128)S(1)} %collective-permute-done.4.low, f32[7,32,256]{2,1,0:T(8,128)S(1)} %collective-permute-done.5.high, ...), custom_call_target="tpu_custom_call" | custom-call | tf_op jit(solution)/shard_map/second/pallas_call | solution.py:250
  52.2 11.2 %all_to_all.11 = f32[32,1,128]{2,1,0:T(1,128)S(1)} all-to-all(f32[32,1,128]{2,1,0:T(1,128)S(1)} %bitcast.23), channel_id=1, replica_groups=mesh['gx'=16,'gy'=2] {'gx','gy'}, dimensions={0} | all-to-all | bytes 32768 | tf_op jit(solution)/shard_map/all_to_all | solution.py:262
  63.4 2.4 %last.1 = (f32[9,8,32,256]{3,2,1,0:T(8,128)}, f32[9,9]{1,0:T(8,128)}) custom-call(f32[32,128]{1,0:T(8,128)S(1)} %bitcast.22, f32[5,8,32,256]{3,2,1,0:T(8,128)S(1)} %get-tuple-element.9.vectors.refs_1_, f32[4,8,32,256]{3,2,1,0:T(8,128)S(1)} %get-tuple-element.15.refs_2_), custom_call_target="tpu_custom_call" | custom-call | tf_op jit(solution)/shard_map/last/pallas_call | solution.py:267
  (12 shorter events, 0.2 us)
Async XLA Ops:
  0.6 10.1 %copy-start.1 = (f32[8,32,256]{2,1,0:T(8,128)S(1)}, f32[8,32,256]{2,1,0:T(8,128)}, u32[]{:S(2)}) copy-start(f32[8,32,256]{2,1,0:T(8,128)} %f.1) | copy-start | bytes 786436
  0.6 10.1 %copy-start.2 = (f32[8,32,256]{2,1,0:T(8,128)S(1)}, f32[8,32,256]{2,1,0:T(8,128)}, u32[]{:S(2)}) copy-start(f32[8,32,256]{2,1,0:T(8,128)} %r.1) | copy-start | bytes 786436
  0.7 3.0 %copy-start = (f32[3,8,32,256]{3,2,1,0:T(8,128)S(1)}, f32[3,8,32,256]{3,2,1,0:T(8,128)}, u32[]{:S(2)}) copy-start(f32[3,8,32,256]{3,2,1,0:T(8,128)} %vel.1) | copy-start | bytes 2359300
  3.7 27.3 %collective-permute-start.1 = (f32[16,32,256]{2,1,0:T(8,128)S(1)}, f32[16,32,256]{2,1,0:T(8,128)S(1)}, u32[]{:S(2)}, u32[]{:S(2)}) collective-permute-start(f32[16,32,256]{2,1,0:T(8,128)S(1)} %get-tuple-element.16), channel_id=1, source_target_pairs={{0,30},{2,0},{4,2},{6,4},{8,6},{10,8},{12,10},{14,12},{16,14},{18,... | collective-permute-start | bytes 1572872 | tf_op jit(solution)/shard_map/ppermute | solution.py:27
  10.7 20.3 %collective-permute-start = (f32[16,32,256]{2,1,0:T(8,128)S(1)}, f32[16,32,256]{2,1,0:T(8,128)S(1)}, u32[]{:S(2)}, u32[]{:S(2)}) collective-permute-start(f32[16,32,256]{2,1,0:T(8,128)S(1)} %get-tuple-element.17), channel_id=1, source_target_pairs={{0,2},{2,4},{4,6},{6,8},{8,10},{10,12},{12,14},{14,16},{16,18},{18... | collective-permute-start | bytes 1572872 | tf_op jit(solution)/shard_map/ppermute | solution.py:27
  11.0 20.3 %collective-permute-start.2 = (f32[40,8,256]{2,1,0:T(8,128)S(1)}, f32[40,8,256]{2,1,0:T(8,128)S(1)}, u32[]{:S(2)}, u32[]{:S(2)}) collective-permute-start(f32[40,8,256]{2,1,0:T(8,128)S(1)} %slice_select_fusion), channel_id=1, source_target_pairs={{0,1},{1,0},{2,3},{3,2},{4,5},{5,4},{6,7},{7,6},{8,9},{9,8},{10,11... | collective-permute-start | bytes 983048 | tf_op jit(solution)/shard_map/ppermute | solution.py:32
  31.2 1.6 %collective-permute-start.3 = (f32[32,8,256]{2,1,0:T(8,128)S(1)}, f32[32,8,256]{2,1,0:T(8,128)S(1)}, u32[]{:S(2)}, u32[]{:S(2)}) collective-permute-start(f32[32,8,256]{2,1,0:T(8,128)S(1)} %slice_select_fusion.1), channel_id=1, source_target_pairs={{0,1},{1,0},{2,3},{3,2},{4,5},{5,4},{6,7},{7,6},{8,9},{9,8},{10,11... | collective-permute-start | bytes 786440 | tf_op jit(solution)/shard_map/ppermute | solution.py:32
  34.5 12.6 %collective-permute-start.4 = (f32[7,32,256]{2,1,0:T(8,128)S(1)}, f32[7,32,256]{2,1,0:T(8,128)S(1)}, u32[]{:S(2)}, u32[]{:S(2)}) collective-permute-start(f32[7,32,256]{2,1,0:T(8,128)S(1)} %get-tuple-element.11), channel_id=1, source_target_pairs={{0,2},{2,4},{4,6},{6,8},{8,10},{10,12},{12,14},{14,16},{16,18},{18... | collective-permute-start | bytes 688136 | tf_op jit(solution)/shard_map/ppermute | solution.py:27
  37.0 10.8 %collective-permute-start.5 = (f32[7,32,256]{2,1,0:T(8,128)S(1)}, f32[7,32,256]{2,1,0:T(8,128)S(1)}, u32[]{:S(2)}, u32[]{:S(2)}) collective-permute-start(f32[7,32,256]{2,1,0:T(8,128)S(1)} %get-tuple-element.12), channel_id=1, source_target_pairs={{0,30},{2,0},{4,2},{6,4},{8,6},{10,8},{12,10},{14,12},{16,14},{18,... | collective-permute-start | bytes 688136 | tf_op jit(solution)/shard_map/ppermute | solution.py:27
  40.2 7.8 %collective-permute-start.6 = (f32[16,8,256]{2,1,0:T(8,128)S(1)}, f32[16,8,256]{2,1,0:T(8,128)S(1)}, u32[]{:S(2)}, u32[]{:S(2)}) collective-permute-start(f32[16,8,256]{2,1,0:T(8,128)S(1)} %get-tuple-element.13), channel_id=1, source_target_pairs={{0,1},{1,0},{2,3},{3,2},{4,5},{5,4},{6,7},{7,6},{8,9},{9,8},{10,11... | collective-permute-start | bytes 393224 | tf_op jit(solution)/shard_map/ppermute | solution.py:32
  48.0 1.4 %collective-permute-start.7 = (f32[14,8,256]{2,1,0:T(8,128)S(1)}, f32[14,8,256]{2,1,0:T(8,128)S(1)}, u32[]{:S(2)}, u32[]{:S(2)}) collective-permute-start(f32[14,8,256]{2,1,0:T(8,128)S(1)} %slice_select_fusion.2), channel_id=1, source_target_pairs={{0,1},{1,0},{2,3},{3,2},{4,5},{5,4},{6,7},{7,6},{8,9},{9,8},{10,11... | collective-permute-start | bytes 344072 | tf_op jit(solution)/shard_map/ppermute | solution.py:32

commit v3 on v2

v3 whole, which is shorter than its diff:
```python
import jax
import jax.numpy as jnp
from jax import lax
from jax.experimental import pallas as pl
from jax.experimental.pallas import tpu as pltpu
from jax.sharding import PartitionSpec as P

BASIS = 9
STEPS = 4
MARGIN = 8
EDGE = 4

DIFFUSION = 0.03
CENTRE_SHIFT = 1.18
HALF_WIDTH = 0.95
EPSILON = 1e-06
LIFT = 1024.0
SCALES = (2.0 / HALF_WIDTH, 1.0 / HALF_WIDTH, 1.0 / HALF_WIDTH, 1.0 / HALF_WIDTH)
SHIFTS = (2.0 * (6.0 * DIFFUSION - CENTRE_SHIFT) / HALF_WIDTH, 0.0, 0.0, 0.0)
AXES = ("gx", "gy")
VMEM = pl.BlockSpec(memory_space=pltpu.VMEM)
HBM = pl.BlockSpec(memory_space=pltpu.MemorySpace.HBM)


COMPUTED = ((1, 1), (2, 1), (2, 2), (3, 1))
GIVEN = ((0, 1), (0, 2), (1, 2))
TIP = (2, 2)
DEPTHS = (2, 1, 2, 1, 1)
OFFSETS = (0, 2, 3, 5, 6)


def pairs_of(low, high):
    return [(i, j) for j in range(low, high) for i in range(j + 1)]


GROUPS = (pairs_of(0, STEPS + 1), pairs_of(STEPS + 1, BASIS))
STARTS = (0, -(-len(GROUPS[0]) // 8) * 8)
GRAM_ROWS = STARTS[1] - (-len(GROUPS[1]) // 8) * 8
PLACE = {pair: start + k for start, group in zip(STARTS, GROUPS) for k, pair in enumerate(group)}


def ring(axis, step):
    count = lax.axis_size(axis)
    return [(i, (i + step) % count) for i in range(count)]


def swap_x(to_low, to_high):
    return lax.ppermute(to_high, "gx", ring("gx", 1)), lax.ppermute(to_low, "gx", ring("gx", -1))


def swap_y(block):
    rows = block.shape[1]
    return swap_rows(block[:, :MARGIN], block[:, rows - MARGIN :])


def swap_rows(low, high):
    if lax.axis_size("gy") == 2:
        return lax.ppermute(jnp.concatenate([low, high], axis=1), "gy", ring("gy", 1))
    above = lax.ppermute(low, "gy", ring("gy", -1))
    below = lax.ppermute(high, "gy", ring("gy", 1))
    return jnp.concatenate([above, below], axis=1)


def doubled(centre, east, west, coef):
    rows, lanes = centre.shape
    kept = east.shape[0]
    north = pltpu.roll(centre, rows - 1, 0)[:kept]
    south = pltpu.roll(centre, 1, 0)[:kept]
    centre = centre[:kept]
    upper = pltpu.roll(centre, lanes - 1, 1)
    lower = pltpu.roll(centre, 1, 1)
    around = (east + west) + (north + south) + (upper + lower)
    slopes = coef[1] * (east - west) + coef[2] * (north - south) + coef[3] * (upper - lower)
    return coef[0] * centre + slopes - (2.0 * DIFFUSION / HALF_WIDTH) * around


def scaled(k, value):
    return value * SCALES[k] + SHIFTS[k]


def products(pairs, bx, by, nz, cell):
    needed = sorted({i for pair in pairs for i in pair})
    tiles = by // 8

    def add(at, totals):
        x, y = at // tiles, pl.multiple_of(at % tiles * 8, 8)
        for z in range(0, nz, 128):
            cells = {i: cell(i, x, pl.ds(y, 8), pl.ds(z, 128)) for i in needed}
            totals = tuple(t + cells[i] * cells[j] for t, (i, j) in zip(totals, pairs))
        return totals

    totals = lax.fori_loop(0, bx * tiles, add, tuple(jnp.zeros((8, 128), jnp.float32) for _ in pairs), unroll=2)
    sublane = lax.broadcasted_iota(jnp.int32, (8, 128), 0)
    rows = []
    for base in range(0, len(pairs), 8):
        packed = jnp.zeros((8, 128), jnp.float32)
        for k, total in enumerate(totals[base : base + 8]):
            for distance in (4, 2, 1):
                total = total + pltpu.roll(total, distance, 0)
            packed = jnp.where(sublane == k, total, packed)
        rows.append(packed)
    return rows


def reader(start, one, two=None):
    def cell(i, x, y, z):
        if i == 0:
            return start[x, y, z]
        if i <= STEPS:
            return one[i - 1, x, y, z]
        return two[i - 1 - STEPS, x, y, z]

    return cell


def second_interior_kernel(by, start, one, coef, given, vectors, gram):
    del given
    bx, _, nz = start.shape
    places = own_places(bx, STEPS, vectors)
    cells = Cells(bx, coef, None, lambda j, x: places[j, x])
    for x in (1, 2, bx - 3, bx - 2):
        cells.known[STEPS + 1, x] = lambda x=x: vectors[0, x]
    for x in range(bx):
        cells.known[STEPS, x] = lambda x=x: one[STEPS - 1, x]
        cells.known[STEPS - 1, x] = lambda x=x: one[STEPS - 2, x]
    cells.interior(STEPS)
    for k, row in enumerate(products(GROUPS[0], bx, by, nz, reader(start, one))):
        gram[8 * k : 8 * k + 8] = row


def copy_all(copies, sem):
    copies = [pltpu.make_async_copy(a, b, sem.at[k]) for k, (a, b) in enumerate(copies)]
    for copy in copies:
        copy.start()
    for copy in copies:
        copy.wait()


def fields_of(f, r, vel):
    return f, r, vel.at[0], vel.at[1], vel.at[2]


REACH = ((0, 3),) + ((1, 3),) * 4
SWAPPED = tuple(sum(2 * (high - low) for low, high in REACH[:k]) for k in range(6))


def edge_rows(block):
    rows = block.shape[-2]
    low, high = block[..., : 2 * EDGE, :], block[..., rows - 2 * EDGE :, :]
    row = lax.broadcasted_iota(jnp.int32, low.shape, low.ndim - 2)
    return jnp.where(row < EDGE, low, high)


def pack_kernel(f, r, vel, fields, to_low, to_high, rows, sem):
    bx = f.shape[0]
    copy_all([(field, fields.at[k]) for k, field in enumerate(fields_of(f, r, vel))], sem)
    for k in range(5):
        depth, at = DEPTHS[k], OFFSETS[k]
        to_low[at : at + depth] = fields[k, 0:depth]
        to_high[at : at + depth] = fields[k, bx - depth : bx]
        (low, high), at = REACH[k], SWAPPED[k]
        rows[at : at + high - low] = edge_rows(fields[k, low:high])
        rows[at + high - low : at + 2 * (high - low)] = edge_rows(fields[k, bx - high : bx - low])


def inner_kernel(fields, rows, to_low, to_high, scratch):
    _, bx, by, _ = fields.shape

    def layer(k, x):
        (low, high), at = REACH[k], SWAPPED[k]
        at += x - low if x < high else high - low + x - (bx - high)
        return jnp.concatenate([fields[k, x], rows[at]], axis=0)

    class Coefficients:
        shape = (4, bx)

        def __getitem__(self, at):
            return scaled(at[0], layer(at[0] + 1, at[1]))

    cells = Cells(bx, Coefficients(), None, lambda j, x: (scratch, {1: 0, 2: 1, bx - 3: 2, bx - 2: 3}[x]))
    for x in (0, 1, 2, 3, bx - 4, bx - 3, bx - 2, bx - 1):
        if 3 <= x < bx - 3:
            cells.known[0, x] = lambda x=x: jnp.concatenate([fields[0, x], jnp.zeros_like(rows[0])], axis=0) * LIFT
        else:
            cells.known[0, x] = lambda x=x: layer(0, x) * LIFT
    to_low[0] = cells.get(1, 1)[:by]
    to_high[0] = cells.get(1, bx - 2)[:by]
    to_low[1] = cells.tip(0, 1, True)[:by]
    to_high[1] = cells.tip(0, bx - 2, False)[:by]


class Cells:
    def __init__(self, bx, coef, edge, place):
        self.bx, self.coef, self.edge, self.place = bx, coef, edge, place
        self.known, self.computed = {}, {}

    def coefficients(self, x):
        if 0 <= x < self.bx:
            return [self.coef[k, x] for k in range(4)]
        return [self.edge[k, 0 if x < 0 else 1] for k in range(4)]

    def get(self, j, x):
        if (j, x) not in self.known:
            if (j, x) in self.computed:
                new = self.computed[j, x]()
            else:
                new = doubled(self.get(j - 1, x), self.get(j - 1, x + 1), self.get(j - 1, x - 1), self.coefficients(x))
                new = new * 0.5 if j == 1 else new - self.get(j - 2, x)
            ref, at = self.place(j, x)
            ref[at] = new
            self.known[j, x] = lambda: ref[at]
        return self.known[j, x]()

    def tip(self, base, x, below):
        j = base + TIP[0]
        centre, beyond = self.get(j - 1, x), self.get(j - 1, x + 1 if below else x - 1)
        nothing = jnp.zeros_like(centre)
        pair = (beyond, nothing) if below else (nothing, beyond)
        return doubled(centre, *pair, self.coefficients(x)) - self.get(j - 2, x)

    def interior(self, base):
        for j in range(1, STEPS):
            for x in range(j, self.bx - j):
                self.get(base + j, x)

    def finish(self, base):
        for j in range(1, STEPS + 1):
            reach = max([m for i, m in COMPUTED if i == j], default=0)
            for x in range(-reach, self.bx + reach):
                self.get(base + j, x)


def halo_layer(bx, m, low_side):
    return -m if low_side else bx - 1 + m


def own_places(bx, base, ref):
    return {(base + j, x): (ref, (j - 1, x)) for j in range(1, STEPS + 1) for x in range(bx)}


def mark_interior(cells, bx, base, ref):
    for j in range(1, STEPS):
        for x in range(j, bx - j):
            cells.known[base + j, x] = lambda j=j, x=x: ref[j - 1, x]


def halo_places(bx, base, scratch, sides=None):
    places, slot = {}, 0
    for j, m in COMPUTED:
        for low_side in (True, False):
            at = (base + j, halo_layer(bx, m, low_side))
            if sides is not None and (j, m) == (STEPS - 1, 1):
                places[at] = (sides, 0 if low_side else 1)
            else:
                places[at] = (scratch, slot)
                slot += 1
    return places


def prepare_kernel(fields, rows, start, coef, vectors):
    _, bx, by, _ = fields.shape
    start[:, 0:by] = fields[0] * LIFT
    start[:, by:] = rows[0:bx] * LIFT
    for k in range(4):
        coef[k, :, 0:by] = scaled(k, fields[k + 1])
        coef[k, :, by:] = scaled(k, rows[bx * (k + 1) : bx * (k + 2)])
    places = own_places(bx, 0, vectors)
    cells = Cells(bx, coef, None, lambda j, x: places[j, x])
    for x in range(bx):
        cells.known[0, x] = lambda x=x: start[x]
    cells.interior(0)


def first_kernel(
    start, coef, low, high, low_later, high_later, corner, given, vectors, to_low, to_high, following, sides, edge, weight, scratch
):
    del given
    bx, by = start.shape[0], low.shape[1]
    size, later = low.shape[0], low_later.shape[0]
    places = own_places(bx, 0, vectors) | own_places(bx, STEPS, following) | halo_places(bx, 0, scratch, sides)
    for side, slab, base in ((0, low, 0), (1, high, size)):
        for k in range(4):
            depth, at = DEPTHS[k + 1], OFFSETS[k + 1]
            at += depth - 1 if side == 0 else 0
            edge[k, side, 0:by] = scaled(k, slab[at])
            edge[k, side, by:] = scaled(k, corner[base + at])
        at = OFFSETS[2] + (0 if side == 0 else 1)
        sign = SCALES[1] if side == 0 else -SCALES[1]
        weight[side, 0:by] = slab[at] * sign - 2.0 * DIFFUSION / HALF_WIDTH
        weight[side, by:] = corner[base + at] * sign - 2.0 * DIFFUSION / HALF_WIDTH
    cells = Cells(bx, coef, edge, lambda j, x: places[j, x])
    mark_interior(cells, bx, 0, vectors)
    for x in range(bx):
        cells.known[0, x] = lambda x=x: start[x]
    for side, slab, after, base, after_base in (
        (0, low, low_later, 0, 2 * size),
        (1, high, high_later, size, 2 * size + later),
    ):

        def wide(ref, at, offset):
            return jnp.concatenate([ref[at], corner[offset + at]], axis=0)

        def starting(m, side=side, slab=slab, base=base):
            return wide(slab, DEPTHS[0] - m if side == 0 else m - 1, base) * LIFT

        near, far = halo_layer(bx, 1, side == 0), halo_layer(bx, 2, side == 0)
        cells.known[0, near] = lambda f=starting: f(1)
        cells.known[0, far] = lambda f=starting: f(2)
        cells.known[1, far] = lambda a=after, o=after_base: wide(a, 0, o)
        cells.computed[2, far] = lambda a=after, o=after_base, side=side, near=near: (
            wide(a, 1, o) + weight[side] * cells.get(1, near)
        )
    cells.finish(0)
    for out, below, one, two in ((to_low, True, 0, 1), (to_high, False, bx - 1, bx - 2)):
        leaving = [
            cells.get(STEPS, one),
            cells.get(STEPS, two),
            cells.get(STEPS + 1, two),
            cells.tip(STEPS, two, below),
        ]
        for at, layer in enumerate(leaving):
            above, under = layer[by : by + MARGIN], layer[by + MARGIN :]
            row = lax.broadcasted_iota(jnp.int32, above.shape, 0)
            out[at, 0:by] = layer[:by]
            out[at, by:] = jnp.where(row < EDGE, above, under)


def second_kernel(start, one, given, sides, coef, edge, weight, low, high, early_gram, two, gram, scratch):
    del given
    bx, _, nz = start.shape
    by = low.shape[1] - 2 * EDGE
    places = own_places(bx, STEPS, two) | halo_places(bx, STEPS, scratch)
    cells = Cells(bx, coef, edge, lambda j, x: places[j, x])
    mark_interior(cells, bx, STEPS, two)
    for x in range(bx):
        cells.known[STEPS, x] = lambda x=x: one[STEPS - 1, x]
        cells.known[STEPS - 1, x] = lambda x=x: one[STEPS - 2, x]
    for side, slab in ((0, low), (1, high)):
        near, far = halo_layer(bx, 1, side == 0), halo_layer(bx, 2, side == 0)

        def wide(at, slab=slab):
            return jnp.concatenate([slab[at], slab[at, by:]], axis=0)

        cells.known[STEPS - 1, near] = lambda side=side: sides[side]
        cells.known[STEPS, near] = lambda f=wide: f(0)
        cells.known[STEPS, far] = lambda f=wide: f(1)
        cells.known[STEPS + 1, far] = lambda f=wide: f(2)
        cells.computed[STEPS + 2, far] = lambda f=wide, side=side, near=near: (
            f(3) + weight[side] * cells.get(STEPS + 1, near)
        )
    cells.finish(STEPS)
    rows = products(GROUPS[1], bx, by, nz, reader(start, one, two))
    sums = jnp.concatenate([early_gram[...]] + rows, axis=0)
    on = lax.broadcasted_iota(jnp.int32, sums.shape, 0) == lax.broadcasted_iota(jnp.int32, sums.shape, 1)
    line = jnp.sum(jnp.where(on, jnp.sum(sums, axis=1, keepdims=True), 0.0), axis=0, keepdims=True)
    gram[...] = jnp.broadcast_to(line, gram.shape)


def last_kernel(cell_count, gram, start, one, two, out, factor, coef, result, sem):
    _, bx, by, nz = result.shape
    total = gram[0:8]
    for row in range(8, gram.shape[0], 8):
        total = total + gram[row : row + 8]
    for distance in (4, 2, 1):
        total = total + pltpu.roll(total, distance, 0)
    total = total * (1.0 / cell_count)
    entry = {pair: jnp.broadcast_to(total[:, k : k + 1], (8, 128)) for pair, k in PLACE.items()}
    divisor = jnp.sqrt(entry[0, 0] * (1.0 / (LIFT * LIFT)) + EPSILON)
    scale = 1.0 / (divisor * LIFT)
    for j in range(BASIS):
        length = jnp.sqrt(entry[j, j])
        inverse = 1.0 / length
        row = {k: entry[j, k] * inverse for k in range(j + 1, BASIS)}
        for i in range(j + 1, BASIS):
            for k in range(i, BASIS):
                entry[i, k] = entry[i, k] - row[i] * row[k]
        entry[j, j] = length
        coef[PLACE[j, j]] = inverse
        for k in range(j + 1, BASIS):
            entry[j, k] = row[k]
            coef[PLACE[j, k]] = row[k]
    cell = reader(start, one, two)
    tiles = by // 8

    def solve(x, carry):
        for y in range(0, tiles, 2):
            windows = [
                (x, slice(8 * t, 8 * t + 8), slice(z, z + 128))
                for t in range(y, min(y + 2, tiles))
                for z in range(0, nz, 128)
            ]
            columns = []
            for j in range(BASIS):
                values = [cell(j, *window) for window in windows]
                for i in range(j):
                    factor_ = coef[PLACE[i, j]]
                    values = [v - factor_ * c for v, c in zip(values, columns[i])]
                factor_ = coef[PLACE[j, j]]
                values = [v * factor_ for v in values]
                for window, value in zip(windows, values):
                    result[(j,) + window] = value
                columns.append(values)
        pltpu.make_async_copy(result.at[:, x], out.at[:, x], sem.at[x]).start()
        return carry

    lax.fori_loop(0, bx, solve, 0)
    sublane = lax.broadcasted_iota(jnp.int32, (8, 128), 0)
    lane = lax.broadcasted_iota(jnp.int32, (8, 128), 1)
    tops = []
    for base in range(0, BASIS, 8):
        packed = jnp.zeros((8, 128), jnp.float32)
        for (i, j), value in entry.items():
            if base <= i < base + 8:
                packed = jnp.where((sublane == i - base) & (lane == j), value, packed)
        tops.append(packed * scale)
    factor[...] = jnp.concatenate(tops, axis=0)[:BASIS, :BASIS]
    for x in range(bx):
        pltpu.make_async_copy(result.at[:, x], out.at[:, x], sem.at[x]).wait()


def shape(*dims):
    return jax.ShapeDtypeStruct(dims, jnp.float32)


def call(kernel, outs, *args, name, scratch=(), us=0.02, in_specs=None, out_specs=None, aliases=None):
    return pl.pallas_call(
        kernel,
        out_shape=outs,
        in_specs=in_specs or [VMEM] * len(args),
        out_specs=out_specs or [VMEM] * len(outs),
        scratch_shapes=scratch,
        input_output_aliases=aliases or {},
        compiler_params=pltpu.CompilerParams(vmem_limit_bytes=24 << 20),
        cost_estimate=pl.CostEstimate(flops=0, transcendentals=0, bytes_accessed=int(us * 3e6)),
        name=name,
    )(*args)


def per_device(forcing, reaction, velocity):
    bx, by, nz = forcing.shape
    devices = lax.axis_size("gx") * lax.axis_size("gy")
    cell_count = float(bx * by * nz * devices)
    wide = by + 2 * MARGIN
    inputs = tuple(pltpu.with_memory_space_constraint(v, pltpu.MemorySpace.HBM) for v in (forcing, reaction, velocity))
    vectors = shape(STEPS, bx, wide, nz)
    fields, to_low, to_high, rows = call(
        pack_kernel,
        [shape(5, bx, by, nz)] + [shape(sum(DEPTHS), by, nz)] * 2 + [shape(SWAPPED[5], 2 * EDGE, nz)],
        *inputs,
        name="pack",
        in_specs=[HBM] * 3,
        scratch=[pltpu.SemaphoreType.DMA((5,))],
    )
    low, high = swap_x(to_low, to_high)
    rows = swap_rows(rows[:, :EDGE], rows[:, EDGE:])
    to_low, to_high = call(
        inner_kernel,
        [shape(2, by, nz)] * 2,
        fields,
        rows,
        name="inner",
        scratch=[pltpu.VMEM((4, by + 2 * EDGE, nz), jnp.float32)],
    )
    low_later, high_later = swap_x(to_low, to_high)
    rows = swap_y(fields.reshape(5 * bx, by, nz))
    start, coef, one = call(
        prepare_kernel, [shape(bx, wide, nz), shape(4, bx, wide, nz), vectors], fields, rows, name="prepare"
    )
    corner = swap_y(jnp.concatenate([low, high, low_later, high_later]))
    one, to_low, to_high, two, sides, edge, weight = call(
        first_kernel,
        [
            vectors,
            shape(4, by + 2 * EDGE, nz),
            shape(4, by + 2 * EDGE, nz),
            vectors,
            shape(2, wide, nz),
            shape(4, 2, wide, nz),
            shape(2, wide, nz),
        ],
        start,
        coef,
        low,
        high,
        low_later,
        high_later,
        corner,
        one,
        name="first",
        scratch=[pltpu.VMEM((2 * len(COMPUTED), wide, nz), jnp.float32)],
        aliases={7: 0},
    )
    low, high = swap_x(to_low, to_high)
    two, early_gram = call(
        lambda *refs: second_interior_kernel(by, *refs),
        [vectors, shape(STARTS[1], 128)],
        start,
        one,
        coef,
        two,
        name="second_interior",
        aliases={3: 0},
    )
    two, gram = call(
        second_kernel,
        [vectors, shape(devices, 128)],
        start,
        one,
        two,
        sides,
        coef,
        edge,
        weight,
        low,
        high,
        early_gram,
        name="second",
        scratch=[pltpu.VMEM((2 * len(COMPUTED), wide, nz), jnp.float32)],
        aliases={2: 0},
    )
    gram = lax.all_to_all(gram, AXES, 0, 0, tiled=True)
    return call(
        lambda *refs: last_kernel(cell_count, *refs),
        [shape(BASIS, bx, by, nz), shape(BASIS, BASIS)],
        gram,
        start,
        one,
        two,
        name="last",
        out_specs=[pl.BlockSpec(memory_space=pl.ANY), VMEM],
        scratch=[
            pltpu.VMEM((GRAM_ROWS, 8, 128), jnp.float32),
            pltpu.VMEM((BASIS, bx, by, nz), jnp.float32),
            pltpu.SemaphoreType.DMA((bx,)),
        ],
    )


def solution(mesh):
    in_specs = (P("gx", "gy", None), P("gx", "gy", None), P(None, "gx", "gy", None))
    out_specs = (P(None, "gx", "gy", None), P())
    return jax.shard_map(per_device, mesh=mesh, in_specs=in_specs, out_specs=out_specs, check_vma=False)
```

time: 66 us -> 50.7 us (0.77)
  waiting for transfers between devices: 30.4 us -> 10.2 us
  starting transfers between devices: 12.9 us -> 18.7 us
  local copies, waits for them, and re-layouts: 3.26 us -> 0.11 us
  Pallas kernels: 7.03 us -> 9.19 us
    ppermute x2 -> x3, waiting for transfers between devices: 26.9 us -> 5.82 us  [swap_x(): lax.ppermute(to_high, 'gx', ring('gx', 1))]
    ppermute x2 -> x3, starting transfers between devices: 10.1 us -> 13.8 us  [swap_x(): lax.ppermute(to_low, 'gx', ring('gx', -1))]
    unnamed x16 -> x3, local copies, waits for them, and re-layouts: 3.16 us -> 0.04 us
    ppermute x2 -> x3, waiting for transfers between devices: 0.72 us -> 3.48 us  [swap_x(): lax.ppermute(to_low, 'gx', ring('gx', -1))]
    pallas_call x3 -> x7, Pallas kernels: 7.03 us -> 9.19 us  [call(): pl.pallas_call(kernel, out_shape=outs, in_specs=in_specs or [VMEM] * len(...]
    ppermute x4 -> x3, waiting for transfers between devices: 2.82 us -> 0.9 us  [swap_rows(): lax.ppermute(jnp.concatenate([low, high], axis=1), 'gy', ring('gy', 1))]
    ppermute x2 -> x3, starting transfers between devices: 2.54 us -> 4.15 us  [swap_x(): lax.ppermute(to_high, 'gx', ring('gx', 1))]
  transfers between devices with their start and end apart: 8 -> 9, of which waited for: 5 -> 7; matrix products, arithmetic and copies ran while one was open for 1% -> 0% of each run, Pallas kernels for 0% -> 3%
where the time goes in v3:
time: 50.7 us; the launch traced here: 50.5 us
  starting transfers between devices  18.7 us (37%)
  blocking collectives  11.5 us (23%)
  waiting for transfers between devices  10.2 us (20%)
  Pallas kernels  9.19 us (18%)
  between operations  0.73 us (1%)
    ppermute x3, starting transfers between devices, swap_x(): lax.ppermute(to_low, 'gx', ring('gx', -1))  13.8 us
    all_to_all x1, blocking collectives, per_device(): gram = lax.all_to_all(gram, AXES, 0, 0, tiled=True)  11.5 us
    pallas_call x7, Pallas kernels, call(): pl.pallas_call(kernel, out_shape=outs, in_specs=in_specs or [VMEM] * len(...  9.19 us
    ppermute x3, waiting for transfers between devices, swap_x(): lax.ppermute(to_high, 'gx', ring('gx', 1))  5.82 us
    ppermute x3, starting transfers between devices, swap_x(): lax.ppermute(to_high, 'gx', ring('gx', 1))  4.15 us
    ppermute x3, waiting for transfers between devices, swap_x(): lax.ppermute(to_low, 'gx', ring('gx', -1))  3.48 us
  transfers between devices with their start and end apart: 9, of which 7 were waited for; matrix products, arithmetic and copies ran while one was open for 0% of the time, Pallas kernels for 3%

profile of v3, /device:TPU:0, one launch (start us, length us, event | category | flops | bytes accessed | tf_op | source)
XLA Modules:
  0.0 50.5 jit_solution(3098389139182339970)
XLA Ops:
  0.6 1.4 %pack.1 = (f32[5,8,32,256]{3,2,1,0:T(8,128)S(1)}, f32[7,32,256]{2,1,0:T(8,128)S(1)}, f32[7,32,256]{2,1,0:T(8,128)S(1)}, f32[22,8,256]{2,1,0:T(8,128)S(1)}) custom-call(f32[8,32,256]{2,1,0:T(8,128)} %f.1, f32[8,32,256]{2,1,0:T(8,128)} %r.1, f32[3,8,32,256]{3,2,1,0:T(8,128)} %vel.1), custom_call_target="tpu_custom_call" | custom-call | bytes 60000 | tf_op jit(solution)/shard_map/pack/pallas_call | solution.py:426
  2.0 0.5 %collective-permute-start.3 = (f32[22,8,256]{2,1,0:T(8,128)S(1)}, f32[22,8,256]{2,1,0:T(8,128)S(1)}, u32[]{:S(2)}, u32[]{:S(2)}) collective-permute-start(f32[22,8,256]{2,1,0:T(8,128)S(1)} %get-tuple-element.27), channel_id=1, source_target_pairs={{0,1},{1,0},{2,3},{3,2},{4,5},{5,4},{6,7},{7,6},{8,9},{9,8},{10,11... | collective-permute-start | bytes 540680 | tf_op jit(solution)/shard_map/ppermute | solution.py:58
  2.5 2.6 %collective-permute-start.1 = (f32[7,32,256]{2,1,0:T(8,128)S(1)}, f32[7,32,256]{2,1,0:T(8,128)S(1)}, u32[]{:S(2)}, u32[]{:S(2)}) collective-permute-start(f32[7,32,256]{2,1,0:T(8,128)S(1)} %get-tuple-element.25), channel_id=1, source_target_pairs={{0,2},{2,4},{4,6},{6,8},{8,10},{10,12},{12,14},{14,16},{16,18},{18... | collective-permute-start | bytes 688136 | tf_op jit(solution)/shard_map/ppermute | solution.py:48
  5.1 4.1 %collective-permute-start.2 = (f32[7,32,256]{2,1,0:T(8,128)S(1)}, f32[7,32,256]{2,1,0:T(8,128)S(1)}, u32[]{:S(2)}, u32[]{:S(2)}) collective-permute-start(f32[7,32,256]{2,1,0:T(8,128)S(1)} %get-tuple-element.26), channel_id=1, source_target_pairs={{0,30},{2,0},{4,2},{6,4},{8,6},{10,8},{12,10},{14,12},{16,14},{18,... | collective-permute-start | bytes 688136 | tf_op jit(solution)/shard_map/ppermute | solution.py:48
  9.3 0.1 collective-permute-start
  9.4 0.0 collective-permute-done.3.rows
  9.4 0.3 inner.1
  9.7 0.1 collective-permute-start.4
  9.7 5.6 %collective-permute-start.5 = (f32[2,32,256]{2,1,0:T(8,128)S(1)}, f32[2,32,256]{2,1,0:T(8,128)S(1)}, u32[]{:S(2)}, u32[]{:S(2)}) collective-permute-start(f32[2,32,256]{2,1,0:T(8,128)S(1)} %get-tuple-element.29), channel_id=1, source_target_pairs={{0,30},{2,0},{4,2},{6,4},{8,6},{10,8},{12,10},{14,12},{16,14},{18,... | collective-permute-start | bytes 196616 | tf_op jit(solution)/shard_map/ppermute | solution.py:48
  15.3 2.0 %collective-permute-done.1.low = f32[7,32,256]{2,1,0:T(8,128)S(1)} collective-permute-done((f32[7,32,256]{2,1,0:T(8,128)S(1)}, f32[7,32,256]{2,1,0:T(8,128)S(1)}, u32[]{:S(2)}, u32[]{:S(2)}) %collective-permute-start.1) | collective-permute-done | bytes 229408 | tf_op jit(solution)/shard_map/ppermute | solution.py:48
  17.3 0.5 %collective-permute-done.2.high = f32[7,32,256]{2,1,0:T(8,128)S(1)} collective-permute-done((f32[7,32,256]{2,1,0:T(8,128)S(1)}, f32[7,32,256]{2,1,0:T(8,128)S(1)}, u32[]{:S(2)}, u32[]{:S(2)}) %collective-permute-start.2) | collective-permute-done | bytes 229408 | tf_op jit(solution)/shard_map/ppermute | solution.py:48
  17.9 0.4 collective-permute-done.4.low_later
  18.3 1.9 %collective-permute-done.5.high_later = f32[2,32,256]{2,1,0:T(8,128)S(1)} collective-permute-done((f32[2,32,256]{2,1,0:T(8,128)S(1)}, f32[2,32,256]{2,1,0:T(8,128)S(1)}, u32[]{:S(2)}, u32[]{:S(2)}) %collective-permute-start.5) | collective-permute-done | bytes 65568 | tf_op jit(solution)/shard_map/ppermute | solution.py:48
  20.3 0.1 collective-permute-start.6
  20.3 0.0 collective-permute-done.rows
  20.4 0.7 %prepare.1 = (f32[8,48,256]{2,1,0:T(8,128)S(1)}, f32[4,8,48,256]{3,2,1,0:T(8,128)S(1)}, f32[4,8,48,256]{3,2,1,0:T(8,128)S(1)}) custom-call(f32[5,8,32,256]{3,2,1,0:T(8,128)S(1)} %get-tuple-element.22.fields, f32[40,16,256]{2,1,0:T(8,128)S(1)} %collective-permute-done.rows), custom_call_target="tpu_custom_call" | custom-call | bytes 60000 | tf_op jit(solution)/shard_map/prepare/pallas_call | solution.py:426
  21.0 0.9 %collective-permute-done.6.corner = f32[18,16,256]{2,1,0:T(8,128)S(1)} collective-permute-done((f32[18,16,256]{2,1,0:T(8,128)S(1)}, f32[18,16,256]{2,1,0:T(8,128)S(1)}, u32[]{:S(2)}, u32[]{:S(2)}) %collective-permute-start.6) | collective-permute-done | bytes 294944 | tf_op jit(solution)/shard_map/ppermute | solution.py:58
  21.9 1.5 %first.1 = (f32[4,8,48,256]{3,2,1,0:T(8,128)S(1)}, f32[4,40,256]{2,1,0:T(8,128)S(1)}, f32[4,40,256]{2,1,0:T(8,128)S(1)}, f32[4,8,48,256]{3,2,1,0:T(8,128)S(1)}, ...) custom-call(f32[8,48,256]{2,1,0:T(8,128)S(1)} %get-tuple-element.23., ...), custom_call_target="tpu_custom_call", output_to_operand_aliasing={{0}: (7, {})} | custom-call | bytes 60000 | tf_op jit(solution)/shard_map/first/pallas_call | solution.py:426
  23.4 1.5 %collective-permute-start.7 = (f32[4,40,256]{2,1,0:T(8,128)S(1)}, f32[4,40,256]{2,1,0:T(8,128)S(1)}, u32[]{:S(2)}, u32[]{:S(2)}) collective-permute-start(f32[4,40,256]{2,1,0:T(8,128)S(1)} %get-tuple-element.37), channel_id=1, source_target_pairs={{0,2},{2,4},{4,6},{6,8},{8,10},{10,12},{12,14},{14,16},{16,18},{18... | collective-permute-start | bytes 491528 | tf_op jit(solution)/shard_map/ppermute | solution.py:48
  24.9 4.1 %collective-permute-start.8 = (f32[4,40,256]{2,1,0:T(8,128)S(1)}, f32[4,40,256]{2,1,0:T(8,128)S(1)}, u32[]{:S(2)}, u32[]{:S(2)}) collective-permute-start(f32[4,40,256]{2,1,0:T(8,128)S(1)} %get-tuple-element.38), channel_id=1, source_target_pairs={{0,30},{2,0},{4,2},{6,4},{8,6},{10,8},{12,10},{14,12},{16,14},{18,... | collective-permute-start | bytes 491528 | tf_op jit(solution)/shard_map/ppermute | solution.py:48
  29.1 0.9 %second_interior.1 = (f32[4,8,48,256]{3,2,1,0:T(8,128)S(1)}, f32[16,128]{1,0:T(8,128)S(1)}) custom-call(f32[8,48,256]{2,1,0:T(8,128)S(1)} %get-tuple-element.23.start.refs_0_.refs_1_, f32[4,8,48,256]{3,2,1,0:T(8,128)S(1)} %get-tuple-element.31.refs_1_.one.refs_2_, ...), custom_call_target="tpu_custom_call", output_to_operand_aliasing={{0}: (3, {})} | custom-call | bytes 60000 | tf_op jit(solution)/shard_map/second_interior/pallas_call | solution.py:426
  29.9 3.5 %collective-permute-done.7.low = f32[4,40,256]{2,1,0:T(8,128)S(1)} collective-permute-done((f32[4,40,256]{2,1,0:T(8,128)S(1)}, f32[4,40,256]{2,1,0:T(8,128)S(1)}, u32[]{:S(2)}, u32[]{:S(2)}) %collective-permute-start.7) | collective-permute-done | bytes 163872 | tf_op jit(solution)/shard_map/ppermute | solution.py:48
  33.4 1.0 %collective-permute-done.8.high = f32[4,40,256]{2,1,0:T(8,128)S(1)} collective-permute-done((f32[4,40,256]{2,1,0:T(8,128)S(1)}, f32[4,40,256]{2,1,0:T(8,128)S(1)}, u32[]{:S(2)}, u32[]{:S(2)}) %collective-permute-start.8) | collective-permute-done | bytes 163872 | tf_op jit(solution)/shard_map/ppermute | solution.py:48
  34.4 2.1 %second.1 = (f32[4,8,48,256]{3,2,1,0:T(8,128)S(1)}, f32[32,128]{1,0:T(8,128)S(1)}) custom-call(f32[8,48,256]{2,1,0:T(8,128)S(1)} %get-tuple-element.23.start.refs_0_.refs_1_, f32[4,8,48,256]{3,2,1,0:T(8,128)S(1)} %get-tuple-element.31.refs_1_.one.refs_2_, f32[4,8,48,256]{3,2,1,0:T(8,128)S(1)} %get-tuple-element.33.given, ...), custom_call_target="tpu_custom_call", output_to_operand_aliasing={{0}: (2, {})} | custom-call | bytes 60000 | tf_op jit(solution)/shard_map/second/pallas_call | solution.py:426
  36.5 11.5 %all_to_all.11 = f32[32,1,128]{2,1,0:T(1,128)S(1)} all-to-all(f32[32,1,128]{2,1,0:T(1,128)S(1)} %bitcast.7), channel_id=1, replica_groups=mesh['gx'=16,'gy'=2] {'gx','gy'}, dimensions={0} | all-to-all | bytes 32768 | tf_op jit(solution)/shard_map/all_to_all | solution.py:521
  48.0 2.5 %last.1 = (f32[9,8,32,256]{3,2,1,0:T(8,128)}, f32[9,9]{1,0:T(8,128)}) custom-call(f32[32,128]{1,0:T(8,128)S(1)} %bitcast.6, f32[8,48,256]{2,1,0:T(8,128)S(1)} %get-tuple-element.23.start.refs_0_.refs_1_, f32[4,8,48,256]{3,2,1,0:T(8,128)S(1)} %get-tuple-element.31.refs_1_.one.refs_2_, f32[4,8,48,256]{3,2,1,0:T(8,128)S(1)} %get-tuple-element.41.refs_3_), custom_call_target="tpu_custom_call" | custom-call | bytes 60000 | tf_op jit(solution)/shard_map/last/pallas_call | solution.py:426
  (8 shorter events, 0.2 us)
Async XLA Ops:
  2.0 7.4 %collective-permute-start.3 = (f32[22,8,256]{2,1,0:T(8,128)S(1)}, f32[22,8,256]{2,1,0:T(8,128)S(1)}, u32[]{:S(2)}, u32[]{:S(2)}) collective-permute-start(f32[22,8,256]{2,1,0:T(8,128)S(1)} %get-tuple-element.27), channel_id=1, source_target_pairs={{0,1},{1,0},{2,3},{3,2},{4,5},{5,4},{6,7},{7,6},{8,9},{9,8},{10,11... | collective-permute-start | bytes 540680 | tf_op jit(solution)/shard_map/ppermute | solution.py:58
  2.5 14.8 %collective-permute-start.1 = (f32[7,32,256]{2,1,0:T(8,128)S(1)}, f32[7,32,256]{2,1,0:T(8,128)S(1)}, u32[]{:S(2)}, u32[]{:S(2)}) collective-permute-start(f32[7,32,256]{2,1,0:T(8,128)S(1)} %get-tuple-element.25), channel_id=1, source_target_pairs={{0,2},{2,4},{4,6},{6,8},{8,10},{10,12},{12,14},{14,16},{16,18},{18... | collective-permute-start | bytes 688136 | tf_op jit(solution)/shard_map/ppermute | solution.py:48
  5.1 12.8 %collective-permute-start.2 = (f32[7,32,256]{2,1,0:T(8,128)S(1)}, f32[7,32,256]{2,1,0:T(8,128)S(1)}, u32[]{:S(2)}, u32[]{:S(2)}) collective-permute-start(f32[7,32,256]{2,1,0:T(8,128)S(1)} %get-tuple-element.26), channel_id=1, source_target_pairs={{0,30},{2,0},{4,2},{6,4},{8,6},{10,8},{12,10},{14,12},{16,14},{18,... | collective-permute-start | bytes 688136 | tf_op jit(solution)/shard_map/ppermute | solution.py:48
  9.3 11.1 %collective-permute-start = (f32[40,16,256]{2,1,0:T(8,128)S(1)}, f32[40,16,256]{2,1,0:T(8,128)S(1)}, u32[]{:S(2)}, u32[]{:S(2)}) collective-permute-start(f32[40,16,256]{2,1,0:T(8,128)S(1)} %pad_maximum_fusion), channel_id=1, source_target_pairs={{0,1},{1,0},{2,3},{3,2},{4,5},{5,4},{6,7},{7,6},{8,9},{9,8},{10,11... | collective-permute-start | bytes 1966088 | tf_op jit(solution)/shard_map/ppermute | solution.py:58
  9.7 8.6 %collective-permute-start.4 = (f32[2,32,256]{2,1,0:T(8,128)S(1)}, f32[2,32,256]{2,1,0:T(8,128)S(1)}, u32[]{:S(2)}, u32[]{:S(2)}) collective-permute-start(f32[2,32,256]{2,1,0:T(8,128)S(1)} %get-tuple-element.28), channel_id=1, source_target_pairs={{0,2},{2,4},{4,6},{6,8},{8,10},{10,12},{12,14},{14,16},{16,18},{18... | collective-permute-start | bytes 196616 | tf_op jit(solution)/shard_map/ppermute | solution.py:48
  9.7 10.5 %collective-permute-start.5 = (f32[2,32,256]{2,1,0:T(8,128)S(1)}, f32[2,32,256]{2,1,0:T(8,128)S(1)}, u32[]{:S(2)}, u32[]{:S(2)}) collective-permute-start(f32[2,32,256]{2,1,0:T(8,128)S(1)} %get-tuple-element.29), channel_id=1, source_target_pairs={{0,30},{2,0},{4,2},{6,4},{8,6},{10,8},{12,10},{14,12},{16,14},{18,... | collective-permute-start | bytes 196616 | tf_op jit(solution)/shard_map/ppermute | solution.py:48
  20.3 1.6 %collective-permute-start.6 = (f32[18,16,256]{2,1,0:T(8,128)S(1)}, f32[18,16,256]{2,1,0:T(8,128)S(1)}, u32[]{:S(2)}, u32[]{:S(2)}) collective-permute-start(f32[18,16,256]{2,1,0:T(8,128)S(1)} %pad_maximum_fusion.1), channel_id=1, source_target_pairs={{0,1},{1,0},{2,3},{3,2},{4,5},{5,4},{6,7},{7,6},{8,9},{9,8},{10,11... | collective-permute-start | bytes 884744 | tf_op jit(solution)/shard_map/ppermute | solution.py:58
  23.4 10.0 %collective-permute-start.7 = (f32[4,40,256]{2,1,0:T(8,128)S(1)}, f32[4,40,256]{2,1,0:T(8,128)S(1)}, u32[]{:S(2)}, u32[]{:S(2)}) collective-permute-start(f32[4,40,256]{2,1,0:T(8,128)S(1)} %get-tuple-element.37), channel_id=1, source_target_pairs={{0,2},{2,4},{4,6},{6,8},{8,10},{10,12},{12,14},{14,16},{16,18},{18... | collective-permute-start | bytes 491528 | tf_op jit(solution)/shard_map/ppermute | solution.py:48
  24.9 9.5 %collective-permute-start.8 = (f32[4,40,256]{2,1,0:T(8,128)S(1)}, f32[4,40,256]{2,1,0:T(8,128)S(1)}, u32[]{:S(2)}, u32[]{:S(2)}) collective-permute-start(f32[4,40,256]{2,1,0:T(8,128)S(1)} %get-tuple-element.38), channel_id=1, source_target_pairs={{0,30},{2,0},{4,2},{6,4},{8,6},{10,8},{12,10},{14,12},{16,14},{18,... | collective-permute-start | bytes 491528 | tf_op jit(solution)/shard_map/ppermute | solution.py:48

commit v4 on v3

--- a/solution.py
+++ b/solution.py
@@ -128,14 +128,6 @@
         gram[8 * k : 8 * k + 8] = row
 
 
-def copy_all(copies, sem):
-    copies = [pltpu.make_async_copy(a, b, sem.at[k]) for k, (a, b) in enumerate(copies)]
-    for copy in copies:
-        copy.start()
-    for copy in copies:
-        copy.wait()
-
-
 def fields_of(f, r, vel):
     return f, r, vel.at[0], vel.at[1], vel.at[2]
 
@@ -153,8 +145,11 @@
 
 def pack_kernel(f, r, vel, fields, to_low, to_high, rows, sem):
     bx = f.shape[0]
-    copy_all([(field, fields.at[k]) for k, field in enumerate(fields_of(f, r, vel))], sem)
+    copies = [pltpu.make_async_copy(field, fields.at[k], sem.at[k]) for k, field in enumerate(fields_of(f, r, vel))]
+    for copy in copies:
+        copy.start()
     for k in range(5):
+        copies[k].wait()
         depth, at = DEPTHS[k], OFFSETS[k]
         to_low[at : at + depth] = fields[k, 0:depth]
         to_high[at : at + depth] = fields[k, bx - depth : bx]
@@ -271,13 +266,32 @@
     cells.interior(0)
 
 
-def first_kernel(
-    start, coef, low, high, low_later, high_later, corner, given, vectors, to_low, to_high, following, sides, edge, weight, scratch
-):
+def wide_layer(slab, corner, at, base):
+    return jnp.concatenate([slab[at], corner[base + at]], axis=0)
+
+
+def know_start(cells, start, low, high, corner):
+    bx, size = start.shape[0], low.shape[0]
+    for x in range(bx):
+        cells.known[0, x] = lambda x=x: start[x]
+    for side, slab, base in ((0, low, 0), (1, high, size)):
+        for m in (1, 2):
+            at = DEPTHS[0] - m if side == 0 else m - 1
+            cells.known[0, halo_layer(bx, m, side == 0)] = lambda slab=slab, base=base, at=at: (
+                wide_layer(slab, corner, at, base) * LIFT
+            )
+
+
+def early_range(j, bx):
+    return range(j - 2, bx - (j - 2))
+
+
+def first_kernel(start, coef, low, high, corner, given, vectors, beside, edge, weight):
     del given
     bx, by = start.shape[0], low.shape[1]
-    size, later = low.shape[0], low_later.shape[0]
-    places = own_places(bx, 0, vectors) | own_places(bx, STEPS, following) | halo_places(bx, 0, scratch, sides)
+    size = low.shape[0]
+    places = own_places(bx, 0, vectors)
+    places[1, -1], places[1, bx] = (beside, 0), (beside, 1)
     for side, slab, base in ((0, low, 0), (1, high, size)):
         for k in range(4):
             depth, at = DEPTHS[k + 1], OFFSETS[k + 1]
@@ -290,25 +304,30 @@
         weight[side, by:] = corner[base + at] * sign - 2.0 * DIFFUSION / HALF_WIDTH
     cells = Cells(bx, coef, edge, lambda j, x: places[j, x])
     mark_interior(cells, bx, 0, vectors)
-    for x in range(bx):
-        cells.known[0, x] = lambda x=x: start[x]
-    for side, slab, after, base, after_base in (
-        (0, low, low_later, 0, 2 * size),
-        (1, high, high_later, size, 2 * size + later),
-    ):
-
-        def wide(ref, at, offset):
-            return jnp.concatenate([ref[at], corner[offset + at]], axis=0)
-
-        def starting(m, side=side, slab=slab, base=base):
-            return wide(slab, DEPTHS[0] - m if side == 0 else m - 1, base) * LIFT
-
+    know_start(cells, start, low, high, corner)
+    for j in range(1, STEPS + 1):
+        for x in early_range(j, bx):
+            cells.get(j, x)
+
+
+def rest_kernel(
+    start, coef, low, high, corner, beside, edge, weight, low_later, high_later, later_corner, given, vectors, to_low, to_high, following, sides, scratch
+):
+    del given
+    bx, by = start.shape[0], low.shape[1]
+    later = low_later.shape[0]
+    places = own_places(bx, 0, vectors) | own_places(bx, STEPS, following) | halo_places(bx, 0, scratch, sides)
+    cells = Cells(bx, coef, edge, lambda j, x: places[j, x])
+    know_start(cells, start, low, high, corner)
+    for j in range(1, STEPS + 1):
+        for x in early_range(j, bx):
+            cells.known[j, x] = lambda j=j, x=x: vectors[j - 1, x]
+    cells.known[1, -1], cells.known[1, bx] = (lambda: beside[0]), (lambda: beside[1])
+    for side, slab, base in ((0, low_later, 0), (1, high_later, later)):
         near, far = halo_layer(bx, 1, side == 0), halo_layer(bx, 2, side == 0)
-        cells.known[0, near] = lambda f=starting: f(1)
-        cells.known[0, far] = lambda f=starting: f(2)
-        cells.known[1, far] = lambda a=after, o=after_base: wide(a, 0, o)
-        cells.computed[2, far] = lambda a=after, o=after_base, side=side, near=near: (
-            wide(a, 1, o) + weight[side] * cells.get(1, near)
+        cells.known[1, far] = lambda slab=slab, base=base: wide_layer(slab, later_corner, 0, base)
+        cells.computed[2, far] = lambda slab=slab, base=base, side=side, near=near: (
+            wide_layer(slab, later_corner, 1, base) + weight[side] * cells.get(1, near)
         )
     cells.finish(0)
     for out, below, one, two in ((to_low, True, 0, 1), (to_high, False, bx - 1, bx - 2)):
@@ -356,7 +375,7 @@
     gram[...] = jnp.broadcast_to(line, gram.shape)
 
 
-def last_kernel(cell_count, gram, start, one, two, out, factor, coef, result, sem):
+def last_kernel(cell_count, gram, start, one, two, out, factor, result, sem):
     _, bx, by, nz = result.shape
     total = gram[0:8]
     for row in range(8, gram.shape[0], 8):
@@ -364,46 +383,30 @@
     for distance in (4, 2, 1):
         total = total + pltpu.roll(total, distance, 0)
     total = total * (1.0 / cell_count)
-    entry = {pair: jnp.broadcast_to(total[:, k : k + 1], (8, 128)) for pair, k in PLACE.items()}
-    divisor = jnp.sqrt(entry[0, 0] * (1.0 / (LIFT * LIFT)) + EPSILON)
-    scale = 1.0 / (divisor * LIFT)
+    cell = reader(start, one, two)
+    entry, inverse, copies = {}, [], []
     for j in range(BASIS):
-        length = jnp.sqrt(entry[j, j])
-        inverse = 1.0 / length
-        row = {k: entry[j, k] * inverse for k in range(j + 1, BASIS)}
-        for i in range(j + 1, BASIS):
-            for k in range(i, BASIS):
-                entry[i, k] = entry[i, k] - row[i] * row[k]
-        entry[j, j] = length
-        coef[PLACE[j, j]] = inverse
-        for k in range(j + 1, BASIS):
-            entry[j, k] = row[k]
-            coef[PLACE[j, k]] = row[k]
-    cell = reader(start, one, two)
-    tiles = by // 8
-
-    def solve(x, carry):
-        for y in range(0, tiles, 2):
-            windows = [
-                (x, slice(8 * t, 8 * t + 8), slice(z, z + 128))
-                for t in range(y, min(y + 2, tiles))
-                for z in range(0, nz, 128)
-            ]
-            columns = []
-            for j in range(BASIS):
-                values = [cell(j, *window) for window in windows]
-                for i in range(j):
-                    factor_ = coef[PLACE[i, j]]
-                    values = [v - factor_ * c for v, c in zip(values, columns[i])]
-                factor_ = coef[PLACE[j, j]]
-                values = [v * factor_ for v in values]
-                for window, value in zip(windows, values):
-                    result[(j,) + window] = value
-                columns.append(values)
-        pltpu.make_async_copy(result.at[:, x], out.at[:, x], sem.at[x]).start()
-        return carry
-
-    lax.fori_loop(0, bx, solve, 0)
+        for i in range(j + 1):
+            k = PLACE[i, j]
+            value = jnp.broadcast_to(total[:, k : k + 1], (8, 128))
+            if (i, j) == (0, 0):
+                mean_square = value * (1.0 / (LIFT * LIFT))
+            for above in range(i):
+                value = value - entry[above, i] * entry[above, j]
+            if i == j:
+                inverse.append(lax.rsqrt(value))
+            entry[i, j] = value * inverse[i]
+        for x in range(bx):
+            for y in range(0, by, 8):
+                for z in range(0, nz, 128):
+                    window = (x, slice(y, y + 8), slice(z, z + 128))
+                    value = cell(j, *window)
+                    for i in range(j):
+                        value = value - entry[i, j] * result[(i,) + window]
+                    result[(j,) + window] = value * inverse[j]
+        copies.append(pltpu.make_async_copy(result.at[j], out.at[j], sem.at[j]))
+        copies[j].start()
+    scale = lax.rsqrt(mean_square + EPSILON) * (1.0 / LIFT)
     sublane = lax.broadcasted_iota(jnp.int32, (8, 128), 0)
     lane = lax.broadcasted_iota(jnp.int32, (8, 128), 1)
     tops = []
@@ -414,8 +417,8 @@
                 packed = jnp.where((sublane == i - base) & (lane == j), value, packed)
         tops.append(packed * scale)
     factor[...] = jnp.concatenate(tops, axis=0)[:BASIS, :BASIS]
-    for x in range(bx):
-        pltpu.make_async_copy(result.at[:, x], out.at[:, x], sem.at[x]).wait()
+    for copy in copies:
+        copy.wait()
 
 
 def shape(*dims):
@@ -466,29 +469,37 @@
     start, coef, one = call(
         prepare_kernel, [shape(bx, wide, nz), shape(4, bx, wide, nz), vectors], fields, rows, name="prepare"
     )
-    corner = swap_y(jnp.concatenate([low, high, low_later, high_later]))
-    one, to_low, to_high, two, sides, edge, weight = call(
+    corner = swap_y(jnp.concatenate([low, high]))
+    one, beside, edge, weight = call(
         first_kernel,
-        [
-            vectors,
-            shape(4, by + 2 * EDGE, nz),
-            shape(4, by + 2 * EDGE, nz),
-            vectors,
-            shape(2, wide, nz),
-            shape(4, 2, wide, nz),
-            shape(2, wide, nz),
-        ],
+        [vectors, shape(2, wide, nz), shape(4, 2, wide, nz), shape(2, wide, nz)],
         start,
         coef,
         low,
         high,
-        low_later,
-        high_later,
         corner,
         one,
         name="first",
+        aliases={5: 0},
+    )
+    one, to_low, to_high, two, sides = call(
+        rest_kernel,
+        [vectors, shape(4, by + 2 * EDGE, nz), shape(4, by + 2 * EDGE, nz), vectors, shape(2, wide, nz)],
+        start,
+        coef,
+        low,
+        high,
+        corner,
+        beside,
+        edge,
+        weight,
+        low_later,
+        high_later,
+        swap_y(jnp.concatenate([low_later, high_later])),
+        one,
+        name="rest",
         scratch=[pltpu.VMEM((2 * len(COMPUTED), wide, nz), jnp.float32)],
-        aliases={7: 0},
+        aliases={11: 0},
     )
     low, high = swap_x(to_low, to_high)
     two, early_gram = call(
@@ -529,9 +540,8 @@
         name="last",
         out_specs=[pl.BlockSpec(memory_space=pl.ANY), VMEM],
         scratch=[
-            pltpu.VMEM((GRAM_ROWS, 8, 128), jnp.float32),
             pltpu.VMEM((BASIS, bx, by, nz), jnp.float32),
-            pltpu.SemaphoreType.DMA((bx,)),
+            pltpu.SemaphoreType.DMA((BASIS,)),
         ],
     )
 

time: 50.7 us -> 49.9 us (0.984)
  waiting for transfers between devices: 10.2 us -> 9.54 us
    ppermute x3 -> x4, waiting for transfers between devices: 0.9 us -> 0.01 us  [swap_rows(): lax.ppermute(jnp.concatenate([low, high], axis=1), 'gy', ring('gy', 1))]
    pallas_call x7 -> x8, Pallas kernels: 9.19 us -> 8.92 us  [call(): pl.pallas_call(kernel, out_shape=outs, in_specs=in_specs or [VMEM] * len(...]
  transfers between devices with their start and end apart: 9 -> 10, of which waited for: 7 -> 6; matrix products, arithmetic and copies ran while one was open for 0% -> 0% of each run, Pallas kernels for 3% -> 5%
where the time goes in v4:
time: 49.9 us; the launch traced here: 49.7 us
  starting transfers between devices  18.8 us (38%)
  blocking collectives  11.5 us (23%)
  waiting for transfers between devices  9.54 us (19%)
  Pallas kernels  8.92 us (18%)
  between operations  0.77 us (2%)
    ppermute x3, starting transfers between devices, swap_x(): lax.ppermute(to_low, 'gx', ring('gx', -1))  13.8 us
    all_to_all x1, blocking collectives, per_device(): gram = lax.all_to_all(gram, AXES, 0, 0, tiled=True)  11.5 us
    pallas_call x8, Pallas kernels, call(): pl.pallas_call(kernel, out_shape=outs, in_specs=in_specs or [VMEM] * len(...  8.92 us
    ppermute x3, waiting for transfers between devices, swap_x(): lax.ppermute(to_high, 'gx', ring('gx', 1))  6.05 us
    ppermute x3, starting transfers between devices, swap_x(): lax.ppermute(to_high, 'gx', ring('gx', 1))  4.15 us
    ppermute x3, waiting for transfers between devices, swap_x(): lax.ppermute(to_low, 'gx', ring('gx', -1))  3.48 us
  transfers between devices with their start and end apart: 10, of which 6 were waited for; matrix products, arithmetic and copies ran while one was open for 0% of the time, Pallas kernels for 5%

profile of v4, /device:TPU:0, one launch (start us, length us, event | category | flops | bytes accessed | tf_op | source)
XLA Modules:
  0.0 49.7 jit_solution(10399433085378904339)
XLA Ops:
  0.6 1.3 %pack.1 = (f32[5,8,32,256]{3,2,1,0:T(8,128)S(1)}, f32[7,32,256]{2,1,0:T(8,128)S(1)}, f32[7,32,256]{2,1,0:T(8,128)S(1)}, f32[22,8,256]{2,1,0:T(8,128)S(1)}) custom-call(f32[8,32,256]{2,1,0:T(8,128)} %f.1, f32[8,32,256]{2,1,0:T(8,128)} %r.1, f32[3,8,32,256]{3,2,1,0:T(8,128)} %vel.1), custom_call_target="tpu_custom_call" | custom-call | bytes 60000 | tf_op jit(solution)/shard_map/pack/pallas_call | solution.py:429
  2.0 0.5 %collective-permute-start.4 = (f32[22,8,256]{2,1,0:T(8,128)S(1)}, f32[22,8,256]{2,1,0:T(8,128)S(1)}, u32[]{:S(2)}, u32[]{:S(2)}) collective-permute-start(f32[22,8,256]{2,1,0:T(8,128)S(1)} %get-tuple-element.33), channel_id=1, source_target_pairs={{0,1},{1,0},{2,3},{3,2},{4,5},{5,4},{6,7},{7,6},{8,9},{9,8},{10,11... | collective-permute-start | bytes 540680 | tf_op jit(solution)/shard_map/ppermute | solution.py:58
  2.5 2.6 %collective-permute-start.1 = (f32[7,32,256]{2,1,0:T(8,128)S(1)}, f32[7,32,256]{2,1,0:T(8,128)S(1)}, u32[]{:S(2)}, u32[]{:S(2)}) collective-permute-start(f32[7,32,256]{2,1,0:T(8,128)S(1)} %get-tuple-element.27), channel_id=1, source_target_pairs={{0,2},{2,4},{4,6},{6,8},{8,10},{10,12},{12,14},{14,16},{16,18},{18... | collective-permute-start | bytes 688136 | tf_op jit(solution)/shard_map/ppermute | solution.py:48
  5.0 4.1 %collective-permute-start.2 = (f32[7,32,256]{2,1,0:T(8,128)S(1)}, f32[7,32,256]{2,1,0:T(8,128)S(1)}, u32[]{:S(2)}, u32[]{:S(2)}) collective-permute-start(f32[7,32,256]{2,1,0:T(8,128)S(1)} %get-tuple-element.28), channel_id=1, source_target_pairs={{0,30},{2,0},{4,2},{6,4},{8,6},{10,8},{12,10},{14,12},{16,14},{18,... | collective-permute-start | bytes 688136 | tf_op jit(solution)/shard_map/ppermute | solution.py:48
  9.2 0.1 collective-permute-start
  9.4 0.0 collective-permute-done.4.rows
  9.4 0.3 inner.1
  9.6 0.1 collective-permute-start.5
  9.7 5.6 %collective-permute-start.6 = (f32[2,32,256]{2,1,0:T(8,128)S(1)}, f32[2,32,256]{2,1,0:T(8,128)S(1)}, u32[]{:S(2)}, u32[]{:S(2)}) collective-permute-start(f32[2,32,256]{2,1,0:T(8,128)S(1)} %get-tuple-element.35), channel_id=1, source_target_pairs={{0,30},{2,0},{4,2},{6,4},{8,6},{10,8},{12,10},{14,12},{16,14},{18,... | collective-permute-start | bytes 196616 | tf_op jit(solution)/shard_map/ppermute | solution.py:48
  15.3 2.0 %collective-permute-done.1.low = f32[7,32,256]{2,1,0:T(8,128)S(1)} collective-permute-done((f32[7,32,256]{2,1,0:T(8,128)S(1)}, f32[7,32,256]{2,1,0:T(8,128)S(1)}, u32[]{:S(2)}, u32[]{:S(2)}) %collective-permute-start.1) | collective-permute-done | bytes 229408 | tf_op jit(solution)/shard_map/ppermute | solution.py:48
  17.3 0.5 %collective-permute-done.2.high = f32[7,32,256]{2,1,0:T(8,128)S(1)} collective-permute-done((f32[7,32,256]{2,1,0:T(8,128)S(1)}, f32[7,32,256]{2,1,0:T(8,128)S(1)}, u32[]{:S(2)}, u32[]{:S(2)}) %collective-permute-start.2) | collective-permute-done | bytes 229408 | tf_op jit(solution)/shard_map/ppermute | solution.py:48
  17.9 0.1 collective-permute-start.3
  18.0 0.3 collective-permute-done.5.low_later
  18.2 1.9 %collective-permute-done.6.high_later = f32[2,32,256]{2,1,0:T(8,128)S(1)} collective-permute-done((f32[2,32,256]{2,1,0:T(8,128)S(1)}, f32[2,32,256]{2,1,0:T(8,128)S(1)}, u32[]{:S(2)}, u32[]{:S(2)}) %collective-permute-start.6) | collective-permute-done | bytes 65568 | tf_op jit(solution)/shard_map/ppermute | solution.py:48
  20.2 0.1 collective-permute-start.7
  20.3 0.0 collective-permute-done.rows
  20.3 0.7 %prepare.1 = (f32[8,48,256]{2,1,0:T(8,128)S(1)}, f32[4,8,48,256]{3,2,1,0:T(8,128)S(1)}, f32[4,8,48,256]{3,2,1,0:T(8,128)S(1)}) custom-call(f32[5,8,32,256]{3,2,1,0:T(8,128)S(1)} %get-tuple-element.24.fields, f32[40,16,256]{2,1,0:T(8,128)S(1)} %collective-permute-done.rows), custom_call_target="tpu_custom_call" | custom-call | bytes 60000 | tf_op jit(solution)/shard_map/prepare/pallas_call | solution.py:429
  21.0 0.0 collective-permute-done.3.corner
  21.0 0.8 %first.1 = (f32[4,8,48,256]{3,2,1,0:T(8,128)S(1)}, f32[2,48,256]{2,1,0:T(8,128)S(1)}, f32[4,2,48,256]{3,2,1,0:T(8,128)S(1)}, f32[2,48,256]{2,1,0:T(8,128)S(1)}) custom-call(f32[8,48,256]{2,1,0:T(8,128)S(1)} %get-tuple-element.25.start.refs_0_.refs_1_, f32[4,8,48,256]{3,2,1,0:T(8,128)S(1)} %get-tuple-element.26.coef.refs_2_, ...), custom_call_target="tpu_custom_call", output_to_operand_aliasing={{0}: (5, {})} | custom-call | bytes 60000 | tf_op jit(solution)/shard_map/first/pallas_call | solution.py:429
  21.8 0.0 collective-permute-done.7.later_corner
  21.8 0.7 %rest.1 = (f32[4,8,48,256]{3,2,1,0:T(8,128)S(1)}, f32[4,40,256]{2,1,0:T(8,128)S(1)}, f32[4,40,256]{2,1,0:T(8,128)S(1)}, f32[4,8,48,256]{3,2,1,0:T(8,128)S(1)}, f32[2,48,256]{2,1,0:T(8,128)S(1)}) custom-call(f32[8,48,256]{2,1,0:T(8,128)S(1)} %get-tuple-element.25.start.refs_0_.refs_1_, ...), custom_call_target="tpu_custom_call", output_to_operand_aliasing={{0}: (11, {})} | custom-call | bytes 60000 | tf_op jit(solution)/shard_map/rest/pallas_call | solution.py:429
  22.5 1.5 %collective-permute-start.8 = (f32[4,40,256]{2,1,0:T(8,128)S(1)}, f32[4,40,256]{2,1,0:T(8,128)S(1)}, u32[]{:S(2)}, u32[]{:S(2)}) collective-permute-start(f32[4,40,256]{2,1,0:T(8,128)S(1)} %get-tuple-element.41), channel_id=1, source_target_pairs={{0,2},{2,4},{4,6},{6,8},{8,10},{10,12},{12,14},{14,16},{16,18},{18... | collective-permute-start | bytes 491528 | tf_op jit(solution)/shard_map/ppermute | solution.py:48
  24.1 4.1 %collective-permute-start.9 = (f32[4,40,256]{2,1,0:T(8,128)S(1)}, f32[4,40,256]{2,1,0:T(8,128)S(1)}, u32[]{:S(2)}, u32[]{:S(2)}) collective-permute-start(f32[4,40,256]{2,1,0:T(8,128)S(1)} %get-tuple-element.42), channel_id=1, source_target_pairs={{0,30},{2,0},{4,2},{6,4},{8,6},{10,8},{12,10},{14,12},{16,14},{18,... | collective-permute-start | bytes 491528 | tf_op jit(solution)/shard_map/ppermute | solution.py:48
  28.2 0.9 %second_interior.1 = (f32[4,8,48,256]{3,2,1,0:T(8,128)S(1)}, f32[16,128]{1,0:T(8,128)S(1)}) custom-call(f32[8,48,256]{2,1,0:T(8,128)S(1)} %get-tuple-element.25.start.refs_0_.refs_1_, f32[4,8,48,256]{3,2,1,0:T(8,128)S(1)} %get-tuple-element.37.refs_1_.one.refs_2_, ...), custom_call_target="tpu_custom_call", output_to_operand_aliasing={{0}: (3, {})} | custom-call | bytes 60000 | tf_op jit(solution)/shard_map/second_interior/pallas_call | solution.py:429
  29.1 3.8 %collective-permute-done.8.low = f32[4,40,256]{2,1,0:T(8,128)S(1)} collective-permute-done((f32[4,40,256]{2,1,0:T(8,128)S(1)}, f32[4,40,256]{2,1,0:T(8,128)S(1)}, u32[]{:S(2)}, u32[]{:S(2)}) %collective-permute-start.8) | collective-permute-done | bytes 163872 | tf_op jit(solution)/shard_map/ppermute | solution.py:48
  32.9 1.0 %collective-permute-done.9.high = f32[4,40,256]{2,1,0:T(8,128)S(1)} collective-permute-done((f32[4,40,256]{2,1,0:T(8,128)S(1)}, f32[4,40,256]{2,1,0:T(8,128)S(1)}, u32[]{:S(2)}, u32[]{:S(2)}) %collective-permute-start.9) | collective-permute-done | bytes 163872 | tf_op jit(solution)/shard_map/ppermute | solution.py:48
  33.9 2.1 %second.1 = (f32[4,8,48,256]{3,2,1,0:T(8,128)S(1)}, f32[32,128]{1,0:T(8,128)S(1)}) custom-call(f32[8,48,256]{2,1,0:T(8,128)S(1)} %get-tuple-element.25.start.refs_0_.refs_1_, f32[4,8,48,256]{3,2,1,0:T(8,128)S(1)} %get-tuple-element.37.refs_1_.one.refs_2_, f32[4,8,48,256]{3,2,1,0:T(8,128)S(1)} %get-tuple-element.39.given, ...), custom_call_target="tpu_custom_call", output_to_operand_aliasing={{0}: (2, {})} | custom-call | bytes 60000 | tf_op jit(solution)/shard_map/second/pallas_call | solution.py:429
  36.0 11.5 %all_to_all.11 = f32[32,1,128]{2,1,0:T(1,128)S(1)} all-to-all(f32[32,1,128]{2,1,0:T(1,128)S(1)} %bitcast.7), channel_id=1, replica_groups=mesh['gx'=16,'gy'=2] {'gx','gy'}, dimensions={0} | all-to-all | bytes 32768 | tf_op jit(solution)/shard_map/all_to_all | solution.py:532
  47.5 2.2 %last.1 = (f32[9,8,32,256]{3,2,1,0:T(8,128)}, f32[9,9]{1,0:T(8,128)}) custom-call(f32[32,128]{1,0:T(8,128)S(1)} %bitcast.6, f32[8,48,256]{2,1,0:T(8,128)S(1)} %get-tuple-element.25.start.refs_0_.refs_1_, f32[4,8,48,256]{3,2,1,0:T(8,128)S(1)} %get-tuple-element.37.refs_1_.one.refs_2_, f32[4,8,48,256]{3,2,1,0:T(8,128)S(1)} %get-tuple-element.45.refs_3_), custom_call_target="tpu_custom_call" | custom-call | bytes 60000 | tf_op jit(solution)/shard_map/last/pallas_call | solution.py:429
  (10 shorter events, 0.2 us)
Async XLA Ops:
  2.0 7.4 %collective-permute-start.4 = (f32[22,8,256]{2,1,0:T(8,128)S(1)}, f32[22,8,256]{2,1,0:T(8,128)S(1)}, u32[]{:S(2)}, u32[]{:S(2)}) collective-permute-start(f32[22,8,256]{2,1,0:T(8,128)S(1)} %get-tuple-element.33), channel_id=1, source_target_pairs={{0,1},{1,0},{2,3},{3,2},{4,5},{5,4},{6,7},{7,6},{8,9},{9,8},{10,11... | collective-permute-start | bytes 540680 | tf_op jit(solution)/shard_map/ppermute | solution.py:58
  2.5 14.8 %collective-permute-start.1 = (f32[7,32,256]{2,1,0:T(8,128)S(1)}, f32[7,32,256]{2,1,0:T(8,128)S(1)}, u32[]{:S(2)}, u32[]{:S(2)}) collective-permute-start(f32[7,32,256]{2,1,0:T(8,128)S(1)} %get-tuple-element.27), channel_id=1, source_target_pairs={{0,2},{2,4},{4,6},{6,8},{8,10},{10,12},{12,14},{14,16},{16,18},{18... | collective-permute-start | bytes 688136 | tf_op jit(solution)/shard_map/ppermute | solution.py:48
  5.0 12.8 %collective-permute-start.2 = (f32[7,32,256]{2,1,0:T(8,128)S(1)}, f32[7,32,256]{2,1,0:T(8,128)S(1)}, u32[]{:S(2)}, u32[]{:S(2)}) collective-permute-start(f32[7,32,256]{2,1,0:T(8,128)S(1)} %get-tuple-element.28), channel_id=1, source_target_pairs={{0,30},{2,0},{4,2},{6,4},{8,6},{10,8},{12,10},{14,12},{16,14},{18,... | collective-permute-start | bytes 688136 | tf_op jit(solution)/shard_map/ppermute | solution.py:48
  9.2 11.1 %collective-permute-start = (f32[40,16,256]{2,1,0:T(8,128)S(1)}, f32[40,16,256]{2,1,0:T(8,128)S(1)}, u32[]{:S(2)}, u32[]{:S(2)}) collective-permute-start(f32[40,16,256]{2,1,0:T(8,128)S(1)} %pad_maximum_fusion), channel_id=1, source_target_pairs={{0,1},{1,0},{2,3},{3,2},{4,5},{5,4},{6,7},{7,6},{8,9},{9,8},{10,11... | collective-permute-start | bytes 1966088 | tf_op jit(solution)/shard_map/ppermute | solution.py:58
  9.6 8.6 %collective-permute-start.5 = (f32[2,32,256]{2,1,0:T(8,128)S(1)}, f32[2,32,256]{2,1,0:T(8,128)S(1)}, u32[]{:S(2)}, u32[]{:S(2)}) collective-permute-start(f32[2,32,256]{2,1,0:T(8,128)S(1)} %get-tuple-element.34), channel_id=1, source_target_pairs={{0,2},{2,4},{4,6},{6,8},{8,10},{10,12},{12,14},{14,16},{16,18},{18... | collective-permute-start | bytes 196616 | tf_op jit(solution)/shard_map/ppermute | solution.py:48
  9.7 10.5 %collective-permute-start.6 = (f32[2,32,256]{2,1,0:T(8,128)S(1)}, f32[2,32,256]{2,1,0:T(8,128)S(1)}, u32[]{:S(2)}, u32[]{:S(2)}) collective-permute-start(f32[2,32,256]{2,1,0:T(8,128)S(1)} %get-tuple-element.35), channel_id=1, source_target_pairs={{0,30},{2,0},{4,2},{6,4},{8,6},{10,8},{12,10},{14,12},{16,14},{18,... | collective-permute-start | bytes 196616 | tf_op jit(solution)/shard_map/ppermute | solution.py:48
  17.9 3.1 %collective-permute-start.3 = (f32[14,16,256]{2,1,0:T(8,128)S(1)}, f32[14,16,256]{2,1,0:T(8,128)S(1)}, u32[]{:S(2)}, u32[]{:S(2)}) collective-permute-start(f32[14,16,256]{2,1,0:T(8,128)S(1)} %pad_maximum_fusion.1), channel_id=1, source_target_pairs={{0,1},{1,0},{2,3},{3,2},{4,5},{5,4},{6,7},{7,6},{8,9},{9,8},{10,11... | collective-permute-start | bytes 688136 | tf_op jit(solution)/shard_map/ppermute | solution.py:58
  20.2 1.6 %collective-permute-start.7 = (f32[4,16,256]{2,1,0:T(8,128)S(1)}, f32[4,16,256]{2,1,0:T(8,128)S(1)}, u32[]{:S(2)}, u32[]{:S(2)}) collective-permute-start(f32[4,16,256]{2,1,0:T(8,128)S(1)} %pad_maximum_fusion.2), channel_id=1, source_target_pairs={{0,1},{1,0},{2,3},{3,2},{4,5},{5,4},{6,7},{7,6},{8,9},{9,8},{10,11... | collective-permute-start | bytes 196616 | tf_op jit(solution)/shard_map/ppermute | solution.py:58
  22.5 10.3 %collective-permute-start.8 = (f32[4,40,256]{2,1,0:T(8,128)S(1)}, f32[4,40,256]{2,1,0:T(8,128)S(1)}, u32[]{:S(2)}, u32[]{:S(2)}) collective-permute-start(f32[4,40,256]{2,1,0:T(8,128)S(1)} %get-tuple-element.41), channel_id=1, source_target_pairs={{0,2},{2,4},{4,6},{6,8},{8,10},{10,12},{12,14},{14,16},{16,18},{18... | collective-permute-start | bytes 491528 | tf_op jit(solution)/shard_map/ppermute | solution.py:48
  24.1 9.8 %collective-permute-start.9 = (f32[4,40,256]{2,1,0:T(8,128)S(1)}, f32[4,40,256]{2,1,0:T(8,128)S(1)}, u32[]{:S(2)}, u32[]{:S(2)}) collective-permute-start(f32[4,40,256]{2,1,0:T(8,128)S(1)} %get-tuple-element.42), channel_id=1, source_target_pairs={{0,30},{2,0},{4,2},{6,4},{8,6},{10,8},{12,10},{14,12},{16,14},{18,... | collective-permute-start | bytes 491528 | tf_op jit(solution)/shard_map/ppermute | solution.py:48

commit v5 on v4

--- a/solution.py
+++ b/solution.py
@@ -78,21 +78,26 @@
     return value * SCALES[k] + SHIFTS[k]
 
 
-def products(pairs, bx, by, nz, cell):
+def products(pairs, first, last, by, nz, cell, totals=None):
     needed = sorted({i for pair in pairs for i in pair})
     tiles = by // 8
 
     def add(at, totals):
-        x, y = at // tiles, pl.multiple_of(at % tiles * 8, 8)
+        x, y = first + at // tiles, pl.multiple_of(at % tiles * 8, 8)
         for z in range(0, nz, 128):
             cells = {i: cell(i, x, pl.ds(y, 8), pl.ds(z, 128)) for i in needed}
             totals = tuple(t + cells[i] * cells[j] for t, (i, j) in zip(totals, pairs))
         return totals
 
-    totals = lax.fori_loop(0, bx * tiles, add, tuple(jnp.zeros((8, 128), jnp.float32) for _ in pairs), unroll=2)
+    if totals is None:
+        totals = tuple(jnp.zeros((8, 128), jnp.float32) for _ in pairs)
+    return lax.fori_loop(0, (last - first) * tiles, add, totals, unroll=2)
+
+
+def summed_rows(totals):
     sublane = lax.broadcasted_iota(jnp.int32, (8, 128), 0)
     rows = []
-    for base in range(0, len(pairs), 8):
+    for base in range(0, len(totals), 8):
         packed = jnp.zeros((8, 128), jnp.float32)
         for k, total in enumerate(totals[base : base + 8]):
             for distance in (4, 2, 1):
@@ -124,7 +129,7 @@
         cells.known[STEPS, x] = lambda x=x: one[STEPS - 1, x]
         cells.known[STEPS - 1, x] = lambda x=x: one[STEPS - 2, x]
     cells.interior(STEPS)
-    for k, row in enumerate(products(GROUPS[0], bx, by, nz, reader(start, one))):
+    for k, row in enumerate(summed_rows(products(GROUPS[0], 0, bx, by, nz, reader(start, one)))):
         gram[8 * k : 8 * k + 8] = row
 
 
@@ -172,7 +177,7 @@
         def __getitem__(self, at):
             return scaled(at[0], layer(at[0] + 1, at[1]))
 
-    cells = Cells(bx, Coefficients(), None, lambda j, x: (scratch, {1: 0, 2: 1, bx - 3: 2, bx - 2: 3}[x]))
+    cells = Cells(bx, Coefficients(), None, lambda j, x: (scratch, ({1: 0, 2: 1, bx - 3: 2, bx - 2: 3}[x],)))
     for x in (0, 1, 2, 3, bx - 4, bx - 3, bx - 2, bx - 1):
         if 3 <= x < bx - 3:
             cells.known[0, x] = lambda x=x: jnp.concatenate([fields[0, x], jnp.zeros_like(rows[0])], axis=0) * LIFT
@@ -196,12 +201,15 @@
 
     def get(self, j, x):
         if (j, x) not in self.known:
+            ref, at = self.place(j, x)
+            rows = ref.shape[-2] - (2 * MARGIN if j == BASIS - 1 else 0)
             if (j, x) in self.computed:
                 new = self.computed[j, x]()
             else:
-                new = doubled(self.get(j - 1, x), self.get(j - 1, x + 1), self.get(j - 1, x - 1), self.coefficients(x))
-                new = new * 0.5 if j == 1 else new - self.get(j - 2, x)
-            ref, at = self.place(j, x)
+                east, west = self.get(j - 1, x + 1)[:rows], self.get(j - 1, x - 1)[:rows]
+                new = doubled(self.get(j - 1, x), east, west, [c[:rows] for c in self.coefficients(x)])
+                new = new * 0.5 if j == 1 else new - self.get(j - 2, x)[:rows]
+            at = at + (slice(0, rows),)
             ref[at] = new
             self.known[j, x] = lambda: ref[at]
         return self.known[j, x]()
@@ -245,9 +253,9 @@
         for low_side in (True, False):
             at = (base + j, halo_layer(bx, m, low_side))
             if sides is not None and (j, m) == (STEPS - 1, 1):
-                places[at] = (sides, 0 if low_side else 1)
+                places[at] = (sides, (0 if low_side else 1,))
             else:
-                places[at] = (scratch, slot)
+                places[at] = (scratch, (slot,))
                 slot += 1
     return places
 
@@ -291,7 +299,7 @@
     bx, by = start.shape[0], low.shape[1]
     size = low.shape[0]
     places = own_places(bx, 0, vectors)
-    places[1, -1], places[1, bx] = (beside, 0), (beside, 1)
+    places[1, -1], places[1, bx] = (beside, (0,)), (beside, (1,))
     for side, slab, base in ((0, low, 0), (1, high, size)):
         for k in range(4):
             depth, at = DEPTHS[k + 1], OFFSETS[k + 1]
@@ -344,31 +352,56 @@
             out[at, by:] = jnp.where(row < EDGE, above, under)
 
 
-def second_kernel(start, one, given, sides, coef, edge, weight, low, high, early_gram, two, gram, scratch):
-    del given
-    bx, _, nz = start.shape
-    by = low.shape[1] - 2 * EDGE
+def second_cells(one, sides, coef, edge, weight, slab, side, two, scratch):
+    bx = coef.shape[1]
+    by = slab.shape[1] - 2 * EDGE
     places = own_places(bx, STEPS, two) | halo_places(bx, STEPS, scratch)
     cells = Cells(bx, coef, edge, lambda j, x: places[j, x])
     mark_interior(cells, bx, STEPS, two)
     for x in range(bx):
         cells.known[STEPS, x] = lambda x=x: one[STEPS - 1, x]
         cells.known[STEPS - 1, x] = lambda x=x: one[STEPS - 2, x]
-    for side, slab in ((0, low), (1, high)):
-        near, far = halo_layer(bx, 1, side == 0), halo_layer(bx, 2, side == 0)
-
-        def wide(at, slab=slab):
-            return jnp.concatenate([slab[at], slab[at, by:]], axis=0)
-
-        cells.known[STEPS - 1, near] = lambda side=side: sides[side]
-        cells.known[STEPS, near] = lambda f=wide: f(0)
-        cells.known[STEPS, far] = lambda f=wide: f(1)
-        cells.known[STEPS + 1, far] = lambda f=wide: f(2)
-        cells.computed[STEPS + 2, far] = lambda f=wide, side=side, near=near: (
-            f(3) + weight[side] * cells.get(STEPS + 1, near)
-        )
-    cells.finish(STEPS)
-    rows = products(GROUPS[1], bx, by, nz, reader(start, one, two))
+    near, far = halo_layer(bx, 1, side == 0), halo_layer(bx, 2, side == 0)
+
+    def wide(at):
+        return jnp.concatenate([slab[at], slab[at, by:]], axis=0)
+
+    cells.known[STEPS - 1, near] = lambda: sides[side]
+    cells.known[STEPS, near] = lambda: wide(0)
+    cells.known[STEPS, far] = lambda: wide(1)
+    cells.known[STEPS + 1, far] = lambda: wide(2)
+    cells.computed[STEPS + 2, far] = lambda: wide(3) + weight[side] * cells.get(STEPS + 1, near)
+    return cells
+
+
+def low_kernel(start, one, given, sides, coef, edge, weight, low, two, partial, scratch):
+    del given
+    bx, _, nz = start.shape
+    by = low.shape[1] - 2 * EDGE
+    cells = second_cells(one, sides, coef, edge, weight, low, 0, two, scratch)
+    for j in range(1, STEPS + 1):
+        reach = max([m for i, m in COMPUTED if i == j], default=0)
+        for x in range(-reach, bx - j):
+            cells.get(STEPS + j, x)
+    totals = products(GROUPS[1], 0, bx - STEPS, by, nz, reader(start, one, two))
+    for k, total in enumerate(totals):
+        partial[k] = total
+
+
+def high_kernel(start, one, given, sides, coef, edge, weight, high, early_gram, partial, two, gram, scratch):
+    del given
+    bx, _, nz = start.shape
+    by = high.shape[1] - 2 * EDGE
+    cells = second_cells(one, sides, coef, edge, weight, high, 1, two, scratch)
+    for j in range(1, STEPS + 1):
+        for x in range(bx - j):
+            cells.known[STEPS + j, x] = lambda j=j, x=x: two[j - 1, x]
+    for j in range(1, STEPS + 1):
+        reach = max([m for i, m in COMPUTED if i == j], default=0)
+        for x in range(bx - j, bx + reach):
+            cells.get(STEPS + j, x)
+    before = tuple(partial[k] for k in range(len(GROUPS[1])))
+    rows = summed_rows(products(GROUPS[1], bx - STEPS, bx, by, nz, reader(start, one, two), before))
     sums = jnp.concatenate([early_gram[...]] + rows, axis=0)
     on = lax.broadcasted_iota(jnp.int32, sums.shape, 0) == lax.broadcasted_iota(jnp.int32, sums.shape, 1)
     line = jnp.sum(jnp.where(on, jnp.sum(sums, axis=1, keepdims=True), 0.0), axis=0, keepdims=True)
@@ -512,8 +545,24 @@
         name="second_interior",
         aliases={3: 0},
     )
+    halo = [pltpu.VMEM((2 * len(COMPUTED), wide, nz), jnp.float32)]
+    two, partial = call(
+        low_kernel,
+        [vectors, shape(len(GROUPS[1]), 8, 128)],
+        start,
+        one,
+        two,
+        sides,
+        coef,
+        edge,
+        weight,
+        low,
+        name="low",
+        scratch=halo,
+        aliases={2: 0},
+    )
     two, gram = call(
-        second_kernel,
+        high_kernel,
         [vectors, shape(devices, 128)],
         start,
         one,
@@ -522,11 +571,11 @@
         coef,
         edge,
         weight,
-        low,
         high,
         early_gram,
-        name="second",
-        scratch=[pltpu.VMEM((2 * len(COMPUTED), wide, nz), jnp.float32)],
+        partial,
+        name="high",
+        scratch=halo,
         aliases={2: 0},
     )
     gram = lax.all_to_all(gram, AXES, 0, 0, tiled=True)

time: 49.9 us -> 48.8 us (0.978)
  waiting for transfers between devices: 9.54 us -> 8.58 us
    ppermute x3, waiting for transfers between devices: 3.48 us -> 2.53 us  [swap_x(): lax.ppermute(to_low, 'gx', ring('gx', -1))]
    pallas_call x8 -> x9, Pallas kernels: 8.92 us -> 8.76 us  [call(): pl.pallas_call(kernel, out_shape=outs, in_specs=in_specs or [VMEM] * len(...]
  transfers between devices with their start and end apart: 10 -> 10, of which waited for: 6 -> 6; matrix products, arithmetic and copies ran while one was open for 0% -> 0% of each run, Pallas kernels for 5% -> 7%
where the time goes in v5:
time: 48.8 us; the launch traced here: 48.6 us
  starting transfers between devices  18.8 us (39%)
  blocking collectives  11.5 us (24%)
  Pallas kernels  8.76 us (18%)
  waiting for transfers between devices  8.58 us (18%)
  between operations  0.78 us (2%)
    ppermute x3, starting transfers between devices, swap_x(): lax.ppermute(to_low, 'gx', ring('gx', -1))  13.8 us
    all_to_all x1, blocking collectives, per_device(): gram = lax.all_to_all(gram, AXES, 0, 0, tiled=True)  11.5 us
    pallas_call x9, Pallas kernels, call(): pl.pallas_call(kernel, out_shape=outs, in_specs=in_specs or [VMEM] * len(...  8.76 us
    ppermute x3, waiting for transfers between devices, swap_x(): lax.ppermute(to_high, 'gx', ring('gx', 1))  6.04 us
    ppermute x3, starting transfers between devices, swap_x(): lax.ppermute(to_high, 'gx', ring('gx', 1))  4.15 us
    ppermute x3, waiting for transfers between devices, swap_x(): lax.ppermute(to_low, 'gx', ring('gx', -1))  2.53 us
  transfers between devices with their start and end apart: 10, of which 6 were waited for; matrix products, arithmetic and copies ran while one was open for 0% of the time, Pallas kernels for 7%

profile of v5, /device:TPU:0, one launch (start us, length us, event | category | flops | bytes accessed | tf_op | source)
XLA Modules:
  0.0 48.6 jit_solution(14511278698318836576)
XLA Ops:
  0.6 1.3 %pack.1 = (f32[5,8,32,256]{3,2,1,0:T(8,128)S(1)}, f32[7,32,256]{2,1,0:T(8,128)S(1)}, f32[7,32,256]{2,1,0:T(8,128)S(1)}, f32[22,8,256]{2,1,0:T(8,128)S(1)}) custom-call(f32[8,32,256]{2,1,0:T(8,128)} %f.1, f32[8,32,256]{2,1,0:T(8,128)} %r.1, f32[3,8,32,256]{3,2,1,0:T(8,128)} %vel.1), custom_call_target="tpu_custom_call" | custom-call | bytes 60000 | tf_op jit(solution)/shard_map/pack/pallas_call | solution.py:462
  2.0 0.5 %collective-permute-start.4 = (f32[22,8,256]{2,1,0:T(8,128)S(1)}, f32[22,8,256]{2,1,0:T(8,128)S(1)}, u32[]{:S(2)}, u32[]{:S(2)}) collective-permute-start(f32[22,8,256]{2,1,0:T(8,128)S(1)} %get-tuple-element.35), channel_id=1, source_target_pairs={{0,1},{1,0},{2,3},{3,2},{4,5},{5,4},{6,7},{7,6},{8,9},{9,8},{10,11... | collective-permute-start | bytes 540680 | tf_op jit(solution)/shard_map/ppermute | solution.py:58
  2.5 2.6 %collective-permute-start.1 = (f32[7,32,256]{2,1,0:T(8,128)S(1)}, f32[7,32,256]{2,1,0:T(8,128)S(1)}, u32[]{:S(2)}, u32[]{:S(2)}) collective-permute-start(f32[7,32,256]{2,1,0:T(8,128)S(1)} %get-tuple-element.29), channel_id=1, source_target_pairs={{0,2},{2,4},{4,6},{6,8},{8,10},{10,12},{12,14},{14,16},{16,18},{18... | collective-permute-start | bytes 688136 | tf_op jit(solution)/shard_map/ppermute | solution.py:48
  5.0 4.1 %collective-permute-start.2 = (f32[7,32,256]{2,1,0:T(8,128)S(1)}, f32[7,32,256]{2,1,0:T(8,128)S(1)}, u32[]{:S(2)}, u32[]{:S(2)}) collective-permute-start(f32[7,32,256]{2,1,0:T(8,128)S(1)} %get-tuple-element.30), channel_id=1, source_target_pairs={{0,30},{2,0},{4,2},{6,4},{8,6},{10,8},{12,10},{14,12},{16,14},{18,... | collective-permute-start | bytes 688136 | tf_op jit(solution)/shard_map/ppermute | solution.py:48
  9.2 0.1 collective-permute-start
  9.4 0.0 collective-permute-done.4.rows
  9.4 0.3 inner.1
  9.6 0.1 collective-permute-start.5
  9.7 5.6 %collective-permute-start.6 = (f32[2,32,256]{2,1,0:T(8,128)S(1)}, f32[2,32,256]{2,1,0:T(8,128)S(1)}, u32[]{:S(2)}, u32[]{:S(2)}) collective-permute-start(f32[2,32,256]{2,1,0:T(8,128)S(1)} %get-tuple-element.37), channel_id=1, source_target_pairs={{0,30},{2,0},{4,2},{6,4},{8,6},{10,8},{12,10},{14,12},{16,14},{18,... | collective-permute-start | bytes 196616 | tf_op jit(solution)/shard_map/ppermute | solution.py:48
  15.3 2.0 %collective-permute-done.1.low = f32[7,32,256]{2,1,0:T(8,128)S(1)} collective-permute-done((f32[7,32,256]{2,1,0:T(8,128)S(1)}, f32[7,32,256]{2,1,0:T(8,128)S(1)}, u32[]{:S(2)}, u32[]{:S(2)}) %collective-permute-start.1) | collective-permute-done | bytes 229408 | tf_op jit(solution)/shard_map/ppermute | solution.py:48
  17.3 0.5 %collective-permute-done.2.high = f32[7,32,256]{2,1,0:T(8,128)S(1)} collective-permute-done((f32[7,32,256]{2,1,0:T(8,128)S(1)}, f32[7,32,256]{2,1,0:T(8,128)S(1)}, u32[]{:S(2)}, u32[]{:S(2)}) %collective-permute-start.2) | collective-permute-done | bytes 229408 | tf_op jit(solution)/shard_map/ppermute | solution.py:48
  17.9 0.1 collective-permute-start.3
  18.0 0.3 collective-permute-done.5.low_later
  18.2 1.9 %collective-permute-done.6.high_later = f32[2,32,256]{2,1,0:T(8,128)S(1)} collective-permute-done((f32[2,32,256]{2,1,0:T(8,128)S(1)}, f32[2,32,256]{2,1,0:T(8,128)S(1)}, u32[]{:S(2)}, u32[]{:S(2)}) %collective-permute-start.6) | collective-permute-done | bytes 65568 | tf_op jit(solution)/shard_map/ppermute | solution.py:48
  20.2 0.1 collective-permute-start.7
  20.3 0.0 collective-permute-done.rows
  20.3 0.7 %prepare.1 = (f32[8,48,256]{2,1,0:T(8,128)S(1)}, f32[4,8,48,256]{3,2,1,0:T(8,128)S(1)}, f32[4,8,48,256]{3,2,1,0:T(8,128)S(1)}) custom-call(f32[5,8,32,256]{3,2,1,0:T(8,128)S(1)} %get-tuple-element.26.fields, f32[40,16,256]{2,1,0:T(8,128)S(1)} %collective-permute-done.rows), custom_call_target="tpu_custom_call" | custom-call | bytes 60000 | tf_op jit(solution)/shard_map/prepare/pallas_call | solution.py:462
  21.0 0.0 collective-permute-done.3.corner
  21.0 0.8 %first.1 = (f32[4,8,48,256]{3,2,1,0:T(8,128)S(1)}, f32[2,48,256]{2,1,0:T(8,128)S(1)}, f32[4,2,48,256]{3,2,1,0:T(8,128)S(1)}, f32[2,48,256]{2,1,0:T(8,128)S(1)}) custom-call(f32[8,48,256]{2,1,0:T(8,128)S(1)} %get-tuple-element.27.start.refs_0_.refs_1_, f32[4,8,48,256]{3,2,1,0:T(8,128)S(1)} %get-tuple-element.28.coef.refs_2_, ...), custom_call_target="tpu_custom_call", output_to_operand_aliasing={{0}: (5, {})} | custom-call | bytes 60000 | tf_op jit(solution)/shard_map/first/pallas_call | solution.py:462
  21.7 0.0 collective-permute-done.7.later_corner
  21.7 0.7 %rest.1 = (f32[4,8,48,256]{3,2,1,0:T(8,128)S(1)}, f32[4,40,256]{2,1,0:T(8,128)S(1)}, f32[4,40,256]{2,1,0:T(8,128)S(1)}, f32[4,8,48,256]{3,2,1,0:T(8,128)S(1)}, f32[2,48,256]{2,1,0:T(8,128)S(1)}) custom-call(f32[8,48,256]{2,1,0:T(8,128)S(1)} %get-tuple-element.27.start.refs_0_.refs_1_, ...), custom_call_target="tpu_custom_call", output_to_operand_aliasing={{0}: (11, {})} | custom-call | bytes 60000 | tf_op jit(solution)/shard_map/rest/pallas_call | solution.py:462
  22.5 1.5 %collective-permute-start.8 = (f32[4,40,256]{2,1,0:T(8,128)S(1)}, f32[4,40,256]{2,1,0:T(8,128)S(1)}, u32[]{:S(2)}, u32[]{:S(2)}) collective-permute-start(f32[4,40,256]{2,1,0:T(8,128)S(1)} %get-tuple-element.43), channel_id=1, source_target_pairs={{0,2},{2,4},{4,6},{6,8},{8,10},{10,12},{12,14},{14,16},{16,18},{18... | collective-permute-start | bytes 491528 | tf_op jit(solution)/shard_map/ppermute | solution.py:48
  24.0 4.1 %collective-permute-start.9 = (f32[4,40,256]{2,1,0:T(8,128)S(1)}, f32[4,40,256]{2,1,0:T(8,128)S(1)}, u32[]{:S(2)}, u32[]{:S(2)}) collective-permute-start(f32[4,40,256]{2,1,0:T(8,128)S(1)} %get-tuple-element.45), channel_id=1, source_target_pairs={{0,30},{2,0},{4,2},{6,4},{8,6},{10,8},{12,10},{14,12},{16,14},{18,... | collective-permute-start | bytes 491528 | tf_op jit(solution)/shard_map/ppermute | solution.py:48
  28.1 0.9 %second_interior.1 = (f32[4,8,48,256]{3,2,1,0:T(8,128)S(1)}, f32[16,128]{1,0:T(8,128)S(1)}) custom-call(f32[8,48,256]{2,1,0:T(8,128)S(1)} %get-tuple-element.27.start.refs_0_.refs_1_, f32[4,8,48,256]{3,2,1,0:T(8,128)S(1)} %get-tuple-element.39.refs_1_.one.refs_2_, ...), custom_call_target="tpu_custom_call", output_to_operand_aliasing={{0}: (3, {})} | custom-call | bytes 60000 | tf_op jit(solution)/shard_map/second_interior/pallas_call | solution.py:462
  29.0 3.8 %collective-permute-done.8.low = f32[4,40,256]{2,1,0:T(8,128)S(1)} collective-permute-done((f32[4,40,256]{2,1,0:T(8,128)S(1)}, f32[4,40,256]{2,1,0:T(8,128)S(1)}, u32[]{:S(2)}, u32[]{:S(2)}) %collective-permute-start.8) | collective-permute-done | bytes 163872 | tf_op jit(solution)/shard_map/ppermute | solution.py:48
  32.8 0.9 %low.1 = (f32[4,8,48,256]{3,2,1,0:T(8,128)S(1)}, f32[30,8,128]{2,1,0:T(8,128)S(1)}) custom-call(f32[8,48,256]{2,1,0:T(8,128)S(1)} %get-tuple-element.27.start.refs_0_.refs_1_, f32[4,8,48,256]{3,2,1,0:T(8,128)S(1)} %get-tuple-element.39.refs_1_.one.refs_2_, f32[4,8,48,256]{3,2,1,0:T(8,128)S(1)} %get-tuple-element.41.given, ...), custom_call_target="tpu_custom_call", output_to_operand_aliasing={{0}: (2, {})} | custom-call | bytes 60000 | tf_op jit(solution)/shard_map/low/pallas_call | solution.py:462
  33.8 0.1 collective-permute-done.9.high
  33.8 1.0 %high.1 = (f32[4,8,48,256]{3,2,1,0:T(8,128)S(1)}, f32[32,128]{1,0:T(8,128)S(1)}) custom-call(f32[8,48,256]{2,1,0:T(8,128)S(1)} %get-tuple-element.27.start.refs_0_.refs_1_, f32[4,8,48,256]{3,2,1,0:T(8,128)S(1)} %get-tuple-element.39.refs_1_.one.refs_2_, f32[4,8,48,256]{3,2,1,0:T(8,128)S(1)} %get-tuple-element.44.given, ...), custom_call_target="tpu_custom_call", output_to_operand_aliasing={{0}: (2, {})} | custom-call | bytes 60000 | tf_op jit(solution)/shard_map/high/pallas_call | solution.py:462
  34.9 11.5 %all_to_all.11 = f32[32,1,128]{2,1,0:T(1,128)S(1)} all-to-all(f32[32,1,128]{2,1,0:T(1,128)S(1)} %bitcast.7), channel_id=1, replica_groups=mesh['gx'=16,'gy'=2] {'gx','gy'}, dimensions={0} | all-to-all | bytes 32768 | tf_op jit(solution)/shard_map/all_to_all | solution.py:581
  46.4 2.2 %last.1 = (f32[9,8,32,256]{3,2,1,0:T(8,128)}, f32[9,9]{1,0:T(8,128)}) custom-call(f32[32,128]{1,0:T(8,128)S(1)} %bitcast.6, f32[8,48,256]{2,1,0:T(8,128)S(1)} %get-tuple-element.27.start.refs_0_.refs_1_, f32[4,8,48,256]{3,2,1,0:T(8,128)S(1)} %get-tuple-element.39.refs_1_.one.refs_2_, f32[4,8,48,256]{3,2,1,0:T(8,128)S(1)} %get-tuple-element.49.refs_3_), custom_call_target="tpu_custom_call" | custom-call | bytes 60000 | tf_op jit(solution)/shard_map/last/pallas_call | solution.py:462
  (10 shorter events, 0.2 us)
Async XLA Ops:
  2.0 7.4 %collective-permute-start.4 = (f32[22,8,256]{2,1,0:T(8,128)S(1)}, f32[22,8,256]{2,1,0:T(8,128)S(1)}, u32[]{:S(2)}, u32[]{:S(2)}) collective-permute-start(f32[22,8,256]{2,1,0:T(8,128)S(1)} %get-tuple-element.35), channel_id=1, source_target_pairs={{0,1},{1,0},{2,3},{3,2},{4,5},{5,4},{6,7},{7,6},{8,9},{9,8},{10,11... | collective-permute-start | bytes 540680 | tf_op jit(solution)/shard_map/ppermute | solution.py:58
  2.5 14.8 %collective-permute-start.1 = (f32[7,32,256]{2,1,0:T(8,128)S(1)}, f32[7,32,256]{2,1,0:T(8,128)S(1)}, u32[]{:S(2)}, u32[]{:S(2)}) collective-permute-start(f32[7,32,256]{2,1,0:T(8,128)S(1)} %get-tuple-element.29), channel_id=1, source_target_pairs={{0,2},{2,4},{4,6},{6,8},{8,10},{10,12},{12,14},{14,16},{16,18},{18... | collective-permute-start | bytes 688136 | tf_op jit(solution)/shard_map/ppermute | solution.py:48
  5.0 12.8 %collective-permute-start.2 = (f32[7,32,256]{2,1,0:T(8,128)S(1)}, f32[7,32,256]{2,1,0:T(8,128)S(1)}, u32[]{:S(2)}, u32[]{:S(2)}) collective-permute-start(f32[7,32,256]{2,1,0:T(8,128)S(1)} %get-tuple-element.30), channel_id=1, source_target_pairs={{0,30},{2,0},{4,2},{6,4},{8,6},{10,8},{12,10},{14,12},{16,14},{18,... | collective-permute-start | bytes 688136 | tf_op jit(solution)/shard_map/ppermute | solution.py:48
  9.2 11.1 %collective-permute-start = (f32[40,16,256]{2,1,0:T(8,128)S(1)}, f32[40,16,256]{2,1,0:T(8,128)S(1)}, u32[]{:S(2)}, u32[]{:S(2)}) collective-permute-start(f32[40,16,256]{2,1,0:T(8,128)S(1)} %pad_maximum_fusion), channel_id=1, source_target_pairs={{0,1},{1,0},{2,3},{3,2},{4,5},{5,4},{6,7},{7,6},{8,9},{9,8},{10,11... | collective-permute-start | bytes 1966088 | tf_op jit(solution)/shard_map/ppermute | solution.py:58
  9.6 8.6 %collective-permute-start.5 = (f32[2,32,256]{2,1,0:T(8,128)S(1)}, f32[2,32,256]{2,1,0:T(8,128)S(1)}, u32[]{:S(2)}, u32[]{:S(2)}) collective-permute-start(f32[2,32,256]{2,1,0:T(8,128)S(1)} %get-tuple-element.36), channel_id=1, source_target_pairs={{0,2},{2,4},{4,6},{6,8},{8,10},{10,12},{12,14},{14,16},{16,18},{18... | collective-permute-start | bytes 196616 | tf_op jit(solution)/shard_map/ppermute | solution.py:48
  9.7 10.5 %collective-permute-start.6 = (f32[2,32,256]{2,1,0:T(8,128)S(1)}, f32[2,32,256]{2,1,0:T(8,128)S(1)}, u32[]{:S(2)}, u32[]{:S(2)}) collective-permute-start(f32[2,32,256]{2,1,0:T(8,128)S(1)} %get-tuple-element.37), channel_id=1, source_target_pairs={{0,30},{2,0},{4,2},{6,4},{8,6},{10,8},{12,10},{14,12},{16,14},{18,... | collective-permute-start | bytes 196616 | tf_op jit(solution)/shard_map/ppermute | solution.py:48
  17.9 3.1 %collective-permute-start.3 = (f32[14,16,256]{2,1,0:T(8,128)S(1)}, f32[14,16,256]{2,1,0:T(8,128)S(1)}, u32[]{:S(2)}, u32[]{:S(2)}) collective-permute-start(f32[14,16,256]{2,1,0:T(8,128)S(1)} %pad_maximum_fusion.1), channel_id=1, source_target_pairs={{0,1},{1,0},{2,3},{3,2},{4,5},{5,4},{6,7},{7,6},{8,9},{9,8},{10,11... | collective-permute-start | bytes 688136 | tf_op jit(solution)/shard_map/ppermute | solution.py:58
  20.2 1.5 %collective-permute-start.7 = (f32[4,16,256]{2,1,0:T(8,128)S(1)}, f32[4,16,256]{2,1,0:T(8,128)S(1)}, u32[]{:S(2)}, u32[]{:S(2)}) collective-permute-start(f32[4,16,256]{2,1,0:T(8,128)S(1)} %pad_maximum_fusion.2), channel_id=1, source_target_pairs={{0,1},{1,0},{2,3},{3,2},{4,5},{5,4},{6,7},{7,6},{8,9},{9,8},{10,11... | collective-permute-start | bytes 196616 | tf_op jit(solution)/shard_map/ppermute | solution.py:58
  22.5 10.3 %collective-permute-start.8 = (f32[4,40,256]{2,1,0:T(8,128)S(1)}, f32[4,40,256]{2,1,0:T(8,128)S(1)}, u32[]{:S(2)}, u32[]{:S(2)}) collective-permute-start(f32[4,40,256]{2,1,0:T(8,128)S(1)} %get-tuple-element.43), channel_id=1, source_target_pairs={{0,2},{2,4},{4,6},{6,8},{8,10},{10,12},{12,14},{14,16},{16,18},{18... | collective-permute-start | bytes 491528 | tf_op jit(solution)/shard_map/ppermute | solution.py:48
  24.0 9.8 %collective-permute-start.9 = (f32[4,40,256]{2,1,0:T(8,128)S(1)}, f32[4,40,256]{2,1,0:T(8,128)S(1)}, u32[]{:S(2)}, u32[]{:S(2)}) collective-permute-start(f32[4,40,256]{2,1,0:T(8,128)S(1)} %get-tuple-element.45), channel_id=1, source_target_pairs={{0,30},{2,0},{4,2},{6,4},{8,6},{10,8},{12,10},{14,12},{16,14},{18,... | collective-permute-start | bytes 491528 | tf_op jit(solution)/shard_map/ppermute | solution.py:48

commit v6 on v5

--- a/solution.py
+++ b/solution.py
@@ -346,15 +346,18 @@
             cells.tip(STEPS, two, below),
         ]
         for at, layer in enumerate(leaving):
-            above, under = layer[by : by + MARGIN], layer[by + MARGIN :]
-            row = lax.broadcasted_iota(jnp.int32, above.shape, 0)
-            out[at, 0:by] = layer[:by]
-            out[at, by:] = jnp.where(row < EDGE, above, under)
+            out[at * by : (at + 1) * by] = layer[:by]
+        tiles = [(layer[by : by + MARGIN], layer[by + MARGIN :]) for layer in leaving[:3]]
+        row = lax.broadcasted_iota(jnp.int32, tiles[0][0].shape, 0)
+        out[4 * by : 4 * by + 8] = jnp.where(row < EDGE, *tiles[0])
+        middle = jnp.where(row < EDGE, pltpu.roll(tiles[2][0], 2, 0), pltpu.roll(tiles[2][1], 6, 0))
+        outer = jnp.where(row < EDGE, *tiles[1])
+        out[4 * by + 8 :] = jnp.where((row == 2) | (row == 5), middle, outer)
 
 
 def second_cells(one, sides, coef, edge, weight, slab, side, two, scratch):
     bx = coef.shape[1]
-    by = slab.shape[1] - 2 * EDGE
+    by = slab.shape[0] // 4 - EDGE
     places = own_places(bx, STEPS, two) | halo_places(bx, STEPS, scratch)
     cells = Cells(bx, coef, edge, lambda j, x: places[j, x])
     mark_interior(cells, bx, STEPS, two)
@@ -364,7 +367,9 @@
     near, far = halo_layer(bx, 1, side == 0), halo_layer(bx, 2, side == 0)
 
     def wide(at):
-        return jnp.concatenate([slab[at], slab[at, by:]], axis=0)
+        first, second = slab[4 * by : 4 * by + 8], slab[4 * by + 8 :]
+        above, below = ((first, first), (second, second), (pltpu.roll(second, 6, 0), pltpu.roll(second, 2, 0)))[min(at, 2)]
+        return jnp.concatenate([slab[at * by : (at + 1) * by], above, below], axis=0)
 
     cells.known[STEPS - 1, near] = lambda: sides[side]
     cells.known[STEPS, near] = lambda: wide(0)
@@ -374,34 +379,36 @@
     return cells
 
 
-def low_kernel(start, one, given, sides, coef, edge, weight, low, two, partial, scratch):
+def reach_of(j):
+    return max([m for i, m in COMPUTED if i == j], default=0)
+
+
+def sooner_kernel(start, one, given, sides, coef, edge, weight, high, two, partial, scratch):
     del given
     bx, _, nz = start.shape
-    by = low.shape[1] - 2 * EDGE
+    by = high.shape[0] // 4 - EDGE
+    cells = second_cells(one, sides, coef, edge, weight, high, 1, two, scratch)
+    for j in range(1, STEPS + 1):
+        for x in range(j, bx + reach_of(j)):
+            cells.get(STEPS + j, x)
+    totals = products(GROUPS[1], STEPS, bx, by, nz, reader(start, one, two))
+    for k, total in enumerate(totals):
+        partial[k] = total
+
+
+def later_kernel(start, one, given, sides, coef, edge, weight, low, early_gram, partial, two, gram, scratch):
+    del given
+    bx, _, nz = start.shape
+    by = low.shape[0] // 4 - EDGE
     cells = second_cells(one, sides, coef, edge, weight, low, 0, two, scratch)
     for j in range(1, STEPS + 1):
-        reach = max([m for i, m in COMPUTED if i == j], default=0)
-        for x in range(-reach, bx - j):
-            cells.get(STEPS + j, x)
-    totals = products(GROUPS[1], 0, bx - STEPS, by, nz, reader(start, one, two))
-    for k, total in enumerate(totals):
-        partial[k] = total
-
-
-def high_kernel(start, one, given, sides, coef, edge, weight, high, early_gram, partial, two, gram, scratch):
-    del given
-    bx, _, nz = start.shape
-    by = high.shape[1] - 2 * EDGE
-    cells = second_cells(one, sides, coef, edge, weight, high, 1, two, scratch)
-    for j in range(1, STEPS + 1):
-        for x in range(bx - j):
+        for x in range(j, bx):
             cells.known[STEPS + j, x] = lambda j=j, x=x: two[j - 1, x]
     for j in range(1, STEPS + 1):
-        reach = max([m for i, m in COMPUTED if i == j], default=0)
-        for x in range(bx - j, bx + reach):
+        for x in range(-reach_of(j), j):
             cells.get(STEPS + j, x)
     before = tuple(partial[k] for k in range(len(GROUPS[1])))
-    rows = summed_rows(products(GROUPS[1], bx - STEPS, bx, by, nz, reader(start, one, two), before))
+    rows = summed_rows(products(GROUPS[1], 0, STEPS, by, nz, reader(start, one, two), before))
     sums = jnp.concatenate([early_gram[...]] + rows, axis=0)
     on = lax.broadcasted_iota(jnp.int32, sums.shape, 0) == lax.broadcasted_iota(jnp.int32, sums.shape, 1)
     line = jnp.sum(jnp.where(on, jnp.sum(sums, axis=1, keepdims=True), 0.0), axis=0, keepdims=True)
@@ -517,7 +524,7 @@
     )
     one, to_low, to_high, two, sides = call(
         rest_kernel,
-        [vectors, shape(4, by + 2 * EDGE, nz), shape(4, by + 2 * EDGE, nz), vectors, shape(2, wide, nz)],
+        [vectors, shape(4 * by + 16, nz), shape(4 * by + 16, nz), vectors, shape(2, wide, nz)],
         start,
         coef,
         low,
@@ -547,7 +554,7 @@
     )
     halo = [pltpu.VMEM((2 * len(COMPUTED), wide, nz), jnp.float32)]
     two, partial = call(
-        low_kernel,
+        sooner_kernel,
         [vectors, shape(len(GROUPS[1]), 8, 128)],
         start,
         one,
@@ -556,13 +563,13 @@
         coef,
         edge,
         weight,
-        low,
-        name="low",
+        high,
+        name="sooner",
         scratch=halo,
         aliases={2: 0},
     )
     two, gram = call(
-        high_kernel,
+        later_kernel,
         [vectors, shape(devices, 128)],
         start,
         one,
@@ -571,10 +578,10 @@
         coef,
         edge,
         weight,
-        high,
+        low,
         early_gram,
         partial,
-        name="high",
+        name="later",
         scratch=halo,
         aliases={2: 0},
     )

time: 48.8 us -> 48.1 us (0.986)
  waiting for transfers between devices: 8.58 us -> 12.5 us
  blocking collectives: 11.5 us -> 8.98 us
  starting transfers between devices: 18.8 us -> 16.8 us
    ppermute x3, waiting for transfers between devices: 2.53 us -> 5.36 us  [swap_x(): lax.ppermute(to_low, 'gx', ring('gx', -1))]
    all_to_all x1, blocking collectives: 11.5 us -> 8.98 us  [per_device(): gram = lax.all_to_all(gram, AXES, 0, 0, tiled=True)]
    ppermute x3, starting transfers between devices: 4.15 us -> 2.61 us  [swap_x(): lax.ppermute(to_high, 'gx', ring('gx', 1))]
    ppermute x3, waiting for transfers between devices: 6.04 us -> 7.1 us  [swap_x(): lax.ppermute(to_high, 'gx', ring('gx', 1))]
where the time goes in v6:
time: 48.1 us; the launch traced here: 47.9 us
  starting transfers between devices  16.8 us (35%)
  waiting for transfers between devices  12.5 us (26%)
  blocking collectives  8.98 us (19%)
  Pallas kernels  8.74 us (18%)
  between operations  0.78 us (2%)
    ppermute x3, starting transfers between devices, swap_x(): lax.ppermute(to_low, 'gx', ring('gx', -1))  13.3 us
    all_to_all x1, blocking collectives, per_device(): gram = lax.all_to_all(gram, AXES, 0, 0, tiled=True)  8.98 us
    pallas_call x9, Pallas kernels, call(): pl.pallas_call(kernel, out_shape=outs, in_specs=in_specs or [VMEM] * len(...  8.74 us
    ppermute x3, waiting for transfers between devices, swap_x(): lax.ppermute(to_high, 'gx', ring('gx', 1))  7.1 us
    ppermute x3, waiting for transfers between devices, swap_x(): lax.ppermute(to_low, 'gx', ring('gx', -1))  5.36 us
    ppermute x3, starting transfers between devices, swap_x(): lax.ppermute(to_high, 'gx', ring('gx', 1))  2.61 us
  transfers between devices with their start and end apart: 10, of which 6 were waited for; matrix products, arithmetic and copies ran while one was open for 0% of the time, Pallas kernels for 7%

profile of v6, /device:TPU:0, one launch (start us, length us, event | category | flops | bytes accessed | tf_op | source)
XLA Modules:
  0.0 47.9 jit_solution(8750932175964939507)
XLA Ops:
  0.6 1.3 %pack.1 = (f32[5,8,32,256]{3,2,1,0:T(8,128)S(1)}, f32[7,32,256]{2,1,0:T(8,128)S(1)}, f32[7,32,256]{2,1,0:T(8,128)S(1)}, f32[22,8,256]{2,1,0:T(8,128)S(1)}) custom-call(f32[8,32,256]{2,1,0:T(8,128)} %f.1, f32[8,32,256]{2,1,0:T(8,128)} %r.1, f32[3,8,32,256]{3,2,1,0:T(8,128)} %vel.1), custom_call_target="tpu_custom_call" | custom-call | bytes 60000 | tf_op jit(solution)/shard_map/pack/pallas_call | solution.py:469
  2.0 0.5 %collective-permute-start.4 = (f32[22,8,256]{2,1,0:T(8,128)S(1)}, f32[22,8,256]{2,1,0:T(8,128)S(1)}, u32[]{:S(2)}, u32[]{:S(2)}) collective-permute-start(f32[22,8,256]{2,1,0:T(8,128)S(1)} %get-tuple-element.35), channel_id=1, source_target_pairs={{0,1},{1,0},{2,3},{3,2},{4,5},{5,4},{6,7},{7,6},{8,9},{9,8},{10,11... | collective-permute-start | bytes 540680 | tf_op jit(solution)/shard_map/ppermute | solution.py:58
  2.5 2.6 %collective-permute-start.1 = (f32[7,32,256]{2,1,0:T(8,128)S(1)}, f32[7,32,256]{2,1,0:T(8,128)S(1)}, u32[]{:S(2)}, u32[]{:S(2)}) collective-permute-start(f32[7,32,256]{2,1,0:T(8,128)S(1)} %get-tuple-element.29), channel_id=1, source_target_pairs={{0,2},{2,4},{4,6},{6,8},{8,10},{10,12},{12,14},{14,16},{16,18},{18... | collective-permute-start | bytes 688136 | tf_op jit(solution)/shard_map/ppermute | solution.py:48
  5.0 4.1 %collective-permute-start.2 = (f32[7,32,256]{2,1,0:T(8,128)S(1)}, f32[7,32,256]{2,1,0:T(8,128)S(1)}, u32[]{:S(2)}, u32[]{:S(2)}) collective-permute-start(f32[7,32,256]{2,1,0:T(8,128)S(1)} %get-tuple-element.30), channel_id=1, source_target_pairs={{0,30},{2,0},{4,2},{6,4},{8,6},{10,8},{12,10},{14,12},{16,14},{18,... | collective-permute-start | bytes 688136 | tf_op jit(solution)/shard_map/ppermute | solution.py:48
  9.2 0.1 collective-permute-start
  9.4 0.0 collective-permute-done.4.rows
  9.4 0.3 inner.1
  9.6 0.1 collective-permute-start.5
  9.7 5.6 %collective-permute-start.6 = (f32[2,32,256]{2,1,0:T(8,128)S(1)}, f32[2,32,256]{2,1,0:T(8,128)S(1)}, u32[]{:S(2)}, u32[]{:S(2)}) collective-permute-start(f32[2,32,256]{2,1,0:T(8,128)S(1)} %get-tuple-element.37), channel_id=1, source_target_pairs={{0,30},{2,0},{4,2},{6,4},{8,6},{10,8},{12,10},{14,12},{16,14},{18,... | collective-permute-start | bytes 196616 | tf_op jit(solution)/shard_map/ppermute | solution.py:48
  15.3 2.0 %collective-permute-done.1.low = f32[7,32,256]{2,1,0:T(8,128)S(1)} collective-permute-done((f32[7,32,256]{2,1,0:T(8,128)S(1)}, f32[7,32,256]{2,1,0:T(8,128)S(1)}, u32[]{:S(2)}, u32[]{:S(2)}) %collective-permute-start.1) | collective-permute-done | bytes 229408 | tf_op jit(solution)/shard_map/ppermute | solution.py:48
  17.3 0.5 %collective-permute-done.2.high = f32[7,32,256]{2,1,0:T(8,128)S(1)} collective-permute-done((f32[7,32,256]{2,1,0:T(8,128)S(1)}, f32[7,32,256]{2,1,0:T(8,128)S(1)}, u32[]{:S(2)}, u32[]{:S(2)}) %collective-permute-start.2) | collective-permute-done | bytes 229408 | tf_op jit(solution)/shard_map/ppermute | solution.py:48
  17.9 0.1 collective-permute-start.3
  18.0 0.3 collective-permute-done.5.low_later
  18.2 1.9 %collective-permute-done.6.high_later = f32[2,32,256]{2,1,0:T(8,128)S(1)} collective-permute-done((f32[2,32,256]{2,1,0:T(8,128)S(1)}, f32[2,32,256]{2,1,0:T(8,128)S(1)}, u32[]{:S(2)}, u32[]{:S(2)}) %collective-permute-start.6) | collective-permute-done | bytes 65568 | tf_op jit(solution)/shard_map/ppermute | solution.py:48
  20.2 0.1 collective-permute-start.7
  20.3 0.0 collective-permute-done.rows
  20.3 0.7 %prepare.1 = (f32[8,48,256]{2,1,0:T(8,128)S(1)}, f32[4,8,48,256]{3,2,1,0:T(8,128)S(1)}, f32[4,8,48,256]{3,2,1,0:T(8,128)S(1)}) custom-call(f32[5,8,32,256]{3,2,1,0:T(8,128)S(1)} %get-tuple-element.26.fields, f32[40,16,256]{2,1,0:T(8,128)S(1)} %collective-permute-done.rows), custom_call_target="tpu_custom_call" | custom-call | bytes 60000 | tf_op jit(solution)/shard_map/prepare/pallas_call | solution.py:469
  21.0 0.0 collective-permute-done.3.corner
  21.0 0.8 %first.1 = (f32[4,8,48,256]{3,2,1,0:T(8,128)S(1)}, f32[2,48,256]{2,1,0:T(8,128)S(1)}, f32[4,2,48,256]{3,2,1,0:T(8,128)S(1)}, f32[2,48,256]{2,1,0:T(8,128)S(1)}) custom-call(f32[8,48,256]{2,1,0:T(8,128)S(1)} %get-tuple-element.27.start.refs_0_.refs_1_, f32[4,8,48,256]{3,2,1,0:T(8,128)S(1)} %get-tuple-element.28.coef.refs_2_, ...), custom_call_target="tpu_custom_call", output_to_operand_aliasing={{0}: (5, {})} | custom-call | bytes 60000 | tf_op jit(solution)/shard_map/first/pallas_call | solution.py:469
  21.7 0.0 collective-permute-done.7.later_corner
  21.7 0.7 %rest.1 = (f32[4,8,48,256]{3,2,1,0:T(8,128)S(1)}, f32[144,256]{1,0:T(8,128)S(1)}, f32[144,256]{1,0:T(8,128)S(1)}, f32[4,8,48,256]{3,2,1,0:T(8,128)S(1)}, f32[2,48,256]{2,1,0:T(8,128)S(1)}) custom-call(f32[8,48,256]{2,1,0:T(8,128)S(1)} %get-tuple-element.27.start.refs_0_.refs_1_, ...), custom_call_target="tpu_custom_call", output_to_operand_aliasing={{0}: (11, {})} | custom-call | bytes 60000 | tf_op jit(solution)/shard_map/rest/pallas_call | solution.py:469
  22.4 3.7 %collective-permute-start.8 = (f32[144,256]{1,0:T(8,128)S(1)}, f32[144,256]{1,0:T(8,128)S(1)}, u32[]{:S(2)}, u32[]{:S(2)}) collective-permute-start(f32[144,256]{1,0:T(8,128)S(1)} %get-tuple-element.43), channel_id=1, source_target_pairs={{0,30},{2,0},{4,2},{6,4},{8,6},{10,8},{12,10},{14,12},{16,14},{18,... | collective-permute-start | bytes 442376 | tf_op jit(solution)/shard_map/ppermute | solution.py:48
  26.1 0.0 collective-permute-start.9
  26.1 0.9 %second_interior.1 = (f32[4,8,48,256]{3,2,1,0:T(8,128)S(1)}, f32[16,128]{1,0:T(8,128)S(1)}) custom-call(f32[8,48,256]{2,1,0:T(8,128)S(1)} %get-tuple-element.27.start.refs_0_.refs_1_, f32[4,8,48,256]{3,2,1,0:T(8,128)S(1)} %get-tuple-element.39.refs_1_.one.refs_2_, ...), custom_call_target="tpu_custom_call", output_to_operand_aliasing={{0}: (3, {})} | custom-call | bytes 60000 | tf_op jit(solution)/shard_map/second_interior/pallas_call | solution.py:469
  27.0 2.9 %collective-permute-done.8.high = f32[144,256]{1,0:T(8,128)S(1)} collective-permute-done((f32[144,256]{1,0:T(8,128)S(1)}, f32[144,256]{1,0:T(8,128)S(1)}, u32[]{:S(2)}, u32[]{:S(2)}) %collective-permute-start.8) | collective-permute-done | bytes 147488 | tf_op jit(solution)/shard_map/ppermute | solution.py:48
  29.9 0.9 %sooner.1 = (f32[4,8,48,256]{3,2,1,0:T(8,128)S(1)}, f32[30,8,128]{2,1,0:T(8,128)S(1)}) custom-call(f32[8,48,256]{2,1,0:T(8,128)S(1)} %get-tuple-element.27.start.refs_0_.refs_1_, f32[4,8,48,256]{3,2,1,0:T(8,128)S(1)} %get-tuple-element.39.refs_1_.one.refs_2_, f32[4,8,48,256]{3,2,1,0:T(8,128)S(1)} %get-tuple-element.41.given, ...), custom_call_target="tpu_custom_call", output_to_operand_aliasing={{0}: (2, {})} | custom-call | bytes 60000 | tf_op jit(solution)/shard_map/sooner/pallas_call | solution.py:469
  30.8 4.9 %collective-permute-done.9.low = f32[144,256]{1,0:T(8,128)S(1)} collective-permute-done((f32[144,256]{1,0:T(8,128)S(1)}, f32[144,256]{1,0:T(8,128)S(1)}, u32[]{:S(2)}, u32[]{:S(2)}) %collective-permute-start.9) | collective-permute-done | bytes 147488 | tf_op jit(solution)/shard_map/ppermute | solution.py:48
  35.7 1.1 %later.1 = (f32[4,8,48,256]{3,2,1,0:T(8,128)S(1)}, f32[32,128]{1,0:T(8,128)S(1)}) custom-call(f32[8,48,256]{2,1,0:T(8,128)S(1)} %get-tuple-element.27.start.refs_0_.refs_1_, f32[4,8,48,256]{3,2,1,0:T(8,128)S(1)} %get-tuple-element.39.refs_1_.one.refs_2_, f32[4,8,48,256]{3,2,1,0:T(8,128)S(1)} %get-tuple-element.44.given, ...), custom_call_target="tpu_custom_call", output_to_operand_aliasing={{0}: (2, {})} | custom-call | bytes 60000 | tf_op jit(solution)/shard_map/later/pallas_call | solution.py:469
  36.7 9.0 %all_to_all.11 = f32[32,1,128]{2,1,0:T(1,128)S(1)} all-to-all(f32[32,1,128]{2,1,0:T(1,128)S(1)} %bitcast.7), channel_id=1, replica_groups=mesh['gx'=16,'gy'=2] {'gx','gy'}, dimensions={0} | all-to-all | bytes 32768 | tf_op jit(solution)/shard_map/all_to_all | solution.py:588
  45.7 2.2 %last.1 = (f32[9,8,32,256]{3,2,1,0:T(8,128)}, f32[9,9]{1,0:T(8,128)}) custom-call(f32[32,128]{1,0:T(8,128)S(1)} %bitcast.6, f32[8,48,256]{2,1,0:T(8,128)S(1)} %get-tuple-element.27.start.refs_0_.refs_1_, f32[4,8,48,256]{3,2,1,0:T(8,128)S(1)} %get-tuple-element.39.refs_1_.one.refs_2_, f32[4,8,48,256]{3,2,1,0:T(8,128)S(1)} %get-tuple-element.49.refs_3_), custom_call_target="tpu_custom_call" | custom-call | bytes 60000 | tf_op jit(solution)/shard_map/last/pallas_call | solution.py:469
  (10 shorter events, 0.2 us)
Async XLA Ops:
  2.0 7.4 %collective-permute-start.4 = (f32[22,8,256]{2,1,0:T(8,128)S(1)}, f32[22,8,256]{2,1,0:T(8,128)S(1)}, u32[]{:S(2)}, u32[]{:S(2)}) collective-permute-start(f32[22,8,256]{2,1,0:T(8,128)S(1)} %get-tuple-element.35), channel_id=1, source_target_pairs={{0,1},{1,0},{2,3},{3,2},{4,5},{5,4},{6,7},{7,6},{8,9},{9,8},{10,11... | collective-permute-start | bytes 540680 | tf_op jit(solution)/shard_map/ppermute | solution.py:58
  2.5 14.8 %collective-permute-start.1 = (f32[7,32,256]{2,1,0:T(8,128)S(1)}, f32[7,32,256]{2,1,0:T(8,128)S(1)}, u32[]{:S(2)}, u32[]{:S(2)}) collective-permute-start(f32[7,32,256]{2,1,0:T(8,128)S(1)} %get-tuple-element.29), channel_id=1, source_target_pairs={{0,2},{2,4},{4,6},{6,8},{8,10},{10,12},{12,14},{14,16},{16,18},{18... | collective-permute-start | bytes 688136 | tf_op jit(solution)/shard_map/ppermute | solution.py:48
  5.0 12.8 %collective-permute-start.2 = (f32[7,32,256]{2,1,0:T(8,128)S(1)}, f32[7,32,256]{2,1,0:T(8,128)S(1)}, u32[]{:S(2)}, u32[]{:S(2)}) collective-permute-start(f32[7,32,256]{2,1,0:T(8,128)S(1)} %get-tuple-element.30), channel_id=1, source_target_pairs={{0,30},{2,0},{4,2},{6,4},{8,6},{10,8},{12,10},{14,12},{16,14},{18,... | collective-permute-start | bytes 688136 | tf_op jit(solution)/shard_map/ppermute | solution.py:48
  9.2 11.1 %collective-permute-start = (f32[40,16,256]{2,1,0:T(8,128)S(1)}, f32[40,16,256]{2,1,0:T(8,128)S(1)}, u32[]{:S(2)}, u32[]{:S(2)}) collective-permute-start(f32[40,16,256]{2,1,0:T(8,128)S(1)} %pad_maximum_fusion), channel_id=1, source_target_pairs={{0,1},{1,0},{2,3},{3,2},{4,5},{5,4},{6,7},{7,6},{8,9},{9,8},{10,11... | collective-permute-start | bytes 1966088 | tf_op jit(solution)/shard_map/ppermute | solution.py:58
  9.6 8.6 %collective-permute-start.5 = (f32[2,32,256]{2,1,0:T(8,128)S(1)}, f32[2,32,256]{2,1,0:T(8,128)S(1)}, u32[]{:S(2)}, u32[]{:S(2)}) collective-permute-start(f32[2,32,256]{2,1,0:T(8,128)S(1)} %get-tuple-element.36), channel_id=1, source_target_pairs={{0,2},{2,4},{4,6},{6,8},{8,10},{10,12},{12,14},{14,16},{16,18},{18... | collective-permute-start | bytes 196616 | tf_op jit(solution)/shard_map/ppermute | solution.py:48
  9.7 10.5 %collective-permute-start.6 = (f32[2,32,256]{2,1,0:T(8,128)S(1)}, f32[2,32,256]{2,1,0:T(8,128)S(1)}, u32[]{:S(2)}, u32[]{:S(2)}) collective-permute-start(f32[2,32,256]{2,1,0:T(8,128)S(1)} %get-tuple-element.37), channel_id=1, source_target_pairs={{0,30},{2,0},{4,2},{6,4},{8,6},{10,8},{12,10},{14,12},{16,14},{18,... | collective-permute-start | bytes 196616 | tf_op jit(solution)/shard_map/ppermute | solution.py:48
  17.9 3.1 %collective-permute-start.3 = (f32[14,16,256]{2,1,0:T(8,128)S(1)}, f32[14,16,256]{2,1,0:T(8,128)S(1)}, u32[]{:S(2)}, u32[]{:S(2)}) collective-permute-start(f32[14,16,256]{2,1,0:T(8,128)S(1)} %pad_maximum_fusion.1), channel_id=1, source_target_pairs={{0,1},{1,0},{2,3},{3,2},{4,5},{5,4},{6,7},{7,6},{8,9},{9,8},{10,11... | collective-permute-start | bytes 688136 | tf_op jit(solution)/shard_map/ppermute | solution.py:58
  20.2 1.5 %collective-permute-start.7 = (f32[4,16,256]{2,1,0:T(8,128)S(1)}, f32[4,16,256]{2,1,0:T(8,128)S(1)}, u32[]{:S(2)}, u32[]{:S(2)}) collective-permute-start(f32[4,16,256]{2,1,0:T(8,128)S(1)} %pad_maximum_fusion.2), channel_id=1, source_target_pairs={{0,1},{1,0},{2,3},{3,2},{4,5},{5,4},{6,7},{7,6},{8,9},{9,8},{10,11... | collective-permute-start | bytes 196616 | tf_op jit(solution)/shard_map/ppermute | solution.py:58
  22.4 7.4 %collective-permute-start.8 = (f32[144,256]{1,0:T(8,128)S(1)}, f32[144,256]{1,0:T(8,128)S(1)}, u32[]{:S(2)}, u32[]{:S(2)}) collective-permute-start(f32[144,256]{1,0:T(8,128)S(1)} %get-tuple-element.43), channel_id=1, source_target_pairs={{0,30},{2,0},{4,2},{6,4},{8,6},{10,8},{12,10},{14,12},{16,14},{18,... | collective-permute-start | bytes 442376 | tf_op jit(solution)/shard_map/ppermute | solution.py:48
  26.1 9.6 %collective-permute-start.9 = (f32[144,256]{1,0:T(8,128)S(1)}, f32[144,256]{1,0:T(8,128)S(1)}, u32[]{:S(2)}, u32[]{:S(2)}) collective-permute-start(f32[144,256]{1,0:T(8,128)S(1)} %get-tuple-element.45), channel_id=1, source_target_pairs={{0,2},{2,4},{4,6},{6,8},{8,10},{10,12},{12,14},{14,16},{16,18},{18... | collective-permute-start | bytes 442376 | tf_op jit(solution)/shard_map/ppermute | solution.py:48

commit v7 on v6

--- a/solution.py
+++ b/solution.py
@@ -91,7 +91,7 @@
 
     if totals is None:
         totals = tuple(jnp.zeros((8, 128), jnp.float32) for _ in pairs)
-    return lax.fori_loop(0, (last - first) * tiles, add, totals, unroll=2)
+    return lax.fori_loop(0, (last - first) * tiles, add, totals, unroll=True)
 
 
 def summed_rows(totals):

time: 48.1 us -> 47.9 us (level)
  Pallas kernels: 8.74 us -> 8.22 us
    pallas_call x9, Pallas kernels: 8.74 us -> 8.22 us  [call(): pl.pallas_call(kernel, out_shape=outs, in_specs=in_specs or [VMEM] * len(...]
  transfers between devices with their start and end apart: 10 -> 10, of which waited for: 6 -> 6; matrix products, arithmetic and copies ran while one was open for 0% -> 0% of each run, Pallas kernels for 7% -> 6%
where the time goes in v7:
time: 47.9 us; the launch traced here: 47.8 us
  starting transfers between devices  16.8 us (35%)
  waiting for transfers between devices  12.8 us (27%)
  blocking collectives  8.99 us (19%)
  Pallas kernels  8.22 us (17%)
  between operations  0.78 us (2%)
    ppermute x3, starting transfers between devices, swap_x(): lax.ppermute(to_low, 'gx', ring('gx', -1))  13.3 us
    all_to_all x1, blocking collectives, per_device(): gram = lax.all_to_all(gram, AXES, 0, 0, tiled=True)  8.99 us
    pallas_call x9, Pallas kernels, call(): pl.pallas_call(kernel, out_shape=outs, in_specs=in_specs or [VMEM] * len(...  8.22 us
    ppermute x3, waiting for transfers between devices, swap_x(): lax.ppermute(to_high, 'gx', ring('gx', 1))  7.25 us
    ppermute x3, waiting for transfers between devices, swap_x(): lax.ppermute(to_low, 'gx', ring('gx', -1))  5.57 us
    ppermute x3, starting transfers between devices, swap_x(): lax.ppermute(to_high, 'gx', ring('gx', 1))  2.61 us
  transfers between devices with their start and end apart: 10, of which 6 were waited for; matrix products, arithmetic and copies ran while one was open for 0% of the time, Pallas kernels for 6%

profile of v7, /device:TPU:0, one launch (start us, length us, event | category | flops | bytes accessed | tf_op | source)
XLA Modules:
  0.0 47.8 jit_solution(11638671236497611679)
XLA Ops:
  0.6 1.3 %pack.1 = (f32[5,8,32,256]{3,2,1,0:T(8,128)S(1)}, f32[7,32,256]{2,1,0:T(8,128)S(1)}, f32[7,32,256]{2,1,0:T(8,128)S(1)}, f32[22,8,256]{2,1,0:T(8,128)S(1)}) custom-call(f32[8,32,256]{2,1,0:T(8,128)} %f.1, f32[8,32,256]{2,1,0:T(8,128)} %r.1, f32[3,8,32,256]{3,2,1,0:T(8,128)} %vel.1), custom_call_target="tpu_custom_call" | custom-call | bytes 60000 | tf_op jit(solution)/shard_map/pack/pallas_call | solution.py:469
  2.0 0.5 %collective-permute-start.4 = (f32[22,8,256]{2,1,0:T(8,128)S(1)}, f32[22,8,256]{2,1,0:T(8,128)S(1)}, u32[]{:S(2)}, u32[]{:S(2)}) collective-permute-start(f32[22,8,256]{2,1,0:T(8,128)S(1)} %get-tuple-element.35), channel_id=1, source_target_pairs={{0,1},{1,0},{2,3},{3,2},{4,5},{5,4},{6,7},{7,6},{8,9},{9,8},{10,11... | collective-permute-start | bytes 540680 | tf_op jit(solution)/shard_map/ppermute | solution.py:58
  2.5 2.6 %collective-permute-start.1 = (f32[7,32,256]{2,1,0:T(8,128)S(1)}, f32[7,32,256]{2,1,0:T(8,128)S(1)}, u32[]{:S(2)}, u32[]{:S(2)}) collective-permute-start(f32[7,32,256]{2,1,0:T(8,128)S(1)} %get-tuple-element.29), channel_id=1, source_target_pairs={{0,2},{2,4},{4,6},{6,8},{8,10},{10,12},{12,14},{14,16},{16,18},{18... | collective-permute-start | bytes 688136 | tf_op jit(solution)/shard_map/ppermute | solution.py:48
  5.0 4.1 %collective-permute-start.2 = (f32[7,32,256]{2,1,0:T(8,128)S(1)}, f32[7,32,256]{2,1,0:T(8,128)S(1)}, u32[]{:S(2)}, u32[]{:S(2)}) collective-permute-start(f32[7,32,256]{2,1,0:T(8,128)S(1)} %get-tuple-element.30), channel_id=1, source_target_pairs={{0,30},{2,0},{4,2},{6,4},{8,6},{10,8},{12,10},{14,12},{16,14},{18,... | collective-permute-start | bytes 688136 | tf_op jit(solution)/shard_map/ppermute | solution.py:48
  9.2 0.1 collective-permute-start
  9.4 0.0 collective-permute-done.4.rows
  9.4 0.3 inner.1
  9.6 0.1 collective-permute-start.5
  9.7 5.6 %collective-permute-start.6 = (f32[2,32,256]{2,1,0:T(8,128)S(1)}, f32[2,32,256]{2,1,0:T(8,128)S(1)}, u32[]{:S(2)}, u32[]{:S(2)}) collective-permute-start(f32[2,32,256]{2,1,0:T(8,128)S(1)} %get-tuple-element.37), channel_id=1, source_target_pairs={{0,30},{2,0},{4,2},{6,4},{8,6},{10,8},{12,10},{14,12},{16,14},{18,... | collective-permute-start | bytes 196616 | tf_op jit(solution)/shard_map/ppermute | solution.py:48
  15.3 2.0 %collective-permute-done.1.low = f32[7,32,256]{2,1,0:T(8,128)S(1)} collective-permute-done((f32[7,32,256]{2,1,0:T(8,128)S(1)}, f32[7,32,256]{2,1,0:T(8,128)S(1)}, u32[]{:S(2)}, u32[]{:S(2)}) %collective-permute-start.1) | collective-permute-done | bytes 229408 | tf_op jit(solution)/shard_map/ppermute | solution.py:48
  17.3 0.5 %collective-permute-done.2.high = f32[7,32,256]{2,1,0:T(8,128)S(1)} collective-permute-done((f32[7,32,256]{2,1,0:T(8,128)S(1)}, f32[7,32,256]{2,1,0:T(8,128)S(1)}, u32[]{:S(2)}, u32[]{:S(2)}) %collective-permute-start.2) | collective-permute-done | bytes 229408 | tf_op jit(solution)/shard_map/ppermute | solution.py:48
  17.9 0.1 collective-permute-start.3
  18.0 0.3 collective-permute-done.5.low_later
  18.2 1.9 %collective-permute-done.6.high_later = f32[2,32,256]{2,1,0:T(8,128)S(1)} collective-permute-done((f32[2,32,256]{2,1,0:T(8,128)S(1)}, f32[2,32,256]{2,1,0:T(8,128)S(1)}, u32[]{:S(2)}, u32[]{:S(2)}) %collective-permute-start.6) | collective-permute-done | bytes 65568 | tf_op jit(solution)/shard_map/ppermute | solution.py:48
  20.2 0.1 collective-permute-start.7
  20.3 0.0 collective-permute-done.rows
  20.3 0.7 %prepare.1 = (f32[8,48,256]{2,1,0:T(8,128)S(1)}, f32[4,8,48,256]{3,2,1,0:T(8,128)S(1)}, f32[4,8,48,256]{3,2,1,0:T(8,128)S(1)}) custom-call(f32[5,8,32,256]{3,2,1,0:T(8,128)S(1)} %get-tuple-element.26.fields, f32[40,16,256]{2,1,0:T(8,128)S(1)} %collective-permute-done.rows), custom_call_target="tpu_custom_call" | custom-call | bytes 60000 | tf_op jit(solution)/shard_map/prepare/pallas_call | solution.py:469
  21.0 0.0 collective-permute-done.3.corner
  21.0 0.8 %first.1 = (f32[4,8,48,256]{3,2,1,0:T(8,128)S(1)}, f32[2,48,256]{2,1,0:T(8,128)S(1)}, f32[4,2,48,256]{3,2,1,0:T(8,128)S(1)}, f32[2,48,256]{2,1,0:T(8,128)S(1)}) custom-call(f32[8,48,256]{2,1,0:T(8,128)S(1)} %get-tuple-element.27.start.refs_0_.refs_1_, f32[4,8,48,256]{3,2,1,0:T(8,128)S(1)} %get-tuple-element.28.coef.refs_2_, ...), custom_call_target="tpu_custom_call", output_to_operand_aliasing={{0}: (5, {})} | custom-call | bytes 60000 | tf_op jit(solution)/shard_map/first/pallas_call | solution.py:469
  21.7 0.0 collective-permute-done.7.later_corner
  21.7 0.7 %rest.1 = (f32[4,8,48,256]{3,2,1,0:T(8,128)S(1)}, f32[144,256]{1,0:T(8,128)S(1)}, f32[144,256]{1,0:T(8,128)S(1)}, f32[4,8,48,256]{3,2,1,0:T(8,128)S(1)}, f32[2,48,256]{2,1,0:T(8,128)S(1)}) custom-call(f32[8,48,256]{2,1,0:T(8,128)S(1)} %get-tuple-element.27.start.refs_0_.refs_1_, ...), custom_call_target="tpu_custom_call", output_to_operand_aliasing={{0}: (11, {})} | custom-call | bytes 60000 | tf_op jit(solution)/shard_map/rest/pallas_call | solution.py:469
  22.4 3.7 %collective-permute-start.8 = (f32[144,256]{1,0:T(8,128)S(1)}, f32[144,256]{1,0:T(8,128)S(1)}, u32[]{:S(2)}, u32[]{:S(2)}) collective-permute-start(f32[144,256]{1,0:T(8,128)S(1)} %get-tuple-element.43), channel_id=1, source_target_pairs={{0,30},{2,0},{4,2},{6,4},{8,6},{10,8},{12,10},{14,12},{16,14},{18,... | collective-permute-start | bytes 442376 | tf_op jit(solution)/shard_map/ppermute | solution.py:48
  26.1 0.0 collective-permute-start.9
  26.1 0.6 %second_interior.1 = (f32[4,8,48,256]{3,2,1,0:T(8,128)S(1)}, f32[16,128]{1,0:T(8,128)S(1)}) custom-call(f32[8,48,256]{2,1,0:T(8,128)S(1)} %get-tuple-element.27.start.refs_0_.refs_1_, f32[4,8,48,256]{3,2,1,0:T(8,128)S(1)} %get-tuple-element.39.refs_1_.one.refs_2_, ...), custom_call_target="tpu_custom_call", output_to_operand_aliasing={{0}: (3, {})} | custom-call | bytes 60000 | tf_op jit(solution)/shard_map/second_interior/pallas_call | solution.py:469
  26.7 3.1 %collective-permute-done.8.high = f32[144,256]{1,0:T(8,128)S(1)} collective-permute-done((f32[144,256]{1,0:T(8,128)S(1)}, f32[144,256]{1,0:T(8,128)S(1)}, u32[]{:S(2)}, u32[]{:S(2)}) %collective-permute-start.8) | collective-permute-done | bytes 147488 | tf_op jit(solution)/shard_map/ppermute | solution.py:48
  29.9 0.8 %sooner.1 = (f32[4,8,48,256]{3,2,1,0:T(8,128)S(1)}, f32[30,8,128]{2,1,0:T(8,128)S(1)}) custom-call(f32[8,48,256]{2,1,0:T(8,128)S(1)} %get-tuple-element.27.start.refs_0_.refs_1_, f32[4,8,48,256]{3,2,1,0:T(8,128)S(1)} %get-tuple-element.39.refs_1_.one.refs_2_, f32[4,8,48,256]{3,2,1,0:T(8,128)S(1)} %get-tuple-element.41.given, ...), custom_call_target="tpu_custom_call", output_to_operand_aliasing={{0}: (2, {})} | custom-call | bytes 60000 | tf_op jit(solution)/shard_map/sooner/pallas_call | solution.py:469
  30.6 5.0 %collective-permute-done.9.low = f32[144,256]{1,0:T(8,128)S(1)} collective-permute-done((f32[144,256]{1,0:T(8,128)S(1)}, f32[144,256]{1,0:T(8,128)S(1)}, u32[]{:S(2)}, u32[]{:S(2)}) %collective-permute-start.9) | collective-permute-done | bytes 147488 | tf_op jit(solution)/shard_map/ppermute | solution.py:48
  35.7 0.9 %later.1 = (f32[4,8,48,256]{3,2,1,0:T(8,128)S(1)}, f32[32,128]{1,0:T(8,128)S(1)}) custom-call(f32[8,48,256]{2,1,0:T(8,128)S(1)} %get-tuple-element.27.start.refs_0_.refs_1_, f32[4,8,48,256]{3,2,1,0:T(8,128)S(1)} %get-tuple-element.39.refs_1_.one.refs_2_, f32[4,8,48,256]{3,2,1,0:T(8,128)S(1)} %get-tuple-element.44.given, ...), custom_call_target="tpu_custom_call", output_to_operand_aliasing={{0}: (2, {})} | custom-call | bytes 60000 | tf_op jit(solution)/shard_map/later/pallas_call | solution.py:469
  36.6 9.0 %all_to_all.11 = f32[32,1,128]{2,1,0:T(1,128)S(1)} all-to-all(f32[32,1,128]{2,1,0:T(1,128)S(1)} %bitcast.7), channel_id=1, replica_groups=mesh['gx'=16,'gy'=2] {'gx','gy'}, dimensions={0} | all-to-all | bytes 32768 | tf_op jit(solution)/shard_map/all_to_all | solution.py:588
  45.6 2.2 %last.1 = (f32[9,8,32,256]{3,2,1,0:T(8,128)}, f32[9,9]{1,0:T(8,128)}) custom-call(f32[32,128]{1,0:T(8,128)S(1)} %bitcast.6, f32[8,48,256]{2,1,0:T(8,128)S(1)} %get-tuple-element.27.start.refs_0_.refs_1_, f32[4,8,48,256]{3,2,1,0:T(8,128)S(1)} %get-tuple-element.39.refs_1_.one.refs_2_, f32[4,8,48,256]{3,2,1,0:T(8,128)S(1)} %get-tuple-element.49.refs_3_), custom_call_target="tpu_custom_call" | custom-call | bytes 60000 | tf_op jit(solution)/shard_map/last/pallas_call | solution.py:469
  (10 shorter events, 0.2 us)
Async XLA Ops:
  2.0 7.4 %collective-permute-start.4 = (f32[22,8,256]{2,1,0:T(8,128)S(1)}, f32[22,8,256]{2,1,0:T(8,128)S(1)}, u32[]{:S(2)}, u32[]{:S(2)}) collective-permute-start(f32[22,8,256]{2,1,0:T(8,128)S(1)} %get-tuple-element.35), channel_id=1, source_target_pairs={{0,1},{1,0},{2,3},{3,2},{4,5},{5,4},{6,7},{7,6},{8,9},{9,8},{10,11... | collective-permute-start | bytes 540680 | tf_op jit(solution)/shard_map/ppermute | solution.py:58
  2.5 14.8 %collective-permute-start.1 = (f32[7,32,256]{2,1,0:T(8,128)S(1)}, f32[7,32,256]{2,1,0:T(8,128)S(1)}, u32[]{:S(2)}, u32[]{:S(2)}) collective-permute-start(f32[7,32,256]{2,1,0:T(8,128)S(1)} %get-tuple-element.29), channel_id=1, source_target_pairs={{0,2},{2,4},{4,6},{6,8},{8,10},{10,12},{12,14},{14,16},{16,18},{18... | collective-permute-start | bytes 688136 | tf_op jit(solution)/shard_map/ppermute | solution.py:48
  5.0 12.8 %collective-permute-start.2 = (f32[7,32,256]{2,1,0:T(8,128)S(1)}, f32[7,32,256]{2,1,0:T(8,128)S(1)}, u32[]{:S(2)}, u32[]{:S(2)}) collective-permute-start(f32[7,32,256]{2,1,0:T(8,128)S(1)} %get-tuple-element.30), channel_id=1, source_target_pairs={{0,30},{2,0},{4,2},{6,4},{8,6},{10,8},{12,10},{14,12},{16,14},{18,... | collective-permute-start | bytes 688136 | tf_op jit(solution)/shard_map/ppermute | solution.py:48
  9.2 11.1 %collective-permute-start = (f32[40,16,256]{2,1,0:T(8,128)S(1)}, f32[40,16,256]{2,1,0:T(8,128)S(1)}, u32[]{:S(2)}, u32[]{:S(2)}) collective-permute-start(f32[40,16,256]{2,1,0:T(8,128)S(1)} %pad_maximum_fusion), channel_id=1, source_target_pairs={{0,1},{1,0},{2,3},{3,2},{4,5},{5,4},{6,7},{7,6},{8,9},{9,8},{10,11... | collective-permute-start | bytes 1966088 | tf_op jit(solution)/shard_map/ppermute | solution.py:58
  9.6 8.6 %collective-permute-start.5 = (f32[2,32,256]{2,1,0:T(8,128)S(1)}, f32[2,32,256]{2,1,0:T(8,128)S(1)}, u32[]{:S(2)}, u32[]{:S(2)}) collective-permute-start(f32[2,32,256]{2,1,0:T(8,128)S(1)} %get-tuple-element.36), channel_id=1, source_target_pairs={{0,2},{2,4},{4,6},{6,8},{8,10},{10,12},{12,14},{14,16},{16,18},{18... | collective-permute-start | bytes 196616 | tf_op jit(solution)/shard_map/ppermute | solution.py:48
  9.7 10.5 %collective-permute-start.6 = (f32[2,32,256]{2,1,0:T(8,128)S(1)}, f32[2,32,256]{2,1,0:T(8,128)S(1)}, u32[]{:S(2)}, u32[]{:S(2)}) collective-permute-start(f32[2,32,256]{2,1,0:T(8,128)S(1)} %get-tuple-element.37), channel_id=1, source_target_pairs={{0,30},{2,0},{4,2},{6,4},{8,6},{10,8},{12,10},{14,12},{16,14},{18,... | collective-permute-start | bytes 196616 | tf_op jit(solution)/shard_map/ppermute | solution.py:48
  17.9 3.1 %collective-permute-start.3 = (f32[14,16,256]{2,1,0:T(8,128)S(1)}, f32[14,16,256]{2,1,0:T(8,128)S(1)}, u32[]{:S(2)}, u32[]{:S(2)}) collective-permute-start(f32[14,16,256]{2,1,0:T(8,128)S(1)} %pad_maximum_fusion.1), channel_id=1, source_target_pairs={{0,1},{1,0},{2,3},{3,2},{4,5},{5,4},{6,7},{7,6},{8,9},{9,8},{10,11... | collective-permute-start | bytes 688136 | tf_op jit(solution)/shard_map/ppermute | solution.py:58
  20.2 1.5 %collective-permute-start.7 = (f32[4,16,256]{2,1,0:T(8,128)S(1)}, f32[4,16,256]{2,1,0:T(8,128)S(1)}, u32[]{:S(2)}, u32[]{:S(2)}) collective-permute-start(f32[4,16,256]{2,1,0:T(8,128)S(1)} %pad_maximum_fusion.2), channel_id=1, source_target_pairs={{0,1},{1,0},{2,3},{3,2},{4,5},{5,4},{6,7},{7,6},{8,9},{9,8},{10,11... | collective-permute-start | bytes 196616 | tf_op jit(solution)/shard_map/ppermute | solution.py:58
  22.4 7.4 %collective-permute-start.8 = (f32[144,256]{1,0:T(8,128)S(1)}, f32[144,256]{1,0:T(8,128)S(1)}, u32[]{:S(2)}, u32[]{:S(2)}) collective-permute-start(f32[144,256]{1,0:T(8,128)S(1)} %get-tuple-element.43), channel_id=1, source_target_pairs={{0,30},{2,0},{4,2},{6,4},{8,6},{10,8},{12,10},{14,12},{16,14},{18,... | collective-permute-start | bytes 442376 | tf_op jit(solution)/shard_map/ppermute | solution.py:48
  26.1 9.6 %collective-permute-start.9 = (f32[144,256]{1,0:T(8,128)S(1)}, f32[144,256]{1,0:T(8,128)S(1)}, u32[]{:S(2)}, u32[]{:S(2)}) collective-permute-start(f32[144,256]{1,0:T(8,128)S(1)} %get-tuple-element.45), channel_id=1, source_target_pairs={{0,2},{2,4},{4,6},{6,8},{8,10},{10,12},{12,14},{14,16},{16,18},{18... | collective-permute-start | bytes 442376 | tf_op jit(solution)/shard_map/ppermute | solution.py:48

commit v8 on v7

--- a/solution.py
+++ b/solution.py
@@ -94,6 +94,17 @@
     return lax.fori_loop(0, (last - first) * tiles, add, totals, unroll=True)
 
 
+def later_products(layers, before, by, nz, cell):
+    totals, at = [], 0
+    for j in range(1, STEPS + 1):
+        pairs = [pair for pair in GROUPS[1] if pair[1] == STEPS + j]
+        group = tuple(before[at : at + len(pairs)])
+        first, last = layers(j)
+        totals += products(pairs, first, last, by, nz, cell, group) if last > first else group
+        at += len(pairs)
+    return totals
+
+
 def summed_rows(totals):
     sublane = lax.broadcasted_iota(jnp.int32, (8, 128), 0)
     rows = []
@@ -118,7 +129,7 @@
     return cell
 
 
-def second_interior_kernel(by, start, one, coef, given, vectors, gram):
+def second_interior_kernel(by, start, one, coef, given, vectors, gram, partial):
     del given
     bx, _, nz = start.shape
     places = own_places(bx, STEPS, vectors)
@@ -131,6 +142,10 @@
     cells.interior(STEPS)
     for k, row in enumerate(summed_rows(products(GROUPS[0], 0, bx, by, nz, reader(start, one)))):
         gram[8 * k : 8 * k + 8] = row
+    none = [jnp.zeros((8, 128), jnp.float32)] * len(GROUPS[1])
+    totals = later_products(lambda j: (j, bx - j), none, by, nz, reader(start, one, vectors))
+    for k, total in enumerate(totals):
+        partial[k] = total
 
 
 def fields_of(f, r, vel):
@@ -383,7 +398,7 @@
     return max([m for i, m in COMPUTED if i == j], default=0)
 
 
-def sooner_kernel(start, one, given, sides, coef, edge, weight, high, two, partial, scratch):
+def sooner_kernel(start, one, given, sides, coef, edge, weight, high, before, two, partial, scratch):
     del given
     bx, _, nz = start.shape
     by = high.shape[0] // 4 - EDGE
@@ -391,7 +406,8 @@
     for j in range(1, STEPS + 1):
         for x in range(j, bx + reach_of(j)):
             cells.get(STEPS + j, x)
-    totals = products(GROUPS[1], STEPS, bx, by, nz, reader(start, one, two))
+    before = [before[k] for k in range(len(GROUPS[1]))]
+    totals = later_products(lambda j: (bx - j, bx), before, by, nz, reader(start, one, two))
     for k, total in enumerate(totals):
         partial[k] = total
 
@@ -407,8 +423,8 @@
     for j in range(1, STEPS + 1):
         for x in range(-reach_of(j), j):
             cells.get(STEPS + j, x)
-    before = tuple(partial[k] for k in range(len(GROUPS[1])))
-    rows = summed_rows(products(GROUPS[1], 0, STEPS, by, nz, reader(start, one, two), before))
+    before = [partial[k] for k in range(len(GROUPS[1]))]
+    rows = summed_rows(later_products(lambda j: (0, j), before, by, nz, reader(start, one, two)))
     sums = jnp.concatenate([early_gram[...]] + rows, axis=0)
     on = lax.broadcasted_iota(jnp.int32, sums.shape, 0) == lax.broadcasted_iota(jnp.int32, sums.shape, 1)
     line = jnp.sum(jnp.where(on, jnp.sum(sums, axis=1, keepdims=True), 0.0), axis=0, keepdims=True)
@@ -542,9 +558,9 @@
         aliases={11: 0},
     )
     low, high = swap_x(to_low, to_high)
-    two, early_gram = call(
+    two, early_gram, partial = call(
         lambda *refs: second_interior_kernel(by, *refs),
-        [vectors, shape(STARTS[1], 128)],
+        [vectors, shape(STARTS[1], 128), shape(len(GROUPS[1]), 8, 128)],
         start,
         one,
         coef,
@@ -564,6 +580,7 @@
         edge,
         weight,
         high,
+        partial,
         name="sooner",
         scratch=halo,
         aliases={2: 0},

time: 47.9 us -> 47.8 us (level)
  transfers between devices with their start and end apart: 10 -> 10, of which waited for: 6 -> 6; matrix products, arithmetic and copies ran while one was open for 0% -> 0% of each run, Pallas kernels for 6% -> 7%
where the time goes in v8:
time: 47.8 us; the launch traced here: 47.7 us
  starting transfers between devices  16.8 us (35%)
  waiting for transfers between devices  12.7 us (27%)
  blocking collectives  8.99 us (19%)
  Pallas kernels  8.22 us (17%)
  between operations  0.78 us (2%)
    ppermute x3, starting transfers between devices, swap_x(): lax.ppermute(to_low, 'gx', ring('gx', -1))  13.3 us
    all_to_all x1, blocking collectives, per_device(): gram = lax.all_to_all(gram, AXES, 0, 0, tiled=True)  8.99 us
    pallas_call x9, Pallas kernels, call(): pl.pallas_call(kernel, out_shape=outs, in_specs=in_specs or [VMEM] * len(...  8.22 us
    ppermute x3, waiting for transfers between devices, swap_x(): lax.ppermute(to_high, 'gx', ring('gx', 1))  7.32 us
    ppermute x3, waiting for transfers between devices, swap_x(): lax.ppermute(to_low, 'gx', ring('gx', -1))  5.41 us
    ppermute x3, starting transfers between devices, swap_x(): lax.ppermute(to_high, 'gx', ring('gx', 1))  2.61 us
  transfers between devices with their start and end apart: 10, of which 6 were waited for; matrix products, arithmetic and copies ran while one was open for 0% of the time, Pallas kernels for 7%

profile of v8, /device:TPU:0, one launch (start us, length us, event | category | flops | bytes accessed | tf_op | source)
XLA Modules:
  0.0 47.7 jit_solution(7280359625134998769)
XLA Ops:
  0.6 1.3 %pack.1 = (f32[5,8,32,256]{3,2,1,0:T(8,128)S(1)}, f32[7,32,256]{2,1,0:T(8,128)S(1)}, f32[7,32,256]{2,1,0:T(8,128)S(1)}, f32[22,8,256]{2,1,0:T(8,128)S(1)}) custom-call(f32[8,32,256]{2,1,0:T(8,128)} %f.1, f32[8,32,256]{2,1,0:T(8,128)} %r.1, f32[3,8,32,256]{3,2,1,0:T(8,128)} %vel.1), custom_call_target="tpu_custom_call" | custom-call | bytes 60000 | tf_op jit(solution)/shard_map/pack/pallas_call | solution.py:485
  2.0 0.5 %collective-permute-start.4 = (f32[22,8,256]{2,1,0:T(8,128)S(1)}, f32[22,8,256]{2,1,0:T(8,128)S(1)}, u32[]{:S(2)}, u32[]{:S(2)}) collective-permute-start(f32[22,8,256]{2,1,0:T(8,128)S(1)} %get-tuple-element.36), channel_id=1, source_target_pairs={{0,1},{1,0},{2,3},{3,2},{4,5},{5,4},{6,7},{7,6},{8,9},{9,8},{10,11... | collective-permute-start | bytes 540680 | tf_op jit(solution)/shard_map/ppermute | solution.py:58
  2.5 2.6 %collective-permute-start.1 = (f32[7,32,256]{2,1,0:T(8,128)S(1)}, f32[7,32,256]{2,1,0:T(8,128)S(1)}, u32[]{:S(2)}, u32[]{:S(2)}) collective-permute-start(f32[7,32,256]{2,1,0:T(8,128)S(1)} %get-tuple-element.30), channel_id=1, source_target_pairs={{0,2},{2,4},{4,6},{6,8},{8,10},{10,12},{12,14},{14,16},{16,18},{18... | collective-permute-start | bytes 688136 | tf_op jit(solution)/shard_map/ppermute | solution.py:48
  5.0 4.1 %collective-permute-start.2 = (f32[7,32,256]{2,1,0:T(8,128)S(1)}, f32[7,32,256]{2,1,0:T(8,128)S(1)}, u32[]{:S(2)}, u32[]{:S(2)}) collective-permute-start(f32[7,32,256]{2,1,0:T(8,128)S(1)} %get-tuple-element.31), channel_id=1, source_target_pairs={{0,30},{2,0},{4,2},{6,4},{8,6},{10,8},{12,10},{14,12},{16,14},{18,... | collective-permute-start | bytes 688136 | tf_op jit(solution)/shard_map/ppermute | solution.py:48
  9.2 0.1 collective-permute-start
  9.4 0.0 collective-permute-done.4.rows
  9.4 0.3 inner.1
  9.6 0.1 collective-permute-start.5
  9.7 5.6 %collective-permute-start.6 = (f32[2,32,256]{2,1,0:T(8,128)S(1)}, f32[2,32,256]{2,1,0:T(8,128)S(1)}, u32[]{:S(2)}, u32[]{:S(2)}) collective-permute-start(f32[2,32,256]{2,1,0:T(8,128)S(1)} %get-tuple-element.38), channel_id=1, source_target_pairs={{0,30},{2,0},{4,2},{6,4},{8,6},{10,8},{12,10},{14,12},{16,14},{18,... | collective-permute-start | bytes 196616 | tf_op jit(solution)/shard_map/ppermute | solution.py:48
  15.3 2.0 %collective-permute-done.1.low = f32[7,32,256]{2,1,0:T(8,128)S(1)} collective-permute-done((f32[7,32,256]{2,1,0:T(8,128)S(1)}, f32[7,32,256]{2,1,0:T(8,128)S(1)}, u32[]{:S(2)}, u32[]{:S(2)}) %collective-permute-start.1) | collective-permute-done | bytes 229408 | tf_op jit(solution)/shard_map/ppermute | solution.py:48
  17.3 0.5 %collective-permute-done.2.high = f32[7,32,256]{2,1,0:T(8,128)S(1)} collective-permute-done((f32[7,32,256]{2,1,0:T(8,128)S(1)}, f32[7,32,256]{2,1,0:T(8,128)S(1)}, u32[]{:S(2)}, u32[]{:S(2)}) %collective-permute-start.2) | collective-permute-done | bytes 229408 | tf_op jit(solution)/shard_map/ppermute | solution.py:48
  17.9 0.1 collective-permute-start.3
  18.0 0.3 collective-permute-done.5.low_later
  18.2 1.9 %collective-permute-done.6.high_later = f32[2,32,256]{2,1,0:T(8,128)S(1)} collective-permute-done((f32[2,32,256]{2,1,0:T(8,128)S(1)}, f32[2,32,256]{2,1,0:T(8,128)S(1)}, u32[]{:S(2)}, u32[]{:S(2)}) %collective-permute-start.6) | collective-permute-done | bytes 65568 | tf_op jit(solution)/shard_map/ppermute | solution.py:48
  20.2 0.1 collective-permute-start.7
  20.3 0.0 collective-permute-done.rows
  20.3 0.7 %prepare.1 = (f32[8,48,256]{2,1,0:T(8,128)S(1)}, f32[4,8,48,256]{3,2,1,0:T(8,128)S(1)}, f32[4,8,48,256]{3,2,1,0:T(8,128)S(1)}) custom-call(f32[5,8,32,256]{3,2,1,0:T(8,128)S(1)} %get-tuple-element.27.fields, f32[40,16,256]{2,1,0:T(8,128)S(1)} %collective-permute-done.rows), custom_call_target="tpu_custom_call" | custom-call | bytes 60000 | tf_op jit(solution)/shard_map/prepare/pallas_call | solution.py:485
  21.0 0.0 collective-permute-done.3.corner
  21.0 0.8 %first.1 = (f32[4,8,48,256]{3,2,1,0:T(8,128)S(1)}, f32[2,48,256]{2,1,0:T(8,128)S(1)}, f32[4,2,48,256]{3,2,1,0:T(8,128)S(1)}, f32[2,48,256]{2,1,0:T(8,128)S(1)}) custom-call(f32[8,48,256]{2,1,0:T(8,128)S(1)} %get-tuple-element.28.start.refs_0_.refs_1_, f32[4,8,48,256]{3,2,1,0:T(8,128)S(1)} %get-tuple-element.29.coef.refs_2_, ...), custom_call_target="tpu_custom_call", output_to_operand_aliasing={{0}: (5, {})} | custom-call | bytes 60000 | tf_op jit(solution)/shard_map/first/pallas_call | solution.py:485
  21.7 0.0 collective-permute-done.7.later_corner
  21.7 0.7 %rest.1 = (f32[4,8,48,256]{3,2,1,0:T(8,128)S(1)}, f32[144,256]{1,0:T(8,128)S(1)}, f32[144,256]{1,0:T(8,128)S(1)}, f32[4,8,48,256]{3,2,1,0:T(8,128)S(1)}, f32[2,48,256]{2,1,0:T(8,128)S(1)}) custom-call(f32[8,48,256]{2,1,0:T(8,128)S(1)} %get-tuple-element.28.start.refs_0_.refs_1_, ...), custom_call_target="tpu_custom_call", output_to_operand_aliasing={{0}: (11, {})} | custom-call | bytes 60000 | tf_op jit(solution)/shard_map/rest/pallas_call | solution.py:485
  22.4 3.7 %collective-permute-start.8 = (f32[144,256]{1,0:T(8,128)S(1)}, f32[144,256]{1,0:T(8,128)S(1)}, u32[]{:S(2)}, u32[]{:S(2)}) collective-permute-start(f32[144,256]{1,0:T(8,128)S(1)} %get-tuple-element.44), channel_id=1, source_target_pairs={{0,30},{2,0},{4,2},{6,4},{8,6},{10,8},{12,10},{14,12},{16,14},{18,... | collective-permute-start | bytes 442376 | tf_op jit(solution)/shard_map/ppermute | solution.py:48
  26.1 0.0 collective-permute-start.9
  26.1 0.8 %second_interior.1 = (f32[4,8,48,256]{3,2,1,0:T(8,128)S(1)}, f32[16,128]{1,0:T(8,128)S(1)}, f32[30,8,128]{2,1,0:T(8,128)S(1)}) custom-call(f32[8,48,256]{2,1,0:T(8,128)S(1)} %get-tuple-element.28.start.refs_0_.refs_1_, f32[4,8,48,256]{3,2,1,0:T(8,128)S(1)} %get-tuple-element.40.refs_1_.one.refs_2_, ...), custom_call_target="tpu_custom_call", output_to_operand_aliasing={{0}: (3, {})} | custom-call | bytes 60000 | tf_op jit(solution)/shard_map/second_interior/pallas_call | solution.py:485
  26.9 2.9 %collective-permute-done.8.high = f32[144,256]{1,0:T(8,128)S(1)} collective-permute-done((f32[144,256]{1,0:T(8,128)S(1)}, f32[144,256]{1,0:T(8,128)S(1)}, u32[]{:S(2)}, u32[]{:S(2)}) %collective-permute-start.8) | collective-permute-done | bytes 147488 | tf_op jit(solution)/shard_map/ppermute | solution.py:48
  29.9 0.7 %sooner.1 = (f32[4,8,48,256]{3,2,1,0:T(8,128)S(1)}, f32[30,8,128]{2,1,0:T(8,128)S(1)}) custom-call(f32[8,48,256]{2,1,0:T(8,128)S(1)} %get-tuple-element.28.start.refs_0_.refs_1_, f32[4,8,48,256]{3,2,1,0:T(8,128)S(1)} %get-tuple-element.40.refs_1_.one.refs_2_, f32[4,8,48,256]{3,2,1,0:T(8,128)S(1)} %get-tuple-element.42.given, ...), custom_call_target="tpu_custom_call", output_to_operand_aliasing={{0}: (2, {})} | custom-call | bytes 60000 | tf_op jit(solution)/shard_map/sooner/pallas_call | solution.py:485
  30.6 5.1 %collective-permute-done.9.low = f32[144,256]{1,0:T(8,128)S(1)} collective-permute-done((f32[144,256]{1,0:T(8,128)S(1)}, f32[144,256]{1,0:T(8,128)S(1)}, u32[]{:S(2)}, u32[]{:S(2)}) %collective-permute-start.9) | collective-permute-done | bytes 147488 | tf_op jit(solution)/shard_map/ppermute | solution.py:48
  35.7 0.8 %later.1 = (f32[4,8,48,256]{3,2,1,0:T(8,128)S(1)}, f32[32,128]{1,0:T(8,128)S(1)}) custom-call(f32[8,48,256]{2,1,0:T(8,128)S(1)} %get-tuple-element.28.start.refs_0_.refs_1_, f32[4,8,48,256]{3,2,1,0:T(8,128)S(1)} %get-tuple-element.40.refs_1_.one.refs_2_, f32[4,8,48,256]{3,2,1,0:T(8,128)S(1)} %get-tuple-element.46.given, ...), custom_call_target="tpu_custom_call", output_to_operand_aliasing={{0}: (2, {})} | custom-call | bytes 60000 | tf_op jit(solution)/shard_map/later/pallas_call | solution.py:485
  36.5 9.0 %all_to_all.11 = f32[32,1,128]{2,1,0:T(1,128)S(1)} all-to-all(f32[32,1,128]{2,1,0:T(1,128)S(1)} %bitcast.7), channel_id=1, replica_groups=mesh['gx'=16,'gy'=2] {'gx','gy'}, dimensions={0} | all-to-all | bytes 32768 | tf_op jit(solution)/shard_map/all_to_all | solution.py:605
  45.5 2.2 %last.1 = (f32[9,8,32,256]{3,2,1,0:T(8,128)}, f32[9,9]{1,0:T(8,128)}) custom-call(f32[32,128]{1,0:T(8,128)S(1)} %bitcast.6, f32[8,48,256]{2,1,0:T(8,128)S(1)} %get-tuple-element.28.start.refs_0_.refs_1_, f32[4,8,48,256]{3,2,1,0:T(8,128)S(1)} %get-tuple-element.40.refs_1_.one.refs_2_, f32[4,8,48,256]{3,2,1,0:T(8,128)S(1)} %get-tuple-element.51.refs_3_), custom_call_target="tpu_custom_call" | custom-call | bytes 60000 | tf_op jit(solution)/shard_map/last/pallas_call | solution.py:485
  (10 shorter events, 0.2 us)
Async XLA Ops:
  2.0 7.4 %collective-permute-start.4 = (f32[22,8,256]{2,1,0:T(8,128)S(1)}, f32[22,8,256]{2,1,0:T(8,128)S(1)}, u32[]{:S(2)}, u32[]{:S(2)}) collective-permute-start(f32[22,8,256]{2,1,0:T(8,128)S(1)} %get-tuple-element.36), channel_id=1, source_target_pairs={{0,1},{1,0},{2,3},{3,2},{4,5},{5,4},{6,7},{7,6},{8,9},{9,8},{10,11... | collective-permute-start | bytes 540680 | tf_op jit(solution)/shard_map/ppermute | solution.py:58
  2.5 14.8 %collective-permute-start.1 = (f32[7,32,256]{2,1,0:T(8,128)S(1)}, f32[7,32,256]{2,1,0:T(8,128)S(1)}, u32[]{:S(2)}, u32[]{:S(2)}) collective-permute-start(f32[7,32,256]{2,1,0:T(8,128)S(1)} %get-tuple-element.30), channel_id=1, source_target_pairs={{0,2},{2,4},{4,6},{6,8},{8,10},{10,12},{12,14},{14,16},{16,18},{18... | collective-permute-start | bytes 688136 | tf_op jit(solution)/shard_map/ppermute | solution.py:48
  5.0 12.8 %collective-permute-start.2 = (f32[7,32,256]{2,1,0:T(8,128)S(1)}, f32[7,32,256]{2,1,0:T(8,128)S(1)}, u32[]{:S(2)}, u32[]{:S(2)}) collective-permute-start(f32[7,32,256]{2,1,0:T(8,128)S(1)} %get-tuple-element.31), channel_id=1, source_target_pairs={{0,30},{2,0},{4,2},{6,4},{8,6},{10,8},{12,10},{14,12},{16,14},{18,... | collective-permute-start | bytes 688136 | tf_op jit(solution)/shard_map/ppermute | solution.py:48
  9.2 11.1 %collective-permute-start = (f32[40,16,256]{2,1,0:T(8,128)S(1)}, f32[40,16,256]{2,1,0:T(8,128)S(1)}, u32[]{:S(2)}, u32[]{:S(2)}) collective-permute-start(f32[40,16,256]{2,1,0:T(8,128)S(1)} %pad_maximum_fusion), channel_id=1, source_target_pairs={{0,1},{1,0},{2,3},{3,2},{4,5},{5,4},{6,7},{7,6},{8,9},{9,8},{10,11... | collective-permute-start | bytes 1966088 | tf_op jit(solution)/shard_map/ppermute | solution.py:58
  9.6 8.6 %collective-permute-start.5 = (f32[2,32,256]{2,1,0:T(8,128)S(1)}, f32[2,32,256]{2,1,0:T(8,128)S(1)}, u32[]{:S(2)}, u32[]{:S(2)}) collective-permute-start(f32[2,32,256]{2,1,0:T(8,128)S(1)} %get-tuple-element.37), channel_id=1, source_target_pairs={{0,2},{2,4},{4,6},{6,8},{8,10},{10,12},{12,14},{14,16},{16,18},{18... | collective-permute-start | bytes 196616 | tf_op jit(solution)/shard_map/ppermute | solution.py:48
  9.7 10.5 %collective-permute-start.6 = (f32[2,32,256]{2,1,0:T(8,128)S(1)}, f32[2,32,256]{2,1,0:T(8,128)S(1)}, u32[]{:S(2)}, u32[]{:S(2)}) collective-permute-start(f32[2,32,256]{2,1,0:T(8,128)S(1)} %get-tuple-element.38), channel_id=1, source_target_pairs={{0,30},{2,0},{4,2},{6,4},{8,6},{10,8},{12,10},{14,12},{16,14},{18,... | collective-permute-start | bytes 196616 | tf_op jit(solution)/shard_map/ppermute | solution.py:48
  17.9 3.1 %collective-permute-start.3 = (f32[14,16,256]{2,1,0:T(8,128)S(1)}, f32[14,16,256]{2,1,0:T(8,128)S(1)}, u32[]{:S(2)}, u32[]{:S(2)}) collective-permute-start(f32[14,16,256]{2,1,0:T(8,128)S(1)} %pad_maximum_fusion.1), channel_id=1, source_target_pairs={{0,1},{1,0},{2,3},{3,2},{4,5},{5,4},{6,7},{7,6},{8,9},{9,8},{10,11... | collective-permute-start | bytes 688136 | tf_op jit(solution)/shard_map/ppermute | solution.py:58
  20.2 1.5 %collective-permute-start.7 = (f32[4,16,256]{2,1,0:T(8,128)S(1)}, f32[4,16,256]{2,1,0:T(8,128)S(1)}, u32[]{:S(2)}, u32[]{:S(2)}) collective-permute-start(f32[4,16,256]{2,1,0:T(8,128)S(1)} %pad_maximum_fusion.2), channel_id=1, source_target_pairs={{0,1},{1,0},{2,3},{3,2},{4,5},{5,4},{6,7},{7,6},{8,9},{9,8},{10,11... | collective-permute-start | bytes 196616 | tf_op jit(solution)/shard_map/ppermute | solution.py:58
  22.4 7.4 %collective-permute-start.8 = (f32[144,256]{1,0:T(8,128)S(1)}, f32[144,256]{1,0:T(8,128)S(1)}, u32[]{:S(2)}, u32[]{:S(2)}) collective-permute-start(f32[144,256]{1,0:T(8,128)S(1)} %get-tuple-element.44), channel_id=1, source_target_pairs={{0,30},{2,0},{4,2},{6,4},{8,6},{10,8},{12,10},{14,12},{16,14},{18,... | collective-permute-start | bytes 442376 | tf_op jit(solution)/shard_map/ppermute | solution.py:48
  26.1 9.6 %collective-permute-start.9 = (f32[144,256]{1,0:T(8,128)S(1)}, f32[144,256]{1,0:T(8,128)S(1)}, u32[]{:S(2)}, u32[]{:S(2)}) collective-permute-start(f32[144,256]{1,0:T(8,128)S(1)} %get-tuple-element.47), channel_id=1, source_target_pairs={{0,2},{2,4},{4,6},{6,8},{8,10},{10,12},{12,14},{14,16},{16,18},{18... | collective-permute-start | bytes 442376 | tf_op jit(solution)/shard_map/ppermute | solution.py:48

commit v9 on v8

--- a/solution.py
+++ b/solution.py
@@ -200,8 +200,8 @@
             cells.known[0, x] = lambda x=x: layer(0, x) * LIFT
     to_low[0] = cells.get(1, 1)[:by]
     to_high[0] = cells.get(1, bx - 2)[:by]
-    to_low[1] = cells.tip(0, 1, True)[:by]
-    to_high[1] = cells.tip(0, bx - 2, False)[:by]
+    to_low[1] = cells.tip(0, 1, True, by)
+    to_high[1] = cells.tip(0, bx - 2, False, by)
 
 
 class Cells:
@@ -229,12 +229,12 @@
             self.known[j, x] = lambda: ref[at]
         return self.known[j, x]()
 
-    def tip(self, base, x, below):
+    def tip(self, base, x, below, by):
         j = base + TIP[0]
-        centre, beyond = self.get(j - 1, x), self.get(j - 1, x + 1 if below else x - 1)
-        nothing = jnp.zeros_like(centre)
+        centre, beyond = self.get(j - 1, x), self.get(j - 1, x + 1 if below else x - 1)[:by]
+        nothing = jnp.zeros_like(beyond)
         pair = (beyond, nothing) if below else (nothing, beyond)
-        return doubled(centre, *pair, self.coefficients(x)) - self.get(j - 2, x)
+        return doubled(centre, *pair, [c[:by] for c in self.coefficients(x)]) - self.get(j - 2, x)[:by]
 
     def interior(self, base):
         for j in range(1, STEPS):
@@ -358,7 +358,7 @@
             cells.get(STEPS, one),
             cells.get(STEPS, two),
             cells.get(STEPS + 1, two),
-            cells.tip(STEPS, two, below),
+            cells.tip(STEPS, two, below, by),
         ]
         for at, layer in enumerate(leaving):
             out[at * by : (at + 1) * by] = layer[:by]

time: 47.8 us -> 47.8 us (level)
  no operation moved by 1% of the time
where the time goes in v9:
time: 47.8 us; the launch traced here: 47.7 us
  starting transfers between devices  16.8 us (35%)
  waiting for transfers between devices  12.7 us (27%)
  blocking collectives  8.99 us (19%)
  Pallas kernels  8.22 us (17%)
  between operations  0.78 us (2%)
    ppermute x3, starting transfers between devices, swap_x(): lax.ppermute(to_low, 'gx', ring('gx', -1))  13.3 us
    all_to_all x1, blocking collectives, per_device(): gram = lax.all_to_all(gram, AXES, 0, 0, tiled=True)  8.99 us
    pallas_call x9, Pallas kernels, call(): pl.pallas_call(kernel, out_shape=outs, in_specs=in_specs or [VMEM] * len(...  8.22 us
    ppermute x3, waiting for transfers between devices, swap_x(): lax.ppermute(to_high, 'gx', ring('gx', 1))  7.32 us
    ppermute x3, waiting for transfers between devices, swap_x(): lax.ppermute(to_low, 'gx', ring('gx', -1))  5.41 us
    ppermute x3, starting transfers between devices, swap_x(): lax.ppermute(to_high, 'gx', ring('gx', 1))  2.61 us
  transfers between devices with their start and end apart: 10, of which 6 were waited for; matrix products, arithmetic and copies ran while one was open for 0% of the time, Pallas kernels for 7%

profile of v9, /device:TPU:0, one launch (start us, length us, event | category | flops | bytes accessed | tf_op | source)
XLA Modules:
  0.0 47.7 jit_solution(7280359625134998769)
XLA Ops:
  0.6 1.3 %pack.1 = (f32[5,8,32,256]{3,2,1,0:T(8,128)S(1)}, f32[7,32,256]{2,1,0:T(8,128)S(1)}, f32[7,32,256]{2,1,0:T(8,128)S(1)}, f32[22,8,256]{2,1,0:T(8,128)S(1)}) custom-call(f32[8,32,256]{2,1,0:T(8,128)} %f.1, f32[8,32,256]{2,1,0:T(8,128)} %r.1, f32[3,8,32,256]{3,2,1,0:T(8,128)} %vel.1), custom_call_target="tpu_custom_call" | custom-call | bytes 60000 | tf_op jit(solution)/shard_map/pack/pallas_call | solution.py:485
  2.0 0.5 %collective-permute-start.4 = (f32[22,8,256]{2,1,0:T(8,128)S(1)}, f32[22,8,256]{2,1,0:T(8,128)S(1)}, u32[]{:S(2)}, u32[]{:S(2)}) collective-permute-start(f32[22,8,256]{2,1,0:T(8,128)S(1)} %get-tuple-element.36), channel_id=1, source_target_pairs={{0,1},{1,0},{2,3},{3,2},{4,5},{5,4},{6,7},{7,6},{8,9},{9,8},{10,11... | collective-permute-start | bytes 540680 | tf_op jit(solution)/shard_map/ppermute | solution.py:58
  2.5 2.6 %collective-permute-start.1 = (f32[7,32,256]{2,1,0:T(8,128)S(1)}, f32[7,32,256]{2,1,0:T(8,128)S(1)}, u32[]{:S(2)}, u32[]{:S(2)}) collective-permute-start(f32[7,32,256]{2,1,0:T(8,128)S(1)} %get-tuple-element.30), channel_id=1, source_target_pairs={{0,2},{2,4},{4,6},{6,8},{8,10},{10,12},{12,14},{14,16},{16,18},{18... | collective-permute-start | bytes 688136 | tf_op jit(solution)/shard_map/ppermute | solution.py:48
  5.0 4.1 %collective-permute-start.2 = (f32[7,32,256]{2,1,0:T(8,128)S(1)}, f32[7,32,256]{2,1,0:T(8,128)S(1)}, u32[]{:S(2)}, u32[]{:S(2)}) collective-permute-start(f32[7,32,256]{2,1,0:T(8,128)S(1)} %get-tuple-element.31), channel_id=1, source_target_pairs={{0,30},{2,0},{4,2},{6,4},{8,6},{10,8},{12,10},{14,12},{16,14},{18,... | collective-permute-start | bytes 688136 | tf_op jit(solution)/shard_map/ppermute | solution.py:48
  9.2 0.1 collective-permute-start
  9.4 0.0 collective-permute-done.4.rows
  9.4 0.3 inner.1
  9.6 0.1 collective-permute-start.5
  9.7 5.6 %collective-permute-start.6 = (f32[2,32,256]{2,1,0:T(8,128)S(1)}, f32[2,32,256]{2,1,0:T(8,128)S(1)}, u32[]{:S(2)}, u32[]{:S(2)}) collective-permute-start(f32[2,32,256]{2,1,0:T(8,128)S(1)} %get-tuple-element.38), channel_id=1, source_target_pairs={{0,30},{2,0},{4,2},{6,4},{8,6},{10,8},{12,10},{14,12},{16,14},{18,... | collective-permute-start | bytes 196616 | tf_op jit(solution)/shard_map/ppermute | solution.py:48
  15.3 2.0 %collective-permute-done.1.low = f32[7,32,256]{2,1,0:T(8,128)S(1)} collective-permute-done((f32[7,32,256]{2,1,0:T(8,128)S(1)}, f32[7,32,256]{2,1,0:T(8,128)S(1)}, u32[]{:S(2)}, u32[]{:S(2)}) %collective-permute-start.1) | collective-permute-done | bytes 229408 | tf_op jit(solution)/shard_map/ppermute | solution.py:48
  17.3 0.5 %collective-permute-done.2.high = f32[7,32,256]{2,1,0:T(8,128)S(1)} collective-permute-done((f32[7,32,256]{2,1,0:T(8,128)S(1)}, f32[7,32,256]{2,1,0:T(8,128)S(1)}, u32[]{:S(2)}, u32[]{:S(2)}) %collective-permute-start.2) | collective-permute-done | bytes 229408 | tf_op jit(solution)/shard_map/ppermute | solution.py:48
  17.9 0.1 collective-permute-start.3
  18.0 0.3 collective-permute-done.5.low_later
  18.2 1.9 %collective-permute-done.6.high_later = f32[2,32,256]{2,1,0:T(8,128)S(1)} collective-permute-done((f32[2,32,256]{2,1,0:T(8,128)S(1)}, f32[2,32,256]{2,1,0:T(8,128)S(1)}, u32[]{:S(2)}, u32[]{:S(2)}) %collective-permute-start.6) | collective-permute-done | bytes 65568 | tf_op jit(solution)/shard_map/ppermute | solution.py:48
  20.2 0.1 collective-permute-start.7
  20.3 0.0 collective-permute-done.rows
  20.3 0.7 %prepare.1 = (f32[8,48,256]{2,1,0:T(8,128)S(1)}, f32[4,8,48,256]{3,2,1,0:T(8,128)S(1)}, f32[4,8,48,256]{3,2,1,0:T(8,128)S(1)}) custom-call(f32[5,8,32,256]{3,2,1,0:T(8,128)S(1)} %get-tuple-element.27.fields, f32[40,16,256]{2,1,0:T(8,128)S(1)} %collective-permute-done.rows), custom_call_target="tpu_custom_call" | custom-call | bytes 60000 | tf_op jit(solution)/shard_map/prepare/pallas_call | solution.py:485
  21.0 0.0 collective-permute-done.3.corner
  21.0 0.8 %first.1 = (f32[4,8,48,256]{3,2,1,0:T(8,128)S(1)}, f32[2,48,256]{2,1,0:T(8,128)S(1)}, f32[4,2,48,256]{3,2,1,0:T(8,128)S(1)}, f32[2,48,256]{2,1,0:T(8,128)S(1)}) custom-call(f32[8,48,256]{2,1,0:T(8,128)S(1)} %get-tuple-element.28.start.refs_0_.refs_1_, f32[4,8,48,256]{3,2,1,0:T(8,128)S(1)} %get-tuple-element.29.coef.refs_2_, ...), custom_call_target="tpu_custom_call", output_to_operand_aliasing={{0}: (5, {})} | custom-call | bytes 60000 | tf_op jit(solution)/shard_map/first/pallas_call | solution.py:485
  21.7 0.0 collective-permute-done.7.later_corner
  21.7 0.7 %rest.1 = (f32[4,8,48,256]{3,2,1,0:T(8,128)S(1)}, f32[144,256]{1,0:T(8,128)S(1)}, f32[144,256]{1,0:T(8,128)S(1)}, f32[4,8,48,256]{3,2,1,0:T(8,128)S(1)}, f32[2,48,256]{2,1,0:T(8,128)S(1)}) custom-call(f32[8,48,256]{2,1,0:T(8,128)S(1)} %get-tuple-element.28.start.refs_0_.refs_1_, ...), custom_call_target="tpu_custom_call", output_to_operand_aliasing={{0}: (11, {})} | custom-call | bytes 60000 | tf_op jit(solution)/shard_map/rest/pallas_call | solution.py:485
  22.4 3.7 %collective-permute-start.8 = (f32[144,256]{1,0:T(8,128)S(1)}, f32[144,256]{1,0:T(8,128)S(1)}, u32[]{:S(2)}, u32[]{:S(2)}) collective-permute-start(f32[144,256]{1,0:T(8,128)S(1)} %get-tuple-element.44), channel_id=1, source_target_pairs={{0,30},{2,0},{4,2},{6,4},{8,6},{10,8},{12,10},{14,12},{16,14},{18,... | collective-permute-start | bytes 442376 | tf_op jit(solution)/shard_map/ppermute | solution.py:48
  26.1 0.0 collective-permute-start.9
  26.1 0.8 %second_interior.1 = (f32[4,8,48,256]{3,2,1,0:T(8,128)S(1)}, f32[16,128]{1,0:T(8,128)S(1)}, f32[30,8,128]{2,1,0:T(8,128)S(1)}) custom-call(f32[8,48,256]{2,1,0:T(8,128)S(1)} %get-tuple-element.28.start.refs_0_.refs_1_, f32[4,8,48,256]{3,2,1,0:T(8,128)S(1)} %get-tuple-element.40.refs_1_.one.refs_2_, ...), custom_call_target="tpu_custom_call", output_to_operand_aliasing={{0}: (3, {})} | custom-call | bytes 60000 | tf_op jit(solution)/shard_map/second_interior/pallas_call | solution.py:485
  26.9 2.9 %collective-permute-done.8.high = f32[144,256]{1,0:T(8,128)S(1)} collective-permute-done((f32[144,256]{1,0:T(8,128)S(1)}, f32[144,256]{1,0:T(8,128)S(1)}, u32[]{:S(2)}, u32[]{:S(2)}) %collective-permute-start.8) | collective-permute-done | bytes 147488 | tf_op jit(solution)/shard_map/ppermute | solution.py:48
  29.9 0.7 %sooner.1 = (f32[4,8,48,256]{3,2,1,0:T(8,128)S(1)}, f32[30,8,128]{2,1,0:T(8,128)S(1)}) custom-call(f32[8,48,256]{2,1,0:T(8,128)S(1)} %get-tuple-element.28.start.refs_0_.refs_1_, f32[4,8,48,256]{3,2,1,0:T(8,128)S(1)} %get-tuple-element.40.refs_1_.one.refs_2_, f32[4,8,48,256]{3,2,1,0:T(8,128)S(1)} %get-tuple-element.42.given, ...), custom_call_target="tpu_custom_call", output_to_operand_aliasing={{0}: (2, {})} | custom-call | bytes 60000 | tf_op jit(solution)/shard_map/sooner/pallas_call | solution.py:485
  30.6 5.1 %collective-permute-done.9.low = f32[144,256]{1,0:T(8,128)S(1)} collective-permute-done((f32[144,256]{1,0:T(8,128)S(1)}, f32[144,256]{1,0:T(8,128)S(1)}, u32[]{:S(2)}, u32[]{:S(2)}) %collective-permute-start.9) | collective-permute-done | bytes 147488 | tf_op jit(solution)/shard_map/ppermute | solution.py:48
  35.7 0.8 %later.1 = (f32[4,8,48,256]{3,2,1,0:T(8,128)S(1)}, f32[32,128]{1,0:T(8,128)S(1)}) custom-call(f32[8,48,256]{2,1,0:T(8,128)S(1)} %get-tuple-element.28.start.refs_0_.refs_1_, f32[4,8,48,256]{3,2,1,0:T(8,128)S(1)} %get-tuple-element.40.refs_1_.one.refs_2_, f32[4,8,48,256]{3,2,1,0:T(8,128)S(1)} %get-tuple-element.46.given, ...), custom_call_target="tpu_custom_call", output_to_operand_aliasing={{0}: (2, {})} | custom-call | bytes 60000 | tf_op jit(solution)/shard_map/later/pallas_call | solution.py:485
  36.5 9.0 %all_to_all.11 = f32[32,1,128]{2,1,0:T(1,128)S(1)} all-to-all(f32[32,1,128]{2,1,0:T(1,128)S(1)} %bitcast.7), channel_id=1, replica_groups=mesh['gx'=16,'gy'=2] {'gx','gy'}, dimensions={0} | all-to-all | bytes 32768 | tf_op jit(solution)/shard_map/all_to_all | solution.py:605
  45.5 2.2 %last.1 = (f32[9,8,32,256]{3,2,1,0:T(8,128)}, f32[9,9]{1,0:T(8,128)}) custom-call(f32[32,128]{1,0:T(8,128)S(1)} %bitcast.6, f32[8,48,256]{2,1,0:T(8,128)S(1)} %get-tuple-element.28.start.refs_0_.refs_1_, f32[4,8,48,256]{3,2,1,0:T(8,128)S(1)} %get-tuple-element.40.refs_1_.one.refs_2_, f32[4,8,48,256]{3,2,1,0:T(8,128)S(1)} %get-tuple-element.51.refs_3_), custom_call_target="tpu_custom_call" | custom-call | bytes 60000 | tf_op jit(solution)/shard_map/last/pallas_call | solution.py:485
  (10 shorter events, 0.2 us)
Async XLA Ops:
  2.0 7.4 %collective-permute-start.4 = (f32[22,8,256]{2,1,0:T(8,128)S(1)}, f32[22,8,256]{2,1,0:T(8,128)S(1)}, u32[]{:S(2)}, u32[]{:S(2)}) collective-permute-start(f32[22,8,256]{2,1,0:T(8,128)S(1)} %get-tuple-element.36), channel_id=1, source_target_pairs={{0,1},{1,0},{2,3},{3,2},{4,5},{5,4},{6,7},{7,6},{8,9},{9,8},{10,11... | collective-permute-start | bytes 540680 | tf_op jit(solution)/shard_map/ppermute | solution.py:58
  2.5 14.8 %collective-permute-start.1 = (f32[7,32,256]{2,1,0:T(8,128)S(1)}, f32[7,32,256]{2,1,0:T(8,128)S(1)}, u32[]{:S(2)}, u32[]{:S(2)}) collective-permute-start(f32[7,32,256]{2,1,0:T(8,128)S(1)} %get-tuple-element.30), channel_id=1, source_target_pairs={{0,2},{2,4},{4,6},{6,8},{8,10},{10,12},{12,14},{14,16},{16,18},{18... | collective-permute-start | bytes 688136 | tf_op jit(solution)/shard_map/ppermute | solution.py:48
  5.0 12.8 %collective-permute-start.2 = (f32[7,32,256]{2,1,0:T(8,128)S(1)}, f32[7,32,256]{2,1,0:T(8,128)S(1)}, u32[]{:S(2)}, u32[]{:S(2)}) collective-permute-start(f32[7,32,256]{2,1,0:T(8,128)S(1)} %get-tuple-element.31), channel_id=1, source_target_pairs={{0,30},{2,0},{4,2},{6,4},{8,6},{10,8},{12,10},{14,12},{16,14},{18,... | collective-permute-start | bytes 688136 | tf_op jit(solution)/shard_map/ppermute | solution.py:48
  9.2 11.1 %collective-permute-start = (f32[40,16,256]{2,1,0:T(8,128)S(1)}, f32[40,16,256]{2,1,0:T(8,128)S(1)}, u32[]{:S(2)}, u32[]{:S(2)}) collective-permute-start(f32[40,16,256]{2,1,0:T(8,128)S(1)} %pad_maximum_fusion), channel_id=1, source_target_pairs={{0,1},{1,0},{2,3},{3,2},{4,5},{5,4},{6,7},{7,6},{8,9},{9,8},{10,11... | collective-permute-start | bytes 1966088 | tf_op jit(solution)/shard_map/ppermute | solution.py:58
  9.6 8.6 %collective-permute-start.5 = (f32[2,32,256]{2,1,0:T(8,128)S(1)}, f32[2,32,256]{2,1,0:T(8,128)S(1)}, u32[]{:S(2)}, u32[]{:S(2)}) collective-permute-start(f32[2,32,256]{2,1,0:T(8,128)S(1)} %get-tuple-element.37), channel_id=1, source_target_pairs={{0,2},{2,4},{4,6},{6,8},{8,10},{10,12},{12,14},{14,16},{16,18},{18... | collective-permute-start | bytes 196616 | tf_op jit(solution)/shard_map/ppermute | solution.py:48
  9.7 10.5 %collective-permute-start.6 = (f32[2,32,256]{2,1,0:T(8,128)S(1)}, f32[2,32,256]{2,1,0:T(8,128)S(1)}, u32[]{:S(2)}, u32[]{:S(2)}) collective-permute-start(f32[2,32,256]{2,1,0:T(8,128)S(1)} %get-tuple-element.38), channel_id=1, source_target_pairs={{0,30},{2,0},{4,2},{6,4},{8,6},{10,8},{12,10},{14,12},{16,14},{18,... | collective-permute-start | bytes 196616 | tf_op jit(solution)/shard_map/ppermute | solution.py:48
  17.9 3.1 %collective-permute-start.3 = (f32[14,16,256]{2,1,0:T(8,128)S(1)}, f32[14,16,256]{2,1,0:T(8,128)S(1)}, u32[]{:S(2)}, u32[]{:S(2)}) collective-permute-start(f32[14,16,256]{2,1,0:T(8,128)S(1)} %pad_maximum_fusion.1), channel_id=1, source_target_pairs={{0,1},{1,0},{2,3},{3,2},{4,5},{5,4},{6,7},{7,6},{8,9},{9,8},{10,11... | collective-permute-start | bytes 688136 | tf_op jit(solution)/shard_map/ppermute | solution.py:58
  20.2 1.5 %collective-permute-start.7 = (f32[4,16,256]{2,1,0:T(8,128)S(1)}, f32[4,16,256]{2,1,0:T(8,128)S(1)}, u32[]{:S(2)}, u32[]{:S(2)}) collective-permute-start(f32[4,16,256]{2,1,0:T(8,128)S(1)} %pad_maximum_fusion.2), channel_id=1, source_target_pairs={{0,1},{1,0},{2,3},{3,2},{4,5},{5,4},{6,7},{7,6},{8,9},{9,8},{10,11... | collective-permute-start | bytes 196616 | tf_op jit(solution)/shard_map/ppermute | solution.py:58
  22.4 7.4 %collective-permute-start.8 = (f32[144,256]{1,0:T(8,128)S(1)}, f32[144,256]{1,0:T(8,128)S(1)}, u32[]{:S(2)}, u32[]{:S(2)}) collective-permute-start(f32[144,256]{1,0:T(8,128)S(1)} %get-tuple-element.44), channel_id=1, source_target_pairs={{0,30},{2,0},{4,2},{6,4},{8,6},{10,8},{12,10},{14,12},{16,14},{18,... | collective-permute-start | bytes 442376 | tf_op jit(solution)/shard_map/ppermute | solution.py:48
  26.1 9.6 %collective-permute-start.9 = (f32[144,256]{1,0:T(8,128)S(1)}, f32[144,256]{1,0:T(8,128)S(1)}, u32[]{:S(2)}, u32[]{:S(2)}) collective-permute-start(f32[144,256]{1,0:T(8,128)S(1)} %get-tuple-element.47), channel_id=1, source_target_pairs={{0,2},{2,4},{4,6},{6,8},{8,10},{10,12},{12,14},{14,16},{16,18},{18... | collective-permute-start | bytes 442376 | tf_op jit(solution)/shard_map/ppermute | solution.py:48
